TPU v7x, 32 devices: a whole 2x2x4 slice. The times are simulated.
32 devices in a mesh: ax: 4 (over z), xs: 8 (over y, x, core).
Axes of the slice: x: 2, y: 2, z: 4, core: 2. Of those that a mesh axis runs over, the one named last changes fastest.
Arguments:
- adjoint: float32 [512, 10, 1024], P('xs', None, 'ax'), may hold values from -6 to 6
- source: float32 [512, 10, 1024], P('xs', None, 'ax'), may hold values from -6 to 6
- speed: float32 [512, 5, 1024], P('xs', None, 'ax'), may hold values from -2 to 2, as said below
- inverse_step: float32 [512, 5, 1024], P('xs', None, 'ax'), as said below
- coupling: float32 [128, 5, 1024], P('xs', None, 'ax'), may hold values from -4 to 4
- face_line: int32 [128], P('xs'), may hold values from 0 to 63
- face_owner: int32 [128], P('xs'), may hold values from 0 to 127, as said below
- line_length: int32 [512], P('xs'), may hold values from 513 to 1024, as said below
Outputs:
- refreshed: float32 [512, 10, 1024], P('xs', None, 'ax')
- residual: float32 [512, 10, 1024], P('xs', None, 'ax')
Inputs may be any that keep to these rules, and one draw needn't show every extreme that they name: Each variable of a line keeps one sign of speed along the whole line, magnitude 0.5 or more. `inverse_step`: positive everywhere. `line_length`: the longest line has all 1024 cells. `face_owner`: each value once; of the 16 faces of one block, at most 2 have slots owned by any one block, and some block has exactly 2 with one owner block.
All inputs are finite; a program needn't handle non-finite values.
Results may differ from a plain program's by a relative error of at most 0.00015.
Values sent between devices are 32-bit elements; how exact they have to be, the bound alone decides.
No kernel may reach another device: no remote copies, remote signals or barrier semaphores. Data moves between devices by JAX's collectives and lax.ppermute only.
A program may use at most 64 MiB of HBM per device.

v0:
```python
import functools
import jax
import jax.numpy as jnp
from jax import lax
from jax.experimental import pallas as pl
from jax.experimental.pallas import tpu as pltpu
from jax.sharding import PartitionSpec as P

FACE_DEV = 8

frequency = 0.7
relaxation = 0.02

SEGS = 8
PACK_ROWS = 24
TABLE = 8
F32 = jnp.float32


def pack_faces(blocks, cap, paired, line_hbm, owner_hbm, adj_hbm, coup_hbm, *rest):
    adj_ref = rest[0]
    outs = rest[1:-5]
    stage, line_ref, owner_ref, coup_ref, sems = rest[-5:]
    vars_, faces, cells = coup_ref.shape
    half = cells // 2
    slots = FACE_DEV * blocks
    small = [
        pltpu.make_async_copy(owner_hbm, owner_ref, sems.at[0]),
        pltpu.make_async_copy(line_hbm, line_ref, sems.at[1]),
        pltpu.make_async_copy(coup_hbm, coup_ref, sems.at[2]),
    ]
    large = [
        pltpu.make_async_copy(adj_hbm.at[:, k], adj_ref.at[:, k], sems.at[3 + k])
        for k in range(vars_)
    ]
    for copy in small + large:
        copy.start()
    for copy in small[:2]:
        copy.wait()
    if blocks * cap != faces:
        for e in range(blocks * cap):
            stage[e, 16:24, :] = jnp.full((8, 128), -1.0, F32)
    dests, places = [], []
    for f in range(faces):
        slot = lax.rem(owner_ref[f], slots)
        dest = lax.div(slot, FACE_DEV)
        spot = jnp.int32(0)
        for other in dests:
            spot = spot + (other == dest).astype(jnp.int32)
        dests.append(dest)
        if paired:
            dest = lax.bitwise_xor(dest, lax.axis_index("xs"))
        entry = dest * cap + jnp.minimum(spot, cap - 1)
        places.append((entry, line_ref[f]))
        number = lax.rem(slot, FACE_DEV).astype(F32)
        stage[entry, 20:24, :] = jnp.full((4, 128), number, F32)
    small[2].wait()
    for k in range(vars_):
        large[k].wait()
        for f, (entry, line) in enumerate(places):
            c = coup_ref[k, f : f + 1, :]
            re = c * adj_ref[0, k, pl.ds(line, 1), :]
            im = c * adj_ref[1, k, pl.ds(line, 1), :]
            stage[entry, 4 * k : 4 * k + 1, :] = re[:, :half]
            stage[entry, 4 * k + 1 : 4 * k + 2, :] = re[:, half:]
            stage[entry, 4 * k + 2 : 4 * k + 3, :] = im[:, :half]
            stage[entry, 4 * k + 3 : 4 * k + 4, :] = im[:, half:]
    size = outs[0].shape[0]
    for i, out in enumerate(outs):
        out[...] = stage[i * size : (i + 1) * size]


def sort_halves(cap, sign_ref, *refs):
    *landed, near_ref, far_ref = refs
    for i, ref in enumerate(landed):
        near_ref[i * cap : (i + 1) * cap] = ref[:cap]
        far_ref[i * cap : (i + 1) * cap] = ref[cap:]


def cells_inside(len_ref, cells):
    row = len_ref[...].astype(F32)
    lines = row.shape[1]
    both = jnp.concatenate([row, row], axis=1)
    column = jnp.broadcast_to(both, (8, both.shape[1])).T[:lines, 0:1]
    cell = lax.axis_index("ax") * cells + lax.broadcasted_iota(jnp.int32, (lines, cells), 1)
    return cell.astype(F32) < column


def cell_terms(v, iv, a_re, a_im, q_re, q_im, inside):
    s = jnp.where(inside, jnp.abs(v), 0.0)
    rd = 1.0 / (iv + 1.5 * s)
    c = s * rd
    g_re, g_im = s * a_re, s * a_im
    h_re = jnp.where(inside, q_re, 0.0) - 1.5 * g_re
    h_im = jnp.where(inside, q_im, 0.0) - 1.5 * g_im
    scale = jnp.where(inside, relaxation * rd, 0.0)
    c2 = jnp.concatenate([c, c], axis=0)
    b2 = jnp.concatenate([g_re + c * h_re, g_im + c * h_im], axis=0)
    half = v.shape[1] // 2
    lane = lax.broadcasted_iota(jnp.int32, (2 * v.shape[0], half), 1)
    low = jnp.concatenate([g_re[:, :half], g_im[:, :half]], axis=0)
    high = jnp.concatenate([g_re[:, half:], g_im[:, half:]], axis=0)
    sign = jnp.concatenate([v[:, :half], v[:, :half]], axis=0)
    edges = jnp.where(lane < 2, low, jnp.where(lane >= half - 2, high, sign)).T
    return c2, b2, h_re, h_im, scale, edges


def orders(sign_row):
    width = sign_row.shape[1]
    pos = jnp.broadcast_to(sign_row, (SEGS, width)) > 0.0
    seg = lax.broadcasted_iota(jnp.int32, (SEGS, width), 0)
    return pos, jnp.where(pos, SEGS - 1 - seg, seg)


def before(value, reach, fill, pos, order):
    up = pltpu.roll(value, reach, 0)
    down = pltpu.roll(value, SEGS - reach, 0)
    return jnp.where(order >= reach, jnp.where(pos, down, up), fill)


def segment_scan(slots, c_t, b_t, c_s, b_s, poses):
    steps = c_s.shape[1]
    width = c_s.shape[3]
    zero = jnp.zeros((SEGS, width), F32)
    real = lax.broadcasted_iota(jnp.int32, (SEGS, width), 1) < width // 2
    first, second = jnp.where(real, 1.0, 0.0), jnp.where(real, 0.0, 1.0)
    state = [(zero, zero, first, second) for _ in slots]
    for t in range(steps):
        for i, k in enumerate(slots):
            pos = poses[i]
            y1, y2, n1, n2 = state[i]
            lo, hi = pl.ds(t, SEGS, stride=steps), pl.ds(steps - 1 - t, SEGS, stride=steps)
            cs, bs = c_t.at[k], b_t.at[k]
            c = jnp.where(pos, cs[hi, :], cs[lo, :])
            b = jnp.where(pos, bs[hi, :], bs[lo, :])
            c_s[k, t] = c
            b_s[k, t] = b
            c1, c2 = 2.0 * c, -0.5 * c
            state[i] = ((b + c2 * y2) + c1 * y1, y1, c2 * n2 + c1 * n1, n1)
    return state


def compose(state, pos, order):
    y1, y2, n1, n2 = state
    width = y1.shape[1]
    real = lax.broadcasted_iota(jnp.int32, (SEGS, width), 1) < width // 2
    o1, o2 = pltpu.roll(n1, width // 2, 1), pltpu.roll(n2, width // 2, 1)
    m11, m12 = jnp.where(real, n1, o1), jnp.where(real, o1, n1)
    m21, m22 = jnp.where(real, n2, o2), jnp.where(real, o2, n2)
    v1, v2 = y1, y2
    prev = functools.partial(before, pos=pos, order=order)
    for reach in (1, 2, 4):
        a11, a12 = prev(m11, reach, 1.0), prev(m12, reach, 0.0)
        a21, a22 = prev(m21, reach, 0.0), prev(m22, reach, 1.0)
        u1, u2 = prev(v1, reach, 0.0), prev(v2, reach, 0.0)
        m11, m12, m21, m22, v1, v2 = (
            m11 * a11 + m12 * a21,
            m11 * a12 + m12 * a22,
            m21 * a11 + m22 * a21,
            m21 * a12 + m22 * a22,
            m11 * u1 + m12 * u2 + v1,
            m21 * u1 + m22 * u2 + v2,
        )
    entry = (
        prev(v1, 1, 0.0),
        prev(v2, 1, 0.0),
        jnp.where(real, prev(m11, 1, 1.0), prev(m12, 1, 0.0)),
        jnp.where(real, prev(m21, 1, 0.0), prev(m22, 1, 1.0)),
    )
    return (m11, m12, m21, m22, v1, v2), entry


def put_maps(msg_ref, sign_ref, ent_ref, k, slot, state, edges):
    half = edges.shape[0]
    sign_row = edges[half // 2 : half // 2 + 1]
    pos, order = orders(sign_row)
    maps, entry = compose(state, pos, order)
    up = sign_row > 0.0
    for row, value in enumerate(maps):
        msg_ref[row, k : k + 1, :] = jnp.where(up, value[0:1], value[SEGS - 1 : SEGS])
    msg_ref[6, k : k + 1, :] = jnp.where(up, edges[0:1], edges[half - 1 : half])
    msg_ref[7, k : k + 1, :] = jnp.where(up, edges[1:2], edges[half - 2 : half - 1])
    sign_ref[k : k + 1, :] = sign_row
    for row, value in enumerate(entry):
        ent_ref[slot, row] = value


def main_maps(
    adj_ref, len_hbm, src_hbm, speed_hbm, inv_hbm,
    msg_ref, sign_ref, ent_ref, c_s, b_s, h_ref, scale_ref, in_ref, src_ref, speed_ref, inv_ref,
    c_t, b_t, len_ref, sems,
):
    vars_, lines, cells = speed_ref.shape
    first = pltpu.make_async_copy(len_hbm, len_ref, sems.at[0])
    first.start()
    copies = []
    for k in range(vars_):
        copies.append([
            pltpu.make_async_copy(speed_hbm.at[k], speed_ref.at[k], sems.at[3 * k + 1]),
            pltpu.make_async_copy(inv_hbm.at[k], inv_ref.at[k], sems.at[3 * k + 2]),
            pltpu.make_async_copy(src_hbm.at[:, k], src_ref.at[:, k], sems.at[3 * k + 3]),
        ])
        for copy in copies[k]:
            copy.start()
    first.wait()
    inside = cells_inside(len_ref, cells)
    in_ref[...] = jnp.where(inside, 1.0, 0.0)
    all_edges, poses = [], []
    for k in range(vars_):
        for copy in copies[k]:
            copy.wait()
        a_re, a_im = adj_ref[0, k], adj_ref[1, k]
        q_re = src_ref[0, k] + frequency * a_im
        q_im = src_ref[1, k] - frequency * a_re
        c2, b2, h_re, h_im, scale, edges = cell_terms(
            speed_ref[k], inv_ref[k], a_re, a_im, q_re, q_im, inside)
        h_ref[0, k], h_ref[1, k] = h_re, h_im
        scale_ref[k] = scale
        c_t[k] = c2.T
        b_t[k] = b2.T
        all_edges.append(edges)
        mid = edges.shape[0] // 2
        poses.append(orders(edges[mid : mid + 1])[0])
    states = segment_scan(range(vars_), c_t, b_t, c_s, b_s, poses)
    for k in range(vars_):
        put_maps(msg_ref, sign_ref, ent_ref, k, k, states[k], all_edges[k])


def face_maps(
    counts, in_ref, adj_ref, src_ref, speed_ref, inv_ref, old_msg, old_sign, *rest
):
    recv = rest[: len(counts)]
    msg_ref, sign_ref, ent_ref, c_s, b_s, h_ref, c_t, b_t = rest[len(counts) :]
    vars_, lines, cells = speed_ref.shape
    sub = lax.broadcasted_iota(jnp.int32, (FACE_DEV, 128), 0).astype(F32)
    acc = [jnp.zeros((FACE_DEV, 128), F32) for _ in range(4 * vars_)]
    for ref, number in zip(recv, counts):
        for e in range(number):
            hit = jnp.broadcast_to(ref[e, 20:21, :], (FACE_DEV, 128)) == sub
            for j in range(4 * vars_):
                row = jnp.broadcast_to(ref[e, j : j + 1, :], (FACE_DEV, 128))
                acc[j] = acc[j] + jnp.where(hit, row, 0.0)
    picks = [min(k, vars_ - 1) for k in range(lines // FACE_DEV)]

    def gather(ref):
        return jnp.concatenate([ref[k, :FACE_DEV] for k in picks], axis=0)

    def faces(j):
        return jnp.concatenate(
            [jnp.concatenate([acc[4 * k + j], acc[4 * k + j + 1]], axis=1) for k in picks], axis=0)

    a_re, a_im = gather(adj_ref.at[0]), gather(adj_ref.at[1])
    q_re = gather(src_ref.at[0]) + frequency * a_im - faces(0)
    q_im = gather(src_ref.at[1]) - frequency * a_re - faces(2)
    inside = jnp.concatenate([in_ref[:FACE_DEV]] * len(picks), axis=0) > 0.0
    c2, b2, h_re, h_im, _, edges = cell_terms(
        gather(speed_ref), gather(inv_ref), a_re, a_im, q_re, q_im, inside)
    h_ref[:lines], h_ref[lines:] = h_re, h_im
    c_t[0] = c2.T
    b_t[0] = b2.T
    mid = edges.shape[0] // 2
    state = segment_scan([0], c_t, b_t, c_s, b_s, [orders(edges[mid : mid + 1])[0]])[0]
    msg_ref[...] = old_msg[...]
    sign_ref[...] = old_sign[...]
    put_maps(msg_ref, sign_ref, ent_ref, vars_, 0, state, edges)


def substitute(
    in_ref, adj_ref, speed_ref, sign_ref, ent_ref, c_s, b_s, h_ref, scale_ref,
    ent_f, c_f, b_f, h_f, low_ref, high_ref,
    part_ref, lift_ref, out_hbm,
    u_s, x_s, u_t, x_t, out_ref, sems,
):
    vars_, lines, cells = speed_ref.shape
    steps, width = c_s.shape[1], c_s.shape[3]
    groups = vars_ + 1
    inside = in_ref[...] > 0.0
    lane = lax.broadcasted_iota(jnp.int32, (lines, cells), 1)
    place = lax.axis_index("ax")
    up_all = sign_ref[...] > 0.0
    near = jnp.where(place >= 1, 1.0, 0.0)
    far = jnp.where(place + 1 <= lax.axis_size("ax") - 1, 1.0, 0.0)
    has = jnp.where(up_all, far, near) > 0.0
    g1 = jnp.where(has, jnp.where(up_all, high_ref[6], low_ref[6]), 0.0)
    g2 = jnp.where(has, jnp.where(up_all, high_ref[7], low_ref[7]), 0.0)
    r0, r1 = 2.0 * g1 - 0.5 * g2, -0.5 * g1
    table = jnp.concatenate(
        [jnp.where(up_all, 0.0, r0), jnp.where(up_all, 0.0, r1),
         jnp.where(up_all, r0, 0.0), jnp.where(up_all, r1, 0.0)]
        + [jnp.zeros((TABLE, width), F32)] * (width // TABLE - 4), axis=0).T
    copies = []
    for k in range(vars_):
        v = speed_ref[k]
        s = jnp.where(inside, jnp.abs(v), 0.0)
        up = v > 0.0
        apart = lane != jnp.where(up, cells - 1, 0)

        def shifted(value):
            return jnp.where(
                apart, jnp.where(up, pltpu.roll(value, cells - 1, 1), pltpu.roll(value, 1, 1)), 0.0)

        for part in range(2):
            at = part * lines + FACE_DEV * k
            h = jnp.concatenate([h_f[at : at + FACE_DEV], h_ref[part, k, FACE_DEV:]], axis=0)
            g = s * adj_ref[part, k]
            rows = table[part * lines : (part + 1) * lines]
            column = lambda r: rows[:, TABLE * r + k : TABLE * r + k + 1]
            flux = shifted(2.0 * g - 0.5 * shifted(g))
            flux = jnp.where(lane == 0, flux + column(0), flux)
            flux = jnp.where(lane == 1, flux + column(1), flux)
            flux = jnp.where(lane == cells - 1, flux + column(2), flux)
            flux = jnp.where(lane == cells - 2, flux + column(3), flux)
            out_ref[part, k] = h + jnp.where(inside, flux, 0.0)
            copies.append(pltpu.make_async_copy(
                out_ref.at[part, k], out_hbm.at[part, k], sems.at[2 * k + part]))
            copies[-1].start()
    poses = [jnp.broadcast_to(sign_ref[k : k + 1, :], (SEGS, width)) > 0.0 for k in range(groups)]
    state = []
    for k in range(groups):
        ent = ent_ref.at[k] if k < vars_ else ent_f.at[0]
        state.append([ent[r] for r in range(4)])
    for t in range(steps):
        lo = pl.ds(steps - 1 - t, SEGS, stride=steps)
        hi = pl.ds(t, SEGS, stride=steps)
        for k in range(groups):
            main = k < vars_
            c = c_s[k, t] if main else c_f[0, t]
            b = b_s[k, t] if main else b_f[0, t]
            y1, y2, n1, n2 = state[k]
            u = 2.0 * y1 - 0.5 * y2
            x = 2.0 * n1 - 0.5 * n2
            new = c * u + b
            state[k] = [new, y1, c * x if main else n1, n1]
            for value, keep, turned in ((u, u_s, u_t), (x, x_s, x_t))[: 2 if main else 1]:
                if t < steps // 2:
                    keep[k, t] = value
                else:
                    other = keep[k, steps - 1 - t]
                    turned.at[k][lo, :] = jnp.where(poses[k], value, other)
                    turned.at[k][hi, :] = jnp.where(poses[k], other, value)
    face_u = u_t[vars_].T
    for k in range(vars_):
        scale = scale_ref[k]
        u = u_t[k].T
        x = x_t[k].T
        for part in range(2):
            at = part * lines + FACE_DEV * k
            lift_ref[part, k] = x[part * lines : (part + 1) * lines] * scale
            h = jnp.concatenate([h_f[at : at + FACE_DEV], h_ref[part, k, FACE_DEV:]], axis=0)
            us = jnp.concatenate(
                [face_u[at : at + FACE_DEV], u[part * lines + FACE_DEV : (part + 1) * lines]], axis=0)
            part_ref[part, k] = jnp.where(inside, adj_ref[part, k], 0.0) + (h + us) * scale
    for copy in copies:
        copy.wait()


def finish(count, sign_ref, part_ref, lift_ref, *rest):
    got = rest[: count - 1]
    new_hbm, new_ref, sems = rest[count - 1 :]
    _, vars_, lines, cells = part_ref.shape
    width = 2 * lines
    place = lax.axis_index("ax")
    pos = sign_ref[...] > 0.0
    zero = jnp.zeros((TABLE, width), F32)
    z1, z2 = zero, zero
    for i in range(count - 1, 0, -1):
        low, high = got[i - 1], got[count - i - 1]
        near = jnp.where(place >= i, 1.0, 0.0)
        far = jnp.where(place + i <= count - 1, 1.0, 0.0)
        has = jnp.where(pos, far, near) > 0.0
        m = [jnp.where(pos, high[r], low[r]) for r in range(6)]
        n1 = m[0] * z1 + m[1] * z2 + m[4]
        n2 = m[2] * z1 + m[3] * z2 + m[5]
        z1, z2 = jnp.where(has, n1, z1), jnp.where(has, n2, z2)
    table = jnp.concatenate([z1, z2] + [zero] * (width // TABLE - 2), axis=0).T
    copies = []
    for k in range(vars_):
        for part in range(2):
            at = part * lines + FACE_DEV * k

            def entering(r):
                face, main = TABLE * r + vars_, TABLE * r + k
                return jnp.concatenate(
                    [table[at : at + FACE_DEV, face : face + 1],
                     table[part * lines + FACE_DEV : (part + 1) * lines, main : main + 1]], axis=0)

            new_ref[part, k] = part_ref[part, k] + (
                lift_ref[0, k] * entering(0) + lift_ref[1, k] * entering(1))
            copies.append(pltpu.make_async_copy(
                new_ref.at[part, k], new_hbm.at[part, k], sems.at[2 * k + part]))
            copies[-1].start()
    for copy in copies:
        copy.wait()


def shards(adjoint, source, speed, inverse_step, coupling, face_line, face_owner, line_length):
    lines, rows, cells = adjoint.shape
    vars_ = speed.shape[1]
    faces = face_line.shape[0]
    blocks = lax.axis_size("xs")
    count = lax.axis_size("ax")
    cap = max(1, faces // blocks)
    width = 2 * lines
    steps = cells // SEGS
    adj = jnp.transpose(adjoint, (1, 0, 2)).reshape(2, vars_, lines, cells)
    src = jnp.transpose(source, (1, 0, 2)).reshape(2, vars_, lines, cells)
    spd = jnp.transpose(speed, (1, 0, 2))
    inv = jnp.transpose(inverse_step, (1, 0, 2))
    cpl = jnp.transpose(coupling, (1, 0, 2))
    vmem = pl.BlockSpec(memory_space=pltpu.VMEM)
    hbm = pl.BlockSpec(memory_space=pltpu.HBM)
    stay = lambda x: pltpu.with_memory_space_constraint(x, pltpu.HBM)
    shape = lambda *dims: jax.ShapeDtypeStruct(dims, F32)
    scratch = lambda *dims: pltpu.VMEM(dims, F32)
    dma = lambda number: pltpu.SemaphoreType.DMA((number,))
    limit = lambda mib: pltpu.CompilerParams(vmem_limit_bytes=mib << 20)
    cost = lambda flops, moved: pl.CostEstimate(
        flops=flops, bytes_accessed=moved, transcendentals=0)
    table_shape = shape(8, TABLE, width)
    sign_shape = shape(TABLE, width)
    order_shape = shape(vars_, steps, SEGS, width)
    field_shape = shape(2, vars_, lines, cells)
    var_shape = shape(vars_, lines, cells)
    face_order = shape(1, steps, SEGS, width)
    paired = blocks == 8
    entries = blocks * cap
    pieces = blocks // 2 if paired else 1
    adj, *packed = pl.pallas_call(
        functools.partial(pack_faces, blocks, cap, paired),
        out_shape=[field_shape] + [shape(entries // pieces, PACK_ROWS, cells // 2)] * pieces,
        in_specs=[hbm] * 4,
        out_specs=[vmem] * (1 + pieces),
        scratch_shapes=[scratch(entries, PACK_ROWS, cells // 2), pltpu.SMEM((faces,), jnp.int32),
                        pltpu.SMEM((faces,), jnp.int32), scratch(vars_, faces, cells), dma(3 + vars_)],
        compiler_params=limit(6),
        name="pack_faces",
    )(stay(face_line), stay(face_owner), stay(adj), stay(cpl))
    hop = lambda x, m: lax.ppermute(x, "xs", [(i, i ^ m) for i in range(blocks)])
    if paired:
        landed = [packed[0]] + [hop(packed[m], 2 * m) for m in range(1, pieces)]
    msg, sign, ent, c_s, b_s, h, scale, mask, src, spd, inv = pl.pallas_call(
        main_maps,
        out_shape=[table_shape, sign_shape, shape(vars_, 4, SEGS, width), order_shape, order_shape,
                   field_shape, var_shape, shape(lines, cells), field_shape, var_shape, var_shape],
        in_specs=[vmem] + [hbm] * 4,
        out_specs=[vmem] * 11,
        scratch_shapes=[scratch(vars_, cells, width)] * 2
        + [pltpu.VMEM((1, lines), jnp.int32), dma(1 + 3 * vars_)],
        compiler_params=limit(14),
        cost_estimate=cost(2 * 10**6, 4 * 10**6),
        name="main_maps",
    )(adj, stay(line_length.reshape(1, lines)), stay(src), stay(spd), stay(inv))
    if paired:
        halves = shape(pieces * cap, PACK_ROWS, cells // 2)
        near_half, far_half = pl.pallas_call(
            functools.partial(sort_halves, cap),
            out_shape=[halves] * 2,
            in_specs=[vmem] * (1 + pieces),
            out_specs=[vmem] * 2,
            compiler_params=limit(4),
            name="sort_halves",
        )(sign, *landed)
        recv, counts = [near_half, hop(far_half, 1)], [pieces * cap] * 2
    else:
        recv, counts = [lax.all_to_all(packed[0], "xs", 0, 0, tiled=True)], [entries]
    msg, sign, ent_f, c_f, b_f, h_f = pl.pallas_call(
        functools.partial(face_maps, counts),
        out_shape=[table_shape, sign_shape, shape(1, 4, SEGS, width), face_order, face_order,
                   shape(width, cells)],
        in_specs=[vmem] * (7 + len(recv)),
        out_specs=[vmem] * 6,
        scratch_shapes=[scratch(1, cells, width)] * 2,
        compiler_params=limit(10),
        name="face_maps",
    )(mask, adj, src, spd, inv, msg, sign, *recv)
    shift = lambda k: lax.ppermute(msg, "ax", [(i, (i + k) % count) for i in range(count)])
    got = [shift(k) for k in range(1, count)]
    kept = scratch(vars_ + 1, steps // 2, SEGS, width)
    part, lift, out = pl.pallas_call(
        substitute,
        out_shape=[field_shape] * 3,
        in_specs=[vmem] * 15,
        out_specs=[vmem] * 2 + [hbm],
        scratch_shapes=[kept, kept, scratch(vars_ + 1, cells, width), scratch(vars_, cells, width),
                        scratch(2, vars_, lines, cells), dma(2 * vars_)],
        compiler_params=limit(18),
        cost_estimate=cost(2 * 10**6, 5 * 10**6),
        name="substitute",
    )(mask, adj, spd, sign, ent, c_s, b_s, h, scale, ent_f, c_f, b_f, h_f, got[0], got[-1])
    new = pl.pallas_call(
        functools.partial(finish, count),
        out_shape=field_shape,
        in_specs=[vmem] * (3 + len(got)),
        out_specs=hbm,
        scratch_shapes=[scratch(2, vars_, lines, cells), dma(2 * vars_)],
        compiler_params=limit(6),
        name="finish",
    )(sign, part, lift, *got)
    back = lambda x: jnp.transpose(x.reshape(rows, lines, cells), (1, 0, 2))
    return (back(new), back(out))


def solution(mesh):
    line = P("xs", None, "ax")
    in_specs = (line,) * 5 + (P("xs"),) * 3
    return jax.shard_map(
        shards, mesh=mesh, in_specs=in_specs, out_specs=(line, line), check_vma=False
    )
```

profile of v0, /device:TPU:0, one launch (start us, length us, event | category | flops | bytes accessed | tf_op | source)
XLA Modules:
  0.0 27.5 jit_solution(4800320170623150935)
XLA Ops:
  0.6 1.3 %pack_faces.1 = (f32[2,5,64,256]{3,2,1,0:T(8,128)S(1)}, f32[4,24,128]{2,1,0:T(8,128)S(1)}, f32[4,24,128]{2,1,0:T(8,128)S(1)}, f32[4,24,128]{2,1,0:T(8,128)S(1)}, f32[4,24,128]{2,1,0:T(8,128)S(1)}) custom-call(s32[16]{0:T(128)} %line_hbm.1, s32[16]{0:T(128)} %owner_hbm.1, f32[2,5,64,256]{3,2,1,0:T(8,128)} %bitcast.16, f32[5,16,256]{2,1,0:T(8,128)} %bitcast.21), custom_call_target="tpu_custom_call" | custom-call | tf_op jit(solution)/shard_map/pack_faces/pallas_call | solution.py:428
  2.0 3.0 %collective-permute-start = (f32[4,24,128]{2,1,0:T(8,128)S(1)}, f32[4,24,128]{2,1,0:T(8,128)S(1)}, u32[]{:S(2)}, u32[]{:S(2)}) collective-permute-start(f32[4,24,128]{2,1,0:T(8,128)S(1)} %get-tuple-element.37), channel_id=1, source_target_pairs={{0,2},{1,3},{2,0},{3,1},{4,6},{5,7},{6,4},{7,5},{8,10},{9,11},{10,... | collective-permute-start | bytes 147464 | tf_op jit(solution)/shard_map/ppermute | solution.py:438
  5.0 1.5 %collective-permute-start.1 = (f32[4,24,128]{2,1,0:T(8,128)S(1)}, f32[4,24,128]{2,1,0:T(8,128)S(1)}, u32[]{:S(2)}, u32[]{:S(2)}) collective-permute-start(f32[4,24,128]{2,1,0:T(8,128)S(1)} %get-tuple-element.38), channel_id=1, source_target_pairs={{0,4},{1,5},{2,6},{3,7},{4,0},{5,1},{6,2},{7,3},{8,12},{9,13},{10,... | collective-permute-start | bytes 147464 | tf_op jit(solution)/shard_map/ppermute | solution.py:438
  6.5 0.0 collective-permute-start.2
  6.5 3.4 %main_maps.1 = (f32[8,8,128]{2,1,0:T(8,128)S(1)}, f32[8,128]{1,0:T(8,128)S(1)}, f32[5,4,8,128]{3,2,1,0:T(8,128)S(1)}, f32[5,32,8,128]{3,2,1,0:T(8,128)S(1)}, f32...) custom-call(f32[2,5,64,256]{3,2,1,0:T(8,128)S(1)} %get-tuple-element, ...), custom_call_target="tpu_custom_call" | custom-call | flops 2000000 | bytes 4000000 | tf_op jit(solution)/shard_map/main_maps/pallas_call | solution.py:441
  9.9 0.0 collective-permute-done.refs_1_
  9.9 0.0 collective-permute-done.1.refs_2_
  9.9 1.5 %collective-permute-done.2.refs_3_ = f32[4,24,128]{2,1,0:T(8,128)S(1)} collective-permute-done((f32[4,24,128]{2,1,0:T(8,128)S(1)}, f32[4,24,128]{2,1,0:T(8,128)S(1)}, u32[]{:S(2)}, u32[]{:S(2)}) %collective-permute-start.2) | collective-permute-done | bytes 49184 | tf_op jit(solution)/shard_map/ppermute | solution.py:438
  11.5 0.1 collective-permute-start.3
  11.6 1.3 %collective-permute-done.3.rest_1_ = f32[8,24,128]{2,1,0:T(8,128)S(1)} collective-permute-done((f32[8,24,128]{2,1,0:T(8,128)S(1)}, f32[8,24,128]{2,1,0:T(8,128)S(1)}, u32[]{:S(2)}, u32[]{:S(2)}) %collective-permute-start.3) | collective-permute-done | bytes 98336 | tf_op jit(solution)/shard_map/ppermute | solution.py:438
  12.9 0.5 %face_maps.1 = (f32[8,8,128]{2,1,0:T(8,128)S(1)}, f32[8,128]{1,0:T(8,128)S(1)}, f32[1,4,8,128]{3,2,1,0:T(8,128)S(1)}, f32[1,32,8,128]{3,2,1,0:T(8,128)S(1)}, f32...) custom-call(f32[64,256]{1,0:T(8,128)S(1)} %get-tuple-element.30.in_ref, ...), custom_call_target="tpu_custom_call" | custom-call | tf_op jit(solution)/shard_map/face_maps/pallas_call | solution.py:466
  13.4 3.7 %collective-permute-start.5 = (f32[8,8,128]{2,1,0:T(8,128)S(1)}, f32[8,8,128]{2,1,0:T(8,128)S(1)}, u32[]{:S(2)}, u32[]{:S(2)}) collective-permute-start(f32[8,8,128]{2,1,0:T(8,128)S(1)} %get-tuple-element.52), channel_id=1, source_target_pairs={{0,24},{8,0},{16,8},{24,16},{1,25},{9,1},{17,9},{25,17},{2,26},{10... | collective-permute-start | bytes 98312 | tf_op jit(solution)/shard_map/ppermute | solution.py:476
  17.0 0.0 collective-permute-start.4
  17.0 1.0 %collective-permute-start.6 = (f32[8,8,128]{2,1,0:T(8,128)S(1)}, f32[8,8,128]{2,1,0:T(8,128)S(1)}, u32[]{:S(2)}, u32[]{:S(2)}) collective-permute-start(f32[8,8,128]{2,1,0:T(8,128)S(1)} %get-tuple-element.52), channel_id=1, source_target_pairs={{0,16},{8,24},{16,0},{24,8},{1,17},{9,25},{17,1},{25,9},{2,18},{10... | collective-permute-start | bytes 98312 | tf_op jit(solution)/shard_map/ppermute | solution.py:476
  18.1 0.7 %collective-permute-done.5.high_ref.rest_2_ = f32[8,8,128]{2,1,0:T(8,128)S(1)} collective-permute-done((f32[8,8,128]{2,1,0:T(8,128)S(1)}, f32[8,8,128]{2,1,0:T(8,128)S(1)}, u32[]{:S(2)}, u32[]{:S(2)}) %collective-permute-start.5) | collective-permute-done | bytes 32800 | tf_op jit(solution)/shard_map/ppermute | solution.py:476
  18.7 4.0 %collective-permute-done.4.low_ref.rest_0_ = f32[8,8,128]{2,1,0:T(8,128)S(1)} collective-permute-done((f32[8,8,128]{2,1,0:T(8,128)S(1)}, f32[8,8,128]{2,1,0:T(8,128)S(1)}, u32[]{:S(2)}, u32[]{:S(2)}) %collective-permute-start.4) | collective-permute-done | bytes 32800 | tf_op jit(solution)/shard_map/ppermute | solution.py:476
  22.8 3.1 %substitute.1 = (f32[2,5,64,256]{3,2,1,0:T(8,128)S(1)}, f32[2,5,64,256]{3,2,1,0:T(8,128)S(1)}, f32[2,5,64,256]{3,2,1,0:T(8,128)}) custom-call(f32[64,256]{1,0:T(8,128)S(1)} %get-tuple-element.30.in_ref, f32[2,5,64,256]{3,2,1,0:T(8,128)S(1)} %get-tuple-element.29.adj_ref, f32[5,64,256]{2,1,0:T(8,128)S(1)} %get-tuple-element.32.speed_ref, ...), custom_call_target="tpu_custom_call" | custom-call | flops 2000000 | bytes 5000000 | tf_op jit(solution)/shard_map/substitute/pallas_call | solution.py:479
  25.9 0.0 collective-permute-done.6.rest_1_
  25.9 1.6 %finish.1 = f32[2,5,64,256]{3,2,1,0:T(8,128)} custom-call(f32[8,128]{1,0:T(8,128)S(1)} %get-tuple-element.42.sign_ref, f32[2,5,64,256]{3,2,1,0:T(8,128)S(1)} %get-tuple-element.53.part_ref, f32[2,5,64,256]{3,2,1,0:T(8,128)S(1)} %get-tuple-element.54.lift_ref, f32[8,8,128]{2,1,0:T(8,128)S(1)} %collective-permute-done.4.low_ref.rest_0_, ...), custom_call_target="tpu_custom_call" | custom-call | tf_op jit(solution)/shard_map/finish/pallas_call | solution.py:490
  (1 shorter events, 0.0 us)
Async XLA Ops:
  2.0 7.9 %collective-permute-start = (f32[4,24,128]{2,1,0:T(8,128)S(1)}, f32[4,24,128]{2,1,0:T(8,128)S(1)}, u32[]{:S(2)}, u32[]{:S(2)}) collective-permute-start(f32[4,24,128]{2,1,0:T(8,128)S(1)} %get-tuple-element.37), channel_id=1, source_target_pairs={{0,2},{1,3},{2,0},{3,1},{4,6},{5,7},{6,4},{7,5},{8,10},{9,11},{10,... | collective-permute-start | bytes 147464 | tf_op jit(solution)/shard_map/ppermute | solution.py:438
  5.0 5.0 %collective-permute-start.1 = (f32[4,24,128]{2,1,0:T(8,128)S(1)}, f32[4,24,128]{2,1,0:T(8,128)S(1)}, u32[]{:S(2)}, u32[]{:S(2)}) collective-permute-start(f32[4,24,128]{2,1,0:T(8,128)S(1)} %get-tuple-element.38), channel_id=1, source_target_pairs={{0,4},{1,5},{2,6},{3,7},{4,0},{5,1},{6,2},{7,3},{8,12},{9,13},{10,... | collective-permute-start | bytes 147464 | tf_op jit(solution)/shard_map/ppermute | solution.py:438
  6.5 5.0 %collective-permute-start.2 = (f32[4,24,128]{2,1,0:T(8,128)S(1)}, f32[4,24,128]{2,1,0:T(8,128)S(1)}, u32[]{:S(2)}, u32[]{:S(2)}) collective-permute-start(f32[4,24,128]{2,1,0:T(8,128)S(1)} %get-tuple-element.39), channel_id=1, source_target_pairs={{0,6},{1,7},{2,4},{3,5},{4,2},{5,3},{6,0},{7,1},{8,14},{9,15},{10,... | collective-permute-start | bytes 147464 | tf_op jit(solution)/shard_map/ppermute | solution.py:438
  11.5 1.4 %collective-permute-start.3 = (f32[8,24,128]{2,1,0:T(8,128)S(1)}, f32[8,24,128]{2,1,0:T(8,128)S(1)}, u32[]{:S(2)}, u32[]{:S(2)}) collective-permute-start(f32[8,24,128]{2,1,0:T(8,128)S(1)} %get-tuple-element.41), channel_id=1, source_target_pairs={{0,1},{1,0},{2,3},{3,2},{4,5},{5,4},{6,7},{7,6},{8,9},{9,8},{10,11... | collective-permute-start | bytes 294920 | tf_op jit(solution)/shard_map/ppermute | solution.py:438
  13.4 5.3 %collective-permute-start.5 = (f32[8,8,128]{2,1,0:T(8,128)S(1)}, f32[8,8,128]{2,1,0:T(8,128)S(1)}, u32[]{:S(2)}, u32[]{:S(2)}) collective-permute-start(f32[8,8,128]{2,1,0:T(8,128)S(1)} %get-tuple-element.52), channel_id=1, source_target_pairs={{0,24},{8,0},{16,8},{24,16},{1,25},{9,1},{17,9},{25,17},{2,26},{10... | collective-permute-start | bytes 98312 | tf_op jit(solution)/shard_map/ppermute | solution.py:476
  17.0 5.7 %collective-permute-start.4 = (f32[8,8,128]{2,1,0:T(8,128)S(1)}, f32[8,8,128]{2,1,0:T(8,128)S(1)}, u32[]{:S(2)}, u32[]{:S(2)}) collective-permute-start(f32[8,8,128]{2,1,0:T(8,128)S(1)} %get-tuple-element.52), channel_id=1, source_target_pairs={{0,8},{8,16},{16,24},{24,0},{1,9},{9,17},{17,25},{25,1},{2,10},{10... | collective-permute-start | bytes 98312 | tf_op jit(solution)/shard_map/ppermute | solution.py:476
  17.0 8.9 %collective-permute-start.6 = (f32[8,8,128]{2,1,0:T(8,128)S(1)}, f32[8,8,128]{2,1,0:T(8,128)S(1)}, u32[]{:S(2)}, u32[]{:S(2)}) collective-permute-start(f32[8,8,128]{2,1,0:T(8,128)S(1)} %get-tuple-element.52), channel_id=1, source_target_pairs={{0,16},{8,24},{16,0},{24,8},{1,17},{9,25},{17,1},{25,9},{2,18},{10... | collective-permute-start | bytes 98312 | tf_op jit(solution)/shard_map/ppermute | solution.py:476
where the time goes:
time: 27.7 us; the launch traced here: 27.5 us
  Pallas kernels  10 us (36%)
  starting transfers between devices  9.28 us (34%)
  waiting for transfers between devices  7.54 us (27%)
  between operations  0.7 us (3%)
    ppermute x3, waiting for transfers between devices, shards(): lax.ppermute(msg, 'ax', [(i, (i + k) % count) for i in range(count)])  4.7 us
    ppermute x3, starting transfers between devices, shards(): lax.ppermute(msg, 'ax', [(i, (i + k) % count) for i in range(count)])  4.67 us
    ppermute x4, starting transfers between devices, shards(): lax.ppermute(x, 'xs', [(i, i ^ m) for i in range(blocks)])  4.61 us
    pallas_call x1, Pallas kernels, shards(): pl.pallas_call(main_maps, out_shape=[table_shape, sign_shape, shape(vars_...  3.39 us
    pallas_call x1, Pallas kernels, shards(): pl.pallas_call(substitute, out_shape=[field_shape] * 3, in_specs=[vmem] *...  3.13 us
    ppermute x4, waiting for transfers between devices, shards(): lax.ppermute(x, 'xs', [(i, i ^ m) for i in range(blocks)])  2.84 us
    pallas_call x1, Pallas kernels, shards(): pl.pallas_call(functools.partial(finish, count), out_shape=field_shape, i...  1.62 us
    pallas_call x1, Pallas kernels, shards(): pl.pallas_call(functools.partial(pack_faces, blocks, cap, paired), out_sh...  1.32 us
  transfers between devices with their start and end apart: 7, of which 4 were waited for; matrix products, arithmetic and copies ran while one was open for 0% of the time, Pallas kernels for 24%

commit v1 on v0

v1 whole, which is shorter than its diff:
```python
import functools
import jax
import jax.numpy as jnp
from jax import lax
from jax.experimental import pallas as pl
from jax.experimental.pallas import tpu as pltpu
from jax.sharding import PartitionSpec as P

FACE_DEV = 8

frequency = 0.7
relaxation = 0.02

SEGS = 8
PACK_ROWS = 24
TABLE = 8
F32 = jnp.float32


def pack_faces(blocks, cap, paired, line_hbm, owner_hbm, adj_hbm, coup_hbm, len_hbm, *rest):
    adj_ref, len_ref = rest[:2]
    outs = rest[2:-5]
    stage, line_ref, owner_ref, coup_ref, sems = rest[-5:]
    vars_, faces, cells = coup_ref.shape
    half = cells // 2
    slots = FACE_DEV * blocks
    small = [
        pltpu.make_async_copy(owner_hbm, owner_ref, sems.at[0]),
        pltpu.make_async_copy(line_hbm, line_ref, sems.at[1]),
        pltpu.make_async_copy(coup_hbm, coup_ref, sems.at[2]),
        pltpu.make_async_copy(len_hbm, len_ref, sems.at[3]),
    ]
    large = [
        pltpu.make_async_copy(adj_hbm.at[:, k], adj_ref.at[:, k], sems.at[4 + k])
        for k in range(vars_)
    ]
    for copy in small + large:
        copy.start()
    for copy in small[:2]:
        copy.wait()
    if blocks * cap != faces:
        for e in range(blocks * cap):
            stage[e, 16:24, :] = jnp.full((8, 128), -1.0, F32)
    dests, places = [], []
    for f in range(faces):
        slot = lax.rem(owner_ref[f], slots)
        dest = lax.div(slot, FACE_DEV)
        spot = jnp.int32(0)
        for other in dests:
            spot = spot + (other == dest).astype(jnp.int32)
        dests.append(dest)
        if paired:
            dest = lax.bitwise_xor(dest, lax.axis_index("xs"))
        entry = dest * cap + jnp.minimum(spot, cap - 1)
        places.append((entry, line_ref[f]))
        number = lax.rem(slot, FACE_DEV).astype(F32)
        stage[entry, 20:24, :] = jnp.full((4, 128), number, F32)
    small[2].wait()
    for k in range(vars_):
        large[k].wait()
        for f, (entry, line) in enumerate(places):
            c = coup_ref[k, f : f + 1, :]
            re = c * adj_ref[0, k, pl.ds(line, 1), :]
            im = c * adj_ref[1, k, pl.ds(line, 1), :]
            stage[entry, 4 * k : 4 * k + 1, :] = re[:, :half]
            stage[entry, 4 * k + 1 : 4 * k + 2, :] = re[:, half:]
            stage[entry, 4 * k + 2 : 4 * k + 3, :] = im[:, :half]
            stage[entry, 4 * k + 3 : 4 * k + 4, :] = im[:, half:]
    small[3].wait()
    size = outs[0].shape[0]
    for i, out in enumerate(outs):
        out[...] = stage[i * size : (i + 1) * size]


def sort_halves(cap, sign_ref, *refs):
    *landed, near_ref, far_ref = refs
    for i, ref in enumerate(landed):
        near_ref[i * cap : (i + 1) * cap] = ref[:cap]
        far_ref[i * cap : (i + 1) * cap] = ref[cap:]


def cells_inside(len_ref, cells):
    row = len_ref[...].astype(F32)
    lines = row.shape[1]
    both = jnp.concatenate([row, row], axis=1)
    column = jnp.broadcast_to(both, (8, both.shape[1])).T[:lines, 0:1]
    cell = lax.axis_index("ax") * cells + lax.broadcasted_iota(jnp.int32, (lines, cells), 1)
    return cell.astype(F32) < column


def coefficients(v, iv, a_re, a_im, inside):
    s = jnp.where(inside, jnp.abs(v), 0.0)
    rd = 1.0 / (iv + 1.5 * s)
    c = s * rd
    g_re, g_im = s * a_re, s * a_im
    scale = jnp.where(inside, relaxation * rd, 0.0)
    half = v.shape[1] // 2
    lane = lax.broadcasted_iota(jnp.int32, (2 * v.shape[0], half), 1)
    low = jnp.concatenate([g_re[:, :half], g_im[:, :half]], axis=0)
    high = jnp.concatenate([g_re[:, half:], g_im[:, half:]], axis=0)
    sign = jnp.concatenate([v[:, :half], v[:, :half]], axis=0)
    edges = jnp.where(lane < 2, low, jnp.where(lane >= half - 2, high, sign)).T
    return c, scale, g_re, g_im, edges


def drives(c, g, q, inside):
    h = jnp.where(inside, q, 0.0) - 1.5 * g
    return h, g + c * h


def doubled(x):
    return jnp.concatenate([x, x], axis=0)


def orders(sign_row):
    width = sign_row.shape[1]
    pos = jnp.broadcast_to(sign_row, (SEGS, width)) > 0.0
    seg = lax.broadcasted_iota(jnp.int32, (SEGS, width), 0)
    return pos, jnp.where(pos, SEGS - 1 - seg, seg)


def before(value, reach, fill, pos, order):
    up = pltpu.roll(value, reach, 0)
    down = pltpu.roll(value, SEGS - reach, 0)
    return jnp.where(order >= reach, jnp.where(pos, down, up), fill)


def segment_scan(slots, c_t, b_t, c_s, b_s, poses):
    steps = c_s.shape[1]
    width = c_s.shape[3]
    zero = jnp.zeros((SEGS, width), F32)
    real = lax.broadcasted_iota(jnp.int32, (SEGS, width), 1) < width // 2
    first, second = jnp.where(real, 1.0, 0.0), jnp.where(real, 0.0, 1.0)
    state = [(zero, zero, first, second) for _ in slots]
    for t in range(steps):
        for i, k in enumerate(slots):
            pos = poses[i]
            y1, y2, n1, n2 = state[i]
            lo, hi = pl.ds(t, SEGS, stride=steps), pl.ds(steps - 1 - t, SEGS, stride=steps)
            cs, bs = c_t.at[k], b_t.at[k]
            c = jnp.where(pos, cs[hi, :], cs[lo, :])
            b = jnp.where(pos, bs[hi, :], bs[lo, :])
            c_s[k, t] = c
            b_s[k, t] = b
            c1, c2 = 2.0 * c, -0.5 * c
            state[i] = ((b + c2 * y2) + c1 * y1, y1, c2 * n2 + c1 * n1, n1)
    return state


def compose(state, pos, order):
    y1, y2, n1, n2 = state
    width = y1.shape[1]
    real = lax.broadcasted_iota(jnp.int32, (SEGS, width), 1) < width // 2
    o1, o2 = pltpu.roll(n1, width // 2, 1), pltpu.roll(n2, width // 2, 1)
    m11, m12 = jnp.where(real, n1, o1), jnp.where(real, o1, n1)
    m21, m22 = jnp.where(real, n2, o2), jnp.where(real, o2, n2)
    v1, v2 = y1, y2
    prev = functools.partial(before, pos=pos, order=order)
    for reach in (1, 2, 4):
        a11, a12 = prev(m11, reach, 1.0), prev(m12, reach, 0.0)
        a21, a22 = prev(m21, reach, 0.0), prev(m22, reach, 1.0)
        u1, u2 = prev(v1, reach, 0.0), prev(v2, reach, 0.0)
        m11, m12, m21, m22, v1, v2 = (
            m11 * a11 + m12 * a21,
            m11 * a12 + m12 * a22,
            m21 * a11 + m22 * a21,
            m21 * a12 + m22 * a22,
            m11 * u1 + m12 * u2 + v1,
            m21 * u1 + m22 * u2 + v2,
        )
    entry = (
        prev(v1, 1, 0.0),
        prev(v2, 1, 0.0),
        jnp.where(real, prev(m11, 1, 1.0), prev(m12, 1, 0.0)),
        jnp.where(real, prev(m21, 1, 0.0), prev(m22, 1, 1.0)),
    )
    return (m11, m12, m21, m22, v1, v2), entry


def put_maps(msg_ref, sign_ref, ent_ref, k, slot, state, edges):
    half = edges.shape[0]
    sign_row = edges[half // 2 : half // 2 + 1]
    pos, order = orders(sign_row)
    maps, entry = compose(state, pos, order)
    up = sign_row > 0.0
    for row, value in enumerate(maps):
        msg_ref[row, k : k + 1, :] = jnp.where(up, value[0:1], value[SEGS - 1 : SEGS])
    msg_ref[6, k : k + 1, :] = jnp.where(up, edges[0:1], edges[half - 1 : half])
    msg_ref[7, k : k + 1, :] = jnp.where(up, edges[1:2], edges[half - 2 : half - 1])
    sign_ref[k : k + 1, :] = sign_row
    for row, value in enumerate(entry):
        ent_ref[slot, row] = value


def main_maps(
    adj_ref, len_ref, speed_ref, inv_ref, src_hbm,
    msg_ref, sign_ref, ent_ref, c_s, b_s, h_ref, scale_ref, in_ref, src_ref,
    c_n, c_t, b_t, sems,
):
    vars_, lines, cells = speed_ref.shape
    copies = [
        pltpu.make_async_copy(src_hbm.at[:, k], src_ref.at[:, k], sems.at[k]) for k in range(vars_)
    ]
    for copy in copies:
        copy.start()
    inside = cells_inside(len_ref, cells)
    in_ref[...] = jnp.where(inside, 1.0, 0.0)
    all_edges, poses = [], []
    for k in range(vars_):
        c, scale, g_re, g_im, edges = coefficients(
            speed_ref[k], inv_ref[k], adj_ref[0, k], adj_ref[1, k], inside)
        c_t[k] = doubled(c).T
        h_ref[0, k], h_ref[1, k] = g_re, g_im
        c_n[k] = c
        scale_ref[k] = scale
        all_edges.append(edges)
        mid = edges.shape[0] // 2
        poses.append(orders(edges[mid : mid + 1])[0])
    for k in range(vars_):
        copies[k].wait()
        c = c_n[k]
        h_re, b_re = drives(c, h_ref[0, k], src_ref[0, k] + frequency * adj_ref[1, k], inside)
        h_im, b_im = drives(c, h_ref[1, k], src_ref[1, k] - frequency * adj_ref[0, k], inside)
        h_ref[0, k], h_ref[1, k] = h_re, h_im
        b_t[k] = jnp.concatenate([b_re, b_im], axis=0).T
    states = segment_scan(range(vars_), c_t, b_t, c_s, b_s, poses)
    for k in range(vars_):
        put_maps(msg_ref, sign_ref, ent_ref, k, k, states[k], all_edges[k])


def face_maps(
    counts, lift_ref, in_ref, adj_ref, src_ref, speed_ref, inv_ref, old_msg, old_sign, *rest
):
    recv = rest[: len(counts)]
    msg_ref, sign_ref, ent_ref, c_s, b_s, h_ref, c_t, b_t = rest[len(counts) :]
    vars_, lines, cells = speed_ref.shape
    sub = lax.broadcasted_iota(jnp.int32, (FACE_DEV, 128), 0).astype(F32)
    acc = [jnp.zeros((FACE_DEV, 128), F32) for _ in range(4 * vars_)]
    for ref, number in zip(recv, counts):
        for e in range(number):
            hit = jnp.broadcast_to(ref[e, 20:21, :], (FACE_DEV, 128)) == sub
            for j in range(4 * vars_):
                row = jnp.broadcast_to(ref[e, j : j + 1, :], (FACE_DEV, 128))
                acc[j] = acc[j] + jnp.where(hit, row, 0.0)
    picks = [min(k, vars_ - 1) for k in range(lines // FACE_DEV)]

    def gather(ref):
        return jnp.concatenate([ref[k, :FACE_DEV] for k in picks], axis=0)

    def faces(j):
        return jnp.concatenate(
            [jnp.concatenate([acc[4 * k + j], acc[4 * k + j + 1]], axis=1) for k in picks], axis=0)

    a_re, a_im = gather(adj_ref.at[0]), gather(adj_ref.at[1])
    q_re = gather(src_ref.at[0]) + frequency * a_im - faces(0)
    q_im = gather(src_ref.at[1]) - frequency * a_re - faces(2)
    inside = jnp.concatenate([in_ref[:FACE_DEV]] * len(picks), axis=0) > 0.0
    c, _, g_re, g_im, edges = coefficients(
        gather(speed_ref), gather(inv_ref), a_re, a_im, inside)
    h_re, b_re = drives(c, g_re, q_re, inside)
    h_im, b_im = drives(c, g_im, q_im, inside)
    h_ref[:lines], h_ref[lines:] = h_re, h_im
    c_t[0] = doubled(c).T
    b_t[0] = jnp.concatenate([b_re, b_im], axis=0).T
    mid = edges.shape[0] // 2
    state = segment_scan([0], c_t, b_t, c_s, b_s, [orders(edges[mid : mid + 1])[0]])[0]
    msg_ref[...] = old_msg[...]
    sign_ref[...] = old_sign[...]
    put_maps(msg_ref, sign_ref, ent_ref, vars_, 0, state, edges)


def unfold(k, t, steps, value, kept, turned, pos):
    if t < steps // 2:
        kept[k, t] = value
    else:
        other = kept[k, steps - 1 - t]
        turned.at[k][pl.ds(steps - 1 - t, SEGS, stride=steps), :] = jnp.where(pos, value, other)
        turned.at[k][pl.ds(t, SEGS, stride=steps), :] = jnp.where(pos, other, value)


def lifts(sign_ref, ent_ref, c_s, scale_ref, after_ref, lift_ref, x_s, x_t):
    vars_, lines, cells = scale_ref.shape
    steps, width = c_s.shape[1], c_s.shape[3]
    poses = [jnp.broadcast_to(sign_ref[k : k + 1, :], (SEGS, width)) > 0.0 for k in range(vars_)]
    state = [(ent_ref[k, 2], ent_ref[k, 3]) for k in range(vars_)]
    for t in range(steps):
        for k in range(vars_):
            n1, n2 = state[k]
            x = 2.0 * n1 - 0.5 * n2
            state[k] = (c_s[k, t] * x, n1)
            unfold(k, t, steps, x, x_s, x_t, poses[k])
    for k in range(vars_):
        x = x_t[k].T
        for part in range(2):
            lift_ref[part, k] = x[part * lines : (part + 1) * lines] * scale_ref[k]


def substitute(
    in_ref, adj_ref, speed_ref, sign_ref, ent_ref, c_s, b_s, h_ref, scale_ref,
    ent_f, c_f, b_f, h_f,
    part_ref, res_ref,
    u_s, u_t,
):
    vars_, lines, cells = speed_ref.shape
    steps, width = c_s.shape[1], c_s.shape[3]
    groups = vars_ + 1
    inside = in_ref[...] > 0.0
    lane = lax.broadcasted_iota(jnp.int32, (lines, cells), 1)
    poses = [jnp.broadcast_to(sign_ref[k : k + 1, :], (SEGS, width)) > 0.0 for k in range(groups)]
    state = []
    for k in range(groups):
        ent = ent_ref.at[k] if k < vars_ else ent_f.at[0]
        state.append((ent[0], ent[1]))
    for t in range(steps):
        for k in range(groups):
            main = k < vars_
            c = c_s[k, t] if main else c_f[0, t]
            b = b_s[k, t] if main else b_f[0, t]
            y1, y2 = state[k]
            u = 2.0 * y1 - 0.5 * y2
            state[k] = (c * u + b, y1)
            unfold(k, t, steps, u, u_s, u_t, poses[k])
    face_u = u_t[vars_].T
    for k in range(vars_):
        scale = scale_ref[k]
        v = speed_ref[k]
        s = jnp.where(inside, jnp.abs(v), 0.0)
        up = v > 0.0
        apart = lane != jnp.where(up, cells - 1, 0)

        def shifted(value):
            return jnp.where(
                apart, jnp.where(up, pltpu.roll(value, cells - 1, 1), pltpu.roll(value, 1, 1)), 0.0)

        u = u_t[k].T
        for part in range(2):
            at = part * lines + FACE_DEV * k
            h = jnp.concatenate([h_f[at : at + FACE_DEV], h_ref[part, k, FACE_DEV:]], axis=0)
            us = jnp.concatenate(
                [face_u[at : at + FACE_DEV], u[part * lines + FACE_DEV : (part + 1) * lines]], axis=0)
            a = adj_ref[part, k]
            part_ref[part, k] = jnp.where(inside, a, 0.0) + (h + us) * scale
            g = s * a
            res_ref[part, k] = h + jnp.where(inside, shifted(2.0 * g - 0.5 * shifted(g)), 0.0)


def finish(count, pairwise, in_ref, sign_ref, part_ref, lift_ref, res_ref, *rest):
    got = rest[: count - 1]
    new_hbm, out_hbm, new_ref, out_ref, sems = rest[count - 1 :]
    _, vars_, lines, cells = part_ref.shape
    width = 2 * lines
    place = lax.axis_index("ax")
    odd = lax.rem(place, 2) == 1
    pos = sign_ref[...] > 0.0
    zero = jnp.zeros((TABLE, width), F32)
    z1, z2, g1, g2 = zero, zero, zero, zero
    for i in range(count - 1, 0, -1):
        near = jnp.where(place >= i, 1.0, 0.0)
        far = jnp.where(place + i <= count - 1, 1.0, 0.0)
        has = jnp.where(pos, far, near) > 0.0

        def field(r):
            if not pairwise:
                return jnp.where(pos, got[count - i - 1][r], got[i - 1][r])
            if i > 1:
                return got[i - 1][r]
            one, three = got[0][r], got[2][r]
            return jnp.where(pos, jnp.where(odd, three, one), jnp.where(odd, one, three))

        m = [field(r) for r in range(8 if i == 1 else 6)]
        n1 = m[0] * z1 + m[1] * z2 + m[4]
        n2 = m[2] * z1 + m[3] * z2 + m[5]
        z1, z2 = jnp.where(has, n1, z1), jnp.where(has, n2, z2)
        if i == 1:
            g1, g2 = jnp.where(has, m[6], 0.0), jnp.where(has, m[7], 0.0)
    r0, r1 = 2.0 * g1 - 0.5 * g2, -0.5 * g1
    table = jnp.concatenate(
        [z1, z2, jnp.where(pos, 0.0, r0), jnp.where(pos, 0.0, r1),
         jnp.where(pos, r0, 0.0), jnp.where(pos, r1, 0.0)]
        + [zero] * (width // TABLE - 6), axis=0).T
    half = cells // 2
    lane = lax.broadcasted_iota(jnp.int32, (lines, half), 1)
    copies = []
    for k in range(vars_):
        for part in range(2):
            at = part * lines + FACE_DEV * k
            rows = slice(part * lines, (part + 1) * lines)
            halo = lambda r: table[rows, TABLE * r + k : TABLE * r + k + 1]

            def entering(r):
                face = TABLE * r + vars_
                return jnp.concatenate(
                    [table[at : at + FACE_DEV, face : face + 1], halo(r)[FACE_DEV:]], axis=0)

            low = jnp.where(lane == 0, halo(2), jnp.where(lane == 1, halo(3), 0.0))
            high = jnp.where(lane == half - 1, halo(4), jnp.where(lane == half - 2, halo(5), 0.0))
            out_ref[part, k, :, :half] = res_ref[part, k, :, :half] + low * in_ref[:, :half]
            out_ref[part, k, :, half:] = res_ref[part, k, :, half:] + high * in_ref[:, half:]
            new_ref[part, k] = part_ref[part, k] + (
                lift_ref[0, k] * entering(0) + lift_ref[1, k] * entering(1))
            for j, (src, dst) in enumerate(((out_ref, out_hbm), (new_ref, new_hbm))):
                copies.append(pltpu.make_async_copy(
                    src.at[part, k], dst.at[part, k], sems.at[4 * k + 2 * part + j]))
                copies[-1].start()
    for copy in copies:
        copy.wait()


def shards(adjoint, source, speed, inverse_step, coupling, face_line, face_owner, line_length):
    lines, rows, cells = adjoint.shape
    vars_ = speed.shape[1]
    faces = face_line.shape[0]
    blocks = lax.axis_size("xs")
    count = lax.axis_size("ax")
    cap = max(1, faces // blocks)
    width = 2 * lines
    steps = cells // SEGS
    adj = jnp.transpose(adjoint, (1, 0, 2)).reshape(2, vars_, lines, cells)
    src = jnp.transpose(source, (1, 0, 2)).reshape(2, vars_, lines, cells)
    spd = jnp.transpose(speed, (1, 0, 2))
    inv = jnp.transpose(inverse_step, (1, 0, 2))
    cpl = jnp.transpose(coupling, (1, 0, 2))
    vmem = pl.BlockSpec(memory_space=pltpu.VMEM)
    hbm = pl.BlockSpec(memory_space=pltpu.HBM)
    stay = lambda x: pltpu.with_memory_space_constraint(x, pltpu.HBM)
    shape = lambda *dims: jax.ShapeDtypeStruct(dims, F32)
    scratch = lambda *dims: pltpu.VMEM(dims, F32)
    dma = lambda number: pltpu.SemaphoreType.DMA((number,))
    limit = lambda mib: pltpu.CompilerParams(vmem_limit_bytes=mib << 20)
    cost = lambda flops, moved: pl.CostEstimate(
        flops=flops, bytes_accessed=moved, transcendentals=0)
    table_shape = shape(8, TABLE, width)
    sign_shape = shape(TABLE, width)
    order_shape = shape(vars_, steps, SEGS, width)
    field_shape = shape(2, vars_, lines, cells)
    var_shape = shape(vars_, lines, cells)
    face_order = shape(1, steps, SEGS, width)
    paired = blocks == 8
    entries = blocks * cap
    pieces = blocks // 2 if paired else 1
    adj, lengths, *packed = pl.pallas_call(
        functools.partial(pack_faces, blocks, cap, paired),
        out_shape=[field_shape, jax.ShapeDtypeStruct((1, lines), jnp.int32)]
        + [shape(entries // pieces, PACK_ROWS, cells // 2)] * pieces,
        in_specs=[hbm] * 5,
        out_specs=[vmem] * (2 + pieces),
        scratch_shapes=[scratch(entries, PACK_ROWS, cells // 2), pltpu.SMEM((faces,), jnp.int32),
                        pltpu.SMEM((faces,), jnp.int32), scratch(vars_, faces, cells), dma(4 + vars_)],
        compiler_params=limit(6),
        cost_estimate=cost(2 * 10**6, 4 * 10**6),
        name="pack_faces",
    )(stay(face_line), stay(face_owner), stay(adj), stay(cpl), stay(line_length.reshape(1, lines)))
    hop = lambda x, m: lax.ppermute(x, "xs", [(i, i ^ m) for i in range(blocks)])
    if paired:
        landed = [packed[0]] + [hop(packed[m], 2 * m) for m in range(1, pieces)]
    msg, sign, ent, c_s, b_s, h, scale, mask, src = pl.pallas_call(
        main_maps,
        out_shape=[table_shape, sign_shape, shape(vars_, 4, SEGS, width), order_shape, order_shape,
                   field_shape, var_shape, shape(lines, cells), field_shape],
        in_specs=[vmem] * 4 + [hbm],
        out_specs=[vmem] * 9,
        scratch_shapes=[scratch(vars_, lines, cells)] + [scratch(vars_, cells, width)] * 2
        + [dma(vars_)],
        compiler_params=limit(14),
        cost_estimate=cost(2 * 10**6, 4 * 10**6),
        name="main_maps",
    )(adj, lengths, spd, inv, stay(src))
    if paired:
        halves = shape(pieces * cap, PACK_ROWS, cells // 2)
        near_half, far_half = pl.pallas_call(
            functools.partial(sort_halves, cap),
            out_shape=[halves] * 2,
            in_specs=[vmem] * (1 + pieces),
            out_specs=[vmem] * 2,
            compiler_params=limit(4),
            name="sort_halves",
        )(sign, *landed)
        recv, counts, after = [near_half, hop(far_half, 1)], [pieces * cap] * 2, near_half
    else:
        recv, counts, after = [lax.all_to_all(packed[0], "xs", 0, 0, tiled=True)], [entries], packed[0]
    kept = lambda number: scratch(number, steps // 2, SEGS, width)
    lift = pl.pallas_call(
        lifts,
        out_shape=field_shape,
        in_specs=[vmem] * 5,
        out_specs=vmem,
        scratch_shapes=[kept(vars_), scratch(vars_, cells, width)],
        compiler_params=limit(8),
        cost_estimate=cost(10**6, 2 * 10**6),
        name="lifts",
    )(sign, ent, c_s, scale, after)
    msg, sign, ent_f, c_f, b_f, h_f = pl.pallas_call(
        functools.partial(face_maps, counts),
        out_shape=[table_shape, sign_shape, shape(1, 4, SEGS, width), face_order, face_order,
                   shape(width, cells)],
        in_specs=[vmem] * (8 + len(recv)),
        out_specs=[vmem] * 6,
        scratch_shapes=[scratch(1, cells, width)] * 2,
        compiler_params=limit(10),
        name="face_maps",
    )(lift, mask, adj, src, spd, inv, msg, sign, *recv)
    pairwise = count == 4
    meet = (lambda i, k: i ^ k) if pairwise else (lambda i, k: (i + k) % count)
    got = [
        lax.ppermute(msg, "ax", [(i, meet(i, k)) for i in range(count)]) for k in range(1, count)
    ]
    part, res = pl.pallas_call(
        substitute,
        out_shape=[field_shape] * 2,
        in_specs=[vmem] * 13,
        out_specs=[vmem] * 2,
        scratch_shapes=[kept(vars_ + 1), scratch(vars_ + 1, cells, width)],
        compiler_params=limit(14),
        cost_estimate=cost(2 * 10**6, 5 * 10**6),
        name="substitute",
    )(mask, adj, spd, sign, ent, c_s, b_s, h, scale, ent_f, c_f, b_f, h_f)
    new, out = pl.pallas_call(
        functools.partial(finish, count, pairwise),
        out_shape=[field_shape] * 2,
        in_specs=[vmem] * (5 + len(got)),
        out_specs=[hbm] * 2,
        scratch_shapes=[scratch(2, vars_, lines, cells)] * 2 + [dma(4 * vars_)],
        compiler_params=limit(8),
        name="finish",
    )(mask, sign, part, lift, res, *got)
    back = lambda x: jnp.transpose(x.reshape(rows, lines, cells), (1, 0, 2))
    return (back(new), back(out))


def solution(mesh):
    line = P("xs", None, "ax")
    in_specs = (line,) * 5 + (P("xs"),) * 3
    return jax.shard_map(
        shards, mesh=mesh, in_specs=in_specs, out_specs=(line, line), check_vma=False
    )
```

time: 27.7 us -> 24.8 us (0.90)
  waiting for transfers between devices: 7.54 us -> 4.56 us
    ppermute x3, waiting for transfers between devices: 4.7 us -> 1.94 us  [shards(): lax.ppermute(msg, 'ax', [(i, meet(i, k)) for i in range(count)])]
    pallas_call x2 -> x3, Pallas kernels: 4.75 us -> 5.34 us  [the longest x1 2.62 us: shards(): pl.pallas_call(functools.partial(finish, count, pairwise), out_shape=[fie...]
    pallas_call x1, Pallas kernels: 3.39 us -> 2.96 us  [shards(): pl.pallas_call(main_maps, out_shape=[table_shape, sign_shape, shape(vars_...]
  transfers between devices with their start and end apart: 7 -> 7, of which waited for: 4 -> 3; matrix products, arithmetic and copies ran while one was open for 0% -> 0% of each run, Pallas kernels for 24% -> 23%
where the time goes in v1:
time: 24.8 us; the launch traced here: 24.6 us
  Pallas kernels  10.2 us (41%)
  starting transfers between devices  9.07 us (37%)
  waiting for transfers between devices  4.56 us (18%)
  between operations  0.72 us (3%)
    ppermute x4, starting transfers between devices, shards(): lax.ppermute(x, 'xs', [(i, i ^ m) for i in range(blocks)])  4.61 us
    ppermute x3, starting transfers between devices, shards(): lax.ppermute(msg, 'ax', [(i, meet(i, k)) for i in range(count)])  4.45 us
    pallas_call x1, Pallas kernels, shards(): pl.pallas_call(main_maps, out_shape=[table_shape, sign_shape, shape(vars_...  2.96 us
    ppermute x4, waiting for transfers between devices, shards(): lax.ppermute(x, 'xs', [(i, i ^ m) for i in range(blocks)])  2.62 us
    pallas_call x1, Pallas kernels, shards(): pl.pallas_call(functools.partial(finish, count, pairwise), out_shape=[fie...  2.62 us
    pallas_call x1, Pallas kernels, shards(): pl.pallas_call(substitute, out_shape=[field_shape] * 2, in_specs=[vmem] *...  2.07 us
    ppermute x3, waiting for transfers between devices, shards(): lax.ppermute(msg, 'ax', [(i, meet(i, k)) for i in range(count)])  1.94 us
    pallas_call x1, Pallas kernels, shards(): pl.pallas_call(functools.partial(pack_faces, blocks, cap, paired), out_sh...  1.4 us
  transfers between devices with their start and end apart: 7, of which 3 were waited for; matrix products, arithmetic and copies ran while one was open for 0% of the time, Pallas kernels for 23%

profile of v1, /device:TPU:0, one launch (start us, length us, event | category | flops | bytes accessed | tf_op | source)
XLA Modules:
  0.0 24.6 jit_solution(6951757680136581714)
XLA Ops:
  0.6 0.0 copy-start
  0.6 0.0 copy-start.1
  0.7 1.4 %pack_faces.1 = (f32[2,5,64,256]{3,2,1,0:T(8,128)S(1)}, s32[1,64]{1,0:T(1,128)S(1)}, f32[4,24,128]{2,1,0:T(8,128)S(1)}, f32[4,24,128]{2,1,0:T(8,128)S(1)}, f32[4...) custom-call(s32[16]{0:T(128)} %line_hbm.1, s32[16]{0:T(128)} %owner_hbm.1, f32[2,5,64,256]{3,2,1,0:T(8,128)} %bitcast.21, ...), custom_call_target="tpu_custom_call" | custom-call | flops 2000000 | bytes 4000000 | tf_op jit(solution)/shard_map/pack_faces/pallas_call | solution.py:441
  2.1 3.0 %collective-permute-start = (f32[4,24,128]{2,1,0:T(8,128)S(1)}, f32[4,24,128]{2,1,0:T(8,128)S(1)}, u32[]{:S(2)}, u32[]{:S(2)}) collective-permute-start(f32[4,24,128]{2,1,0:T(8,128)S(1)} %get-tuple-element.37), channel_id=1, source_target_pairs={{0,2},{1,3},{2,0},{3,1},{4,6},{5,7},{6,4},{7,5},{8,10},{9,11},{10,... | collective-permute-start | bytes 147464 | tf_op jit(solution)/shard_map/ppermute | solution.py:453
  5.1 1.5 %collective-permute-start.1 = (f32[4,24,128]{2,1,0:T(8,128)S(1)}, f32[4,24,128]{2,1,0:T(8,128)S(1)}, u32[]{:S(2)}, u32[]{:S(2)}) collective-permute-start(f32[4,24,128]{2,1,0:T(8,128)S(1)} %get-tuple-element.38), channel_id=1, source_target_pairs={{0,4},{1,5},{2,6},{3,7},{4,0},{5,1},{6,2},{7,3},{8,12},{9,13},{10,... | collective-permute-start | bytes 147464 | tf_op jit(solution)/shard_map/ppermute | solution.py:453
  6.6 0.0 collective-permute-start.2
  6.6 0.0 copy-done
  6.6 0.0 copy-done.1
  6.6 3.0 %main_maps.1 = (f32[8,8,128]{2,1,0:T(8,128)S(1)}, f32[8,128]{1,0:T(8,128)S(1)}, f32[5,4,8,128]{3,2,1,0:T(8,128)S(1)}, f32[5,32,8,128]{3,2,1,0:T(8,128)S(1)}, f32...) custom-call(f32[2,5,64,256]{3,2,1,0:T(8,128)S(1)} %get-tuple-element, ...), custom_call_target="tpu_custom_call" | custom-call | flops 2000000 | bytes 4000000 | tf_op jit(solution)/shard_map/main_maps/pallas_call | solution.py:456
  9.6 0.0 collective-permute-done.refs_1_
  9.6 0.0 collective-permute-done.1.refs_2_
  9.6 2.0 %collective-permute-done.2.refs_3_ = f32[4,24,128]{2,1,0:T(8,128)S(1)} collective-permute-done((f32[4,24,128]{2,1,0:T(8,128)S(1)}, f32[4,24,128]{2,1,0:T(8,128)S(1)}, u32[]{:S(2)}, u32[]{:S(2)}) %collective-permute-start.2) | collective-permute-done | bytes 49184 | tf_op jit(solution)/shard_map/ppermute | solution.py:453
  11.6 0.1 collective-permute-start.3
  11.7 0.6 %lifts.1.lift_ref = f32[2,5,64,256]{3,2,1,0:T(8,128)S(1)} custom-call(f32[8,128]{1,0:T(8,128)S(1)} %get-tuple-element.32.sign_ref.old_sign, f32[5,4,8,128]{3,2,1,0:T(8,128)S(1)} %get-tuple-element.33.ent_ref, f32[5,32,8,128]{3,2,1,0:T(8,128)S(1)} %get-tuple-element.34.c_s, f32[5,64,256]{2,1,0:T(8,128)S(1)} %get-tuple-element.35.scale_ref, ...), custom_call_target="tpu_custom_call" | custom-call | flops 1000000 | bytes 2000000 | tf_op jit(solution)/shard_map/lifts/pallas_call | solution.py:482
  12.3 0.6 %collective-permute-done.3.rest_1_ = f32[8,24,128]{2,1,0:T(8,128)S(1)} collective-permute-done((f32[8,24,128]{2,1,0:T(8,128)S(1)}, f32[8,24,128]{2,1,0:T(8,128)S(1)}, u32[]{:S(2)}, u32[]{:S(2)}) %collective-permute-start.3) | collective-permute-done | bytes 98336 | tf_op jit(solution)/shard_map/ppermute | solution.py:453
  13.0 0.5 %face_maps.1 = (f32[8,8,128]{2,1,0:T(8,128)S(1)}, f32[8,128]{1,0:T(8,128)S(1)}, f32[1,4,8,128]{3,2,1,0:T(8,128)S(1)}, f32[1,32,8,128]{3,2,1,0:T(8,128)S(1)}, f32...) custom-call(f32[2,5,64,256]{3,2,1,0:T(8,128)S(1)} %lifts.1.lift_ref, f32[64,256]{1,0:T(8,128)S(1)} %get-tuple-element.31.in_ref, ...), custom_call_target="tpu_custom_call" | custom-call | tf_op jit(solution)/shard_map/face_maps/pallas_call | solution.py:492
  13.5 3.7 %collective-permute-start.6 = (f32[8,8,128]{2,1,0:T(8,128)S(1)}, f32[8,8,128]{2,1,0:T(8,128)S(1)}, u32[]{:S(2)}, u32[]{:S(2)}) collective-permute-start(f32[8,8,128]{2,1,0:T(8,128)S(1)} %get-tuple-element.53), channel_id=1, source_target_pairs={{0,24},{8,16},{16,8},{24,0},{1,25},{9,17},{17,9},{25,1},{2,26},{10... | collective-permute-start | bytes 98312 | tf_op jit(solution)/shard_map/ppermute | solution.py:505
  17.2 0.0 collective-permute-start.5
  17.2 0.8 %collective-permute-start.4 = (f32[8,8,128]{2,1,0:T(8,128)S(1)}, f32[8,8,128]{2,1,0:T(8,128)S(1)}, u32[]{:S(2)}, u32[]{:S(2)}) collective-permute-start(f32[8,8,128]{2,1,0:T(8,128)S(1)} %get-tuple-element.53), channel_id=1, source_target_pairs={{0,8},{8,0},{16,24},{24,16},{1,9},{9,1},{17,25},{25,17},{2,10},{10... | collective-permute-start | bytes 98312 | tf_op jit(solution)/shard_map/ppermute | solution.py:505
  17.9 2.1 %substitute.1 = (f32[2,5,64,256]{3,2,1,0:T(8,128)S(1)}, f32[2,5,64,256]{3,2,1,0:T(8,128)S(1)}) custom-call(f32[64,256]{1,0:T(8,128)S(1)} %get-tuple-element.31.in_ref, f32[2,5,64,256]{3,2,1,0:T(8,128)S(1)} %get-tuple-element.29.adj_ref, f32[5,64,256]{2,1,0:T(8,128)S(1)} %bitcast.18, f32[8,128]{1,0:T(8,128)S(1)} %get-tuple-element.44.sign_ref, ...), custom_call_target="tpu_custom_call" | custom-call | flops 2000000 | bytes 5000000 | tf_op jit(solution)/shard_map/substitute/pallas_call | solution.py:507
  20.0 0.0 collective-permute-done.6.rest_2_
  20.0 1.9 %collective-permute-done.5.rest_1_ = f32[8,8,128]{2,1,0:T(8,128)S(1)} collective-permute-done((f32[8,8,128]{2,1,0:T(8,128)S(1)}, f32[8,8,128]{2,1,0:T(8,128)S(1)}, u32[]{:S(2)}, u32[]{:S(2)}) %collective-permute-start.5) | collective-permute-done | bytes 32800 | tf_op jit(solution)/shard_map/ppermute | solution.py:505
  22.0 0.0 collective-permute-done.4.rest_0_
  22.0 2.6 %finish.1 = (f32[2,5,64,256]{3,2,1,0:T(8,128)}, f32[2,5,64,256]{3,2,1,0:T(8,128)}) custom-call(f32[64,256]{1,0:T(8,128)S(1)} %get-tuple-element.31.in_ref, f32[8,128]{1,0:T(8,128)S(1)} %get-tuple-element.44.sign_ref, f32[2,5,64,256]{3,2,1,0:T(8,128)S(1)} %get-tuple-element.51.part_ref, f32[2,5,64,256]{3,2,1,0:T(8,128)S(1)} %lifts.1.lift_ref, ...), custom_call_target="tpu_custom_call" | custom-call | tf_op jit(solution)/shard_map/finish/pallas_call | solution.py:517
  (1 shorter events, 0.0 us)
Async XLA Ops:
  0.6 6.0 %copy-start = (f32[64,5,256]{2,0,1:T(8,128)S(1)}, f32[64,5,256]{2,0,1:T(8,128)}, u32[]{:S(2)}) copy-start(f32[64,5,256]{2,0,1:T(8,128)} %param.10) | copy-start | bytes 983044
  0.6 6.0 %copy-start.1 = (f32[64,5,256]{2,0,1:T(8,128)S(1)}, f32[64,5,256]{2,0,1:T(8,128)}, u32[]{:S(2)}) copy-start(f32[64,5,256]{2,0,1:T(8,128)} %param.11) | copy-start | bytes 983044
  2.1 7.5 %collective-permute-start = (f32[4,24,128]{2,1,0:T(8,128)S(1)}, f32[4,24,128]{2,1,0:T(8,128)S(1)}, u32[]{:S(2)}, u32[]{:S(2)}) collective-permute-start(f32[4,24,128]{2,1,0:T(8,128)S(1)} %get-tuple-element.37), channel_id=1, source_target_pairs={{0,2},{1,3},{2,0},{3,1},{4,6},{5,7},{6,4},{7,5},{8,10},{9,11},{10,... | collective-permute-start | bytes 147464 | tf_op jit(solution)/shard_map/ppermute | solution.py:453
  5.1 4.5 %collective-permute-start.1 = (f32[4,24,128]{2,1,0:T(8,128)S(1)}, f32[4,24,128]{2,1,0:T(8,128)S(1)}, u32[]{:S(2)}, u32[]{:S(2)}) collective-permute-start(f32[4,24,128]{2,1,0:T(8,128)S(1)} %get-tuple-element.38), channel_id=1, source_target_pairs={{0,4},{1,5},{2,6},{3,7},{4,0},{5,1},{6,2},{7,3},{8,12},{9,13},{10,... | collective-permute-start | bytes 147464 | tf_op jit(solution)/shard_map/ppermute | solution.py:453
  6.6 5.0 %collective-permute-start.2 = (f32[4,24,128]{2,1,0:T(8,128)S(1)}, f32[4,24,128]{2,1,0:T(8,128)S(1)}, u32[]{:S(2)}, u32[]{:S(2)}) collective-permute-start(f32[4,24,128]{2,1,0:T(8,128)S(1)} %get-tuple-element.39), channel_id=1, source_target_pairs={{0,6},{1,7},{2,4},{3,5},{4,2},{5,3},{6,0},{7,1},{8,14},{9,15},{10,... | collective-permute-start | bytes 147464 | tf_op jit(solution)/shard_map/ppermute | solution.py:453
  11.6 1.4 %collective-permute-start.3 = (f32[8,24,128]{2,1,0:T(8,128)S(1)}, f32[8,24,128]{2,1,0:T(8,128)S(1)}, u32[]{:S(2)}, u32[]{:S(2)}) collective-permute-start(f32[8,24,128]{2,1,0:T(8,128)S(1)} %get-tuple-element.43), channel_id=1, source_target_pairs={{0,1},{1,0},{2,3},{3,2},{4,5},{5,4},{6,7},{7,6},{8,9},{9,8},{10,11... | collective-permute-start | bytes 294920 | tf_op jit(solution)/shard_map/ppermute | solution.py:453
  13.5 6.5 %collective-permute-start.6 = (f32[8,8,128]{2,1,0:T(8,128)S(1)}, f32[8,8,128]{2,1,0:T(8,128)S(1)}, u32[]{:S(2)}, u32[]{:S(2)}) collective-permute-start(f32[8,8,128]{2,1,0:T(8,128)S(1)} %get-tuple-element.53), channel_id=1, source_target_pairs={{0,24},{8,16},{16,8},{24,0},{1,25},{9,17},{17,9},{25,1},{2,26},{10... | collective-permute-start | bytes 98312 | tf_op jit(solution)/shard_map/ppermute | solution.py:505
  17.2 4.8 %collective-permute-start.5 = (f32[8,8,128]{2,1,0:T(8,128)S(1)}, f32[8,8,128]{2,1,0:T(8,128)S(1)}, u32[]{:S(2)}, u32[]{:S(2)}) collective-permute-start(f32[8,8,128]{2,1,0:T(8,128)S(1)} %get-tuple-element.53), channel_id=1, source_target_pairs={{0,16},{8,24},{16,0},{24,8},{1,17},{9,25},{17,1},{25,9},{2,18},{10... | collective-permute-start | bytes 98312 | tf_op jit(solution)/shard_map/ppermute | solution.py:505
  17.2 4.8 %collective-permute-start.4 = (f32[8,8,128]{2,1,0:T(8,128)S(1)}, f32[8,8,128]{2,1,0:T(8,128)S(1)}, u32[]{:S(2)}, u32[]{:S(2)}) collective-permute-start(f32[8,8,128]{2,1,0:T(8,128)S(1)} %get-tuple-element.53), channel_id=1, source_target_pairs={{0,8},{8,0},{16,24},{24,16},{1,9},{9,1},{17,25},{25,17},{2,10},{10... | collective-permute-start | bytes 98312 | tf_op jit(solution)/shard_map/ppermute | solution.py:505

commit v2 on v1

--- a/solution.py
+++ b/solution.py
@@ -17,10 +17,9 @@
 F32 = jnp.float32
 
 
-def pack_faces(blocks, cap, paired, line_hbm, owner_hbm, adj_hbm, coup_hbm, len_hbm, *rest):
-    adj_ref, len_ref = rest[:2]
-    outs = rest[2:-5]
-    stage, line_ref, owner_ref, coup_ref, sems = rest[-5:]
+def pack_faces(blocks, cap, paired, line_hbm, owner_hbm, adj_hbm, coup_hbm, len_hbm, inv_hbm, *rest):
+    adj_ref, len_ref, inv_ref, stage = rest[:4]
+    line_ref, owner_ref, coup_ref, sems = rest[4:]
     vars_, faces, cells = coup_ref.shape
     half = cells // 2
     slots = FACE_DEV * blocks
@@ -34,7 +33,8 @@
         pltpu.make_async_copy(adj_hbm.at[:, k], adj_ref.at[:, k], sems.at[4 + k])
         for k in range(vars_)
     ]
-    for copy in small + large:
+    step = pltpu.make_async_copy(inv_hbm, inv_ref, sems.at[4 + vars_])
+    for copy in small + large + [step]:
         copy.start()
     for copy in small[:2]:
         copy.wait()
@@ -67,12 +67,16 @@
             stage[entry, 4 * k + 2 : 4 * k + 3, :] = im[:, :half]
             stage[entry, 4 * k + 3 : 4 * k + 4, :] = im[:, half:]
     small[3].wait()
+    step.wait()
+
+
+def deal(packed_ref, *outs):
     size = outs[0].shape[0]
     for i, out in enumerate(outs):
-        out[...] = stage[i * size : (i + 1) * size]
-
-
-def sort_halves(cap, sign_ref, *refs):
+        out[...] = packed_ref[i * size : (i + 1) * size]
+
+
+def sort_halves(cap, after_ref, *refs):
     *landed, near_ref, far_ref = refs
     for i, ref in enumerate(landed):
         near_ref[i * cap : (i + 1) * cap] = ref[:cap]
@@ -193,36 +197,26 @@
 
 
 def main_maps(
-    adj_ref, len_ref, speed_ref, inv_ref, src_hbm,
-    msg_ref, sign_ref, ent_ref, c_s, b_s, h_ref, scale_ref, in_ref, src_ref,
-    c_n, c_t, b_t, sems,
+    adj_ref, len_ref, src_ref, speed_ref, inv_ref,
+    msg_ref, sign_ref, ent_ref, c_s, b_s, h_ref, scale_ref, in_ref,
+    c_t, b_t,
 ):
     vars_, lines, cells = speed_ref.shape
-    copies = [
-        pltpu.make_async_copy(src_hbm.at[:, k], src_ref.at[:, k], sems.at[k]) for k in range(vars_)
-    ]
-    for copy in copies:
-        copy.start()
     inside = cells_inside(len_ref, cells)
     in_ref[...] = jnp.where(inside, 1.0, 0.0)
     all_edges, poses = [], []
     for k in range(vars_):
-        c, scale, g_re, g_im, edges = coefficients(
-            speed_ref[k], inv_ref[k], adj_ref[0, k], adj_ref[1, k], inside)
+        a_re, a_im = adj_ref[0, k], adj_ref[1, k]
+        c, scale, g_re, g_im, edges = coefficients(speed_ref[k], inv_ref[k], a_re, a_im, inside)
+        h_re, b_re = drives(c, g_re, src_ref[0, k] + frequency * a_im, inside)
+        h_im, b_im = drives(c, g_im, src_ref[1, k] - frequency * a_re, inside)
+        h_ref[0, k], h_ref[1, k] = h_re, h_im
+        scale_ref[k] = scale
         c_t[k] = doubled(c).T
-        h_ref[0, k], h_ref[1, k] = g_re, g_im
-        c_n[k] = c
-        scale_ref[k] = scale
+        b_t[k] = jnp.concatenate([b_re, b_im], axis=0).T
         all_edges.append(edges)
         mid = edges.shape[0] // 2
         poses.append(orders(edges[mid : mid + 1])[0])
-    for k in range(vars_):
-        copies[k].wait()
-        c = c_n[k]
-        h_re, b_re = drives(c, h_ref[0, k], src_ref[0, k] + frequency * adj_ref[1, k], inside)
-        h_im, b_im = drives(c, h_ref[1, k], src_ref[1, k] - frequency * adj_ref[0, k], inside)
-        h_ref[0, k], h_ref[1, k] = h_re, h_im
-        b_t[k] = jnp.concatenate([b_re, b_im], axis=0).T
     states = segment_scan(range(vars_), c_t, b_t, c_s, b_s, poses)
     for k in range(vars_):
         put_maps(msg_ref, sign_ref, ent_ref, k, k, states[k], all_edges[k])
@@ -296,16 +290,13 @@
 
 
 def substitute(
-    in_ref, adj_ref, speed_ref, sign_ref, ent_ref, c_s, b_s, h_ref, scale_ref,
-    ent_f, c_f, b_f, h_f,
-    part_ref, res_ref,
-    u_s, u_t,
+    in_ref, adj_ref, sign_ref, ent_ref, c_s, b_s, h_ref, scale_ref, ent_f, c_f, b_f, h_f,
+    part_ref, u_s, u_t,
 ):
-    vars_, lines, cells = speed_ref.shape
+    vars_, lines, cells = scale_ref.shape
     steps, width = c_s.shape[1], c_s.shape[3]
     groups = vars_ + 1
     inside = in_ref[...] > 0.0
-    lane = lax.broadcasted_iota(jnp.int32, (lines, cells), 1)
     poses = [jnp.broadcast_to(sign_ref[k : k + 1, :], (SEGS, width)) > 0.0 for k in range(groups)]
     state = []
     for k in range(groups):
@@ -323,28 +314,42 @@
     face_u = u_t[vars_].T
     for k in range(vars_):
         scale = scale_ref[k]
-        v = speed_ref[k]
-        s = jnp.where(inside, jnp.abs(v), 0.0)
-        up = v > 0.0
-        apart = lane != jnp.where(up, cells - 1, 0)
-
-        def shifted(value):
-            return jnp.where(
-                apart, jnp.where(up, pltpu.roll(value, cells - 1, 1), pltpu.roll(value, 1, 1)), 0.0)
-
         u = u_t[k].T
         for part in range(2):
             at = part * lines + FACE_DEV * k
             h = jnp.concatenate([h_f[at : at + FACE_DEV], h_ref[part, k, FACE_DEV:]], axis=0)
             us = jnp.concatenate(
                 [face_u[at : at + FACE_DEV], u[part * lines + FACE_DEV : (part + 1) * lines]], axis=0)
-            a = adj_ref[part, k]
-            part_ref[part, k] = jnp.where(inside, a, 0.0) + (h + us) * scale
-            g = s * a
-            res_ref[part, k] = h + jnp.where(inside, shifted(2.0 * g - 0.5 * shifted(g)), 0.0)
-
-
-def finish(count, pairwise, in_ref, sign_ref, part_ref, lift_ref, res_ref, *rest):
+            part_ref[part, k] = jnp.where(inside, adj_ref[part, k], 0.0) + (h + us) * scale
+
+
+def fluxes(after_ref, in_ref, adj_ref, speed_ref, flux_ref):
+    vars_, lines, cells = speed_ref.shape
+    half = cells // 2
+    lane = lax.broadcasted_iota(jnp.int32, (lines, half), 1)
+    for k in range(vars_):
+        v = speed_ref[k]
+        s = jnp.abs(v) * in_ref[...]
+        up = v[:, :half] > 0.0
+        last = jnp.where(up, lane, 0) == half - 1
+        first = jnp.where(up, 1, lane) == 0
+
+        def shifted(low, high):
+            low, high = (
+                jnp.where(up, pltpu.roll(x, half - 1, 1), pltpu.roll(x, 1, 1)) for x in (low, high))
+            return (jnp.where(last, high, jnp.where(first, 0.0, low)),
+                    jnp.where(first, low, jnp.where(last, 0.0, high)))
+
+        for part in range(2):
+            g = s * adj_ref[part, k]
+            low, high = g[:, :half], g[:, half:]
+            near = shifted(low, high)
+            low, high = shifted(2.0 * low - 0.5 * near[0], 2.0 * high - 0.5 * near[1])
+            flux_ref[part, k, :, :half] = low * in_ref[:, :half]
+            flux_ref[part, k, :, half:] = high * in_ref[:, half:]
+
+
+def finish(count, pairwise, in_ref, sign_ref, part_ref, lift_ref, h_ref, h_f, flux_ref, *rest):
     got = rest[: count - 1]
     new_hbm, out_hbm, new_ref, out_ref, sems = rest[count - 1 :]
     _, vars_, lines, cells = part_ref.shape
@@ -374,28 +379,33 @@
         if i == 1:
             g1, g2 = jnp.where(has, m[6], 0.0), jnp.where(has, m[7], 0.0)
     r0, r1 = 2.0 * g1 - 0.5 * g2, -0.5 * g1
-    table = jnp.concatenate(
-        [z1, z2, jnp.where(pos, 0.0, r0), jnp.where(pos, 0.0, r1),
-         jnp.where(pos, r0, 0.0), jnp.where(pos, r1, 0.0)]
-        + [zero] * (width // TABLE - 6), axis=0).T
+    down0, down1 = jnp.where(pos, 0.0, r0), jnp.where(pos, 0.0, r1)
+    up0, up1 = jnp.where(pos, r0, 0.0), jnp.where(pos, r1, 0.0)
+    table = jnp.concatenate([z1, z2, jnp.zeros((width - 2 * TABLE, width), F32)], axis=0).T
     half = cells // 2
-    lane = lax.broadcasted_iota(jnp.int32, (lines, half), 1)
+    sub = lax.broadcasted_iota(jnp.int32, (8, width), 0)
+    left = lax.broadcasted_iota(jnp.int32, (lines, half), 1) < half // 2
     copies = []
     for k in range(vars_):
+        row = lambda x: jnp.broadcast_to(x[k : k + 1, :], (8, width))
+        low = jnp.where(sub == 0, row(down0), jnp.where(sub == 1, row(down1), 0.0))
+        high = jnp.where(sub == 7, row(up0), jnp.where(sub == 6, row(up1), 0.0))
+        edges = jnp.concatenate([low, jnp.zeros((half - 16, width), F32), high], axis=0).T
         for part in range(2):
             at = part * lines + FACE_DEV * k
             rows = slice(part * lines, (part + 1) * lines)
-            halo = lambda r: table[rows, TABLE * r + k : TABLE * r + k + 1]
 
             def entering(r):
-                face = TABLE * r + vars_
+                face, main = TABLE * r + vars_, TABLE * r + k
                 return jnp.concatenate(
-                    [table[at : at + FACE_DEV, face : face + 1], halo(r)[FACE_DEV:]], axis=0)
-
-            low = jnp.where(lane == 0, halo(2), jnp.where(lane == 1, halo(3), 0.0))
-            high = jnp.where(lane == half - 1, halo(4), jnp.where(lane == half - 2, halo(5), 0.0))
-            out_ref[part, k, :, :half] = res_ref[part, k, :, :half] + low * in_ref[:, :half]
-            out_ref[part, k, :, half:] = res_ref[part, k, :, half:] + high * in_ref[:, half:]
+                    [table[at : at + FACE_DEV, face : face + 1],
+                     table[part * lines + FACE_DEV : (part + 1) * lines, main : main + 1]], axis=0)
+
+            edge = edges[rows]
+            h = jnp.concatenate([h_f[at : at + FACE_DEV], h_ref[part, k, FACE_DEV:]], axis=0)
+            h = h + flux_ref[part, k]
+            out_ref[part, k, :, :half] = h[:, :half] + jnp.where(left, edge, 0.0) * in_ref[:, :half]
+            out_ref[part, k, :, half:] = h[:, half:] + jnp.where(left, 0.0, edge) * in_ref[:, half:]
             new_ref[part, k] = part_ref[part, k] + (
                 lift_ref[0, k] * entering(0) + lift_ref[1, k] * entering(1))
             for j, (src, dst) in enumerate(((out_ref, out_hbm), (new_ref, new_hbm))):
@@ -438,33 +448,41 @@
     paired = blocks == 8
     entries = blocks * cap
     pieces = blocks // 2 if paired else 1
-    adj, lengths, *packed = pl.pallas_call(
+    adj, lengths, inv, packed = pl.pallas_call(
         functools.partial(pack_faces, blocks, cap, paired),
-        out_shape=[field_shape, jax.ShapeDtypeStruct((1, lines), jnp.int32)]
-        + [shape(entries // pieces, PACK_ROWS, cells // 2)] * pieces,
-        in_specs=[hbm] * 5,
-        out_specs=[vmem] * (2 + pieces),
-        scratch_shapes=[scratch(entries, PACK_ROWS, cells // 2), pltpu.SMEM((faces,), jnp.int32),
-                        pltpu.SMEM((faces,), jnp.int32), scratch(vars_, faces, cells), dma(4 + vars_)],
+        out_shape=[field_shape, jax.ShapeDtypeStruct((1, lines), jnp.int32), var_shape,
+                   shape(entries, PACK_ROWS, cells // 2)],
+        in_specs=[hbm] * 6,
+        out_specs=[vmem] * 4,
+        scratch_shapes=[pltpu.SMEM((faces,), jnp.int32), pltpu.SMEM((faces,), jnp.int32),
+                        scratch(vars_, faces, cells), dma(5 + vars_)],
         compiler_params=limit(6),
-        cost_estimate=cost(2 * 10**6, 4 * 10**6),
         name="pack_faces",
-    )(stay(face_line), stay(face_owner), stay(adj), stay(cpl), stay(line_length.reshape(1, lines)))
+    )(stay(face_line), stay(face_owner), stay(adj), stay(cpl), stay(line_length.reshape(1, lines)),
+      stay(inv))
+    packed = pl.pallas_call(
+        deal,
+        out_shape=[shape(entries // pieces, PACK_ROWS, cells // 2)] * pieces,
+        in_specs=[vmem],
+        out_specs=[vmem] * pieces,
+        compiler_params=limit(4),
+        cost_estimate=cost(2 * 10**6, 4 * 10**7),
+        name="deal",
+    )(packed)
     hop = lambda x, m: lax.ppermute(x, "xs", [(i, i ^ m) for i in range(blocks)])
     if paired:
         landed = [packed[0]] + [hop(packed[m], 2 * m) for m in range(1, pieces)]
-    msg, sign, ent, c_s, b_s, h, scale, mask, src = pl.pallas_call(
+    msg, sign, ent, c_s, b_s, h, scale, mask = pl.pallas_call(
         main_maps,
         out_shape=[table_shape, sign_shape, shape(vars_, 4, SEGS, width), order_shape, order_shape,
-                   field_shape, var_shape, shape(lines, cells), field_shape],
-        in_specs=[vmem] * 4 + [hbm],
-        out_specs=[vmem] * 9,
-        scratch_shapes=[scratch(vars_, lines, cells)] + [scratch(vars_, cells, width)] * 2
-        + [dma(vars_)],
+                   field_shape, var_shape, shape(lines, cells)],
+        in_specs=[vmem] * 5,
+        out_specs=[vmem] * 8,
+        scratch_shapes=[scratch(vars_, cells, width)] * 2,
         compiler_params=limit(14),
         cost_estimate=cost(2 * 10**6, 4 * 10**6),
         name="main_maps",
-    )(adj, lengths, spd, inv, stay(src))
+    )(adj, lengths, src, spd, inv)
     if paired:
         halves = shape(pieces * cap, PACK_ROWS, cells // 2)
         near_half, far_half = pl.pallas_call(
@@ -504,25 +522,34 @@
     got = [
         lax.ppermute(msg, "ax", [(i, meet(i, k)) for i in range(count)]) for k in range(1, count)
     ]
-    part, res = pl.pallas_call(
+    part = pl.pallas_call(
         substitute,
-        out_shape=[field_shape] * 2,
-        in_specs=[vmem] * 13,
-        out_specs=[vmem] * 2,
+        out_shape=field_shape,
+        in_specs=[vmem] * 12,
+        out_specs=vmem,
         scratch_shapes=[kept(vars_ + 1), scratch(vars_ + 1, cells, width)],
         compiler_params=limit(14),
-        cost_estimate=cost(2 * 10**6, 5 * 10**6),
+        cost_estimate=cost(2 * 10**6, 3 * 10**6),
         name="substitute",
-    )(mask, adj, spd, sign, ent, c_s, b_s, h, scale, ent_f, c_f, b_f, h_f)
+    )(mask, adj, sign, ent, c_s, b_s, h, scale, ent_f, c_f, b_f, h_f)
+    flux = pl.pallas_call(
+        fluxes,
+        out_shape=field_shape,
+        in_specs=[vmem] * 4,
+        out_specs=vmem,
+        compiler_params=limit(6),
+        cost_estimate=cost(10**6, 2 * 10**6),
+        name="fluxes",
+    )(part, mask, adj, spd)
     new, out = pl.pallas_call(
         functools.partial(finish, count, pairwise),
         out_shape=[field_shape] * 2,
-        in_specs=[vmem] * (5 + len(got)),
+        in_specs=[vmem] * (7 + len(got)),
         out_specs=[hbm] * 2,
         scratch_shapes=[scratch(2, vars_, lines, cells)] * 2 + [dma(4 * vars_)],
-        compiler_params=limit(8),
+        compiler_params=limit(10),
         name="finish",
-    )(mask, sign, part, lift, res, *got)
+    )(mask, sign, part, lift, h, h_f, flux, *got)
     back = lambda x: jnp.transpose(x.reshape(rows, lines, cells), (1, 0, 2))
     return (back(new), back(out))
 

time: 24.8 us -> 24.2 us (0.976)
  Pallas kernels: 10.2 us -> 8.87 us
  waiting for transfers between devices: 4.56 us -> 5.35 us
    ppermute x4, waiting for transfers between devices: 2.62 us -> 3.53 us  [shards(): lax.ppermute(x, 'xs', [(i, i ^ m) for i in range(blocks)])]
    pallas_call x1, Pallas kernels: 2.96 us -> 2.05 us  [shards(): pl.pallas_call(main_maps, out_shape=[table_shape, sign_shape, shape(vars_...]
    pallas_call x1, Pallas kernels: 2.62 us -> 1.93 us  [shards(): pl.pallas_call(functools.partial(finish, count, pairwise), out_shape=[fie...]
    pallas_call x1 -> x3, Pallas kernels: 2.07 us -> 2.2 us  [the longest x1 1.37 us: shards(): pl.pallas_call(fluxes, out_shape=field_shape, in_specs=[vmem] * 4, out_sp...]
  transfers between devices with their start and end apart: 7 -> 7, of which waited for: 3 -> 4; matrix products, arithmetic and copies ran while one was open for 0% -> 0% of each run, Pallas kernels for 23% -> 20%
where the time goes in v2:
time: 24.2 us; the launch traced here: 24 us
  starting transfers between devices  9.07 us (37%)
  Pallas kernels  8.87 us (37%)
  waiting for transfers between devices  5.35 us (22%)
  between operations  0.73 us (3%)
    ppermute x4, starting transfers between devices, shards(): lax.ppermute(x, 'xs', [(i, i ^ m) for i in range(blocks)])  4.62 us
    ppermute x3, starting transfers between devices, shards(): lax.ppermute(msg, 'ax', [(i, meet(i, k)) for i in range(count)])  4.45 us
    ppermute x4, waiting for transfers between devices, shards(): lax.ppermute(x, 'xs', [(i, i ^ m) for i in range(blocks)])  3.53 us
    pallas_call x1, Pallas kernels, shards(): pl.pallas_call(main_maps, out_shape=[table_shape, sign_shape, shape(vars_...  2.05 us
    pallas_call x1, Pallas kernels, shards(): pl.pallas_call(functools.partial(finish, count, pairwise), out_shape=[fie...  1.93 us
    ppermute x3, waiting for transfers between devices, shards(): lax.ppermute(msg, 'ax', [(i, meet(i, k)) for i in range(count)])  1.82 us
    pallas_call x1, Pallas kernels, shards(): pl.pallas_call(functools.partial(pack_faces, blocks, cap, paired), out_sh...  1.49 us
    pallas_call x1, Pallas kernels, shards(): pl.pallas_call(fluxes, out_shape=field_shape, in_specs=[vmem] * 4, out_sp...  1.37 us
  transfers between devices with their start and end apart: 7, of which 4 were waited for; matrix products, arithmetic and copies ran while one was open for 0% of the time, Pallas kernels for 20%

profile of v2, /device:TPU:0, one launch (start us, length us, event | category | flops | bytes accessed | tf_op | source)
XLA Modules:
  0.0 24.0 jit_solution(1426187231843279924)
XLA Ops:
  0.6 0.0 copy-start.1
  0.6 0.0 copy-start
  0.7 1.5 %pack_faces.1 = (f32[2,5,64,256]{3,2,1,0:T(8,128)S(1)}, s32[1,64]{1,0:T(1,128)S(1)}, f32[5,64,256]{2,1,0:T(8,128)S(1)}, f32[16,24,128]{2,1,0:T(8,128)S(1)}) custom-call(s32[16]{0:T(128)} %line_hbm.1, s32[16]{0:T(128)} %owner_hbm.1, f32[2,5,64,256]{3,2,1,0:T(8,128)} %bitcast.21, f32[5,16,256]{2,1,0:T(8,128)} %bitcast.23, s32[1,64]{1,0:T(1,128)} %bitcast.24, ...), custom_call_target="tpu_custom_call" | custom-call | tf_op jit(solution)/shard_map/pack_faces/pallas_call | solution.py:451
  2.2 3.0 %collective-permute-start = (f32[4,24,128]{2,1,0:T(8,128)S(1)}, f32[4,24,128]{2,1,0:T(8,128)S(1)}, u32[]{:S(2)}, u32[]{:S(2)}) collective-permute-start(f32[4,24,128]{2,1,0:T(8,128)S(1)} %get-tuple-element.38), channel_id=1, source_target_pairs={{0,2},{1,3},{2,0},{3,1},{4,6},{5,7},{6,4},{7,5},{8,10},{9,11},{10,... | collective-permute-start | bytes 147464 | tf_op jit(solution)/shard_map/ppermute | solution.py:472
  5.2 1.5 %collective-permute-start.1 = (f32[4,24,128]{2,1,0:T(8,128)S(1)}, f32[4,24,128]{2,1,0:T(8,128)S(1)}, u32[]{:S(2)}, u32[]{:S(2)}) collective-permute-start(f32[4,24,128]{2,1,0:T(8,128)S(1)} %get-tuple-element.39), channel_id=1, source_target_pairs={{0,4},{1,5},{2,6},{3,7},{4,0},{5,1},{6,2},{7,3},{8,12},{9,13},{10,... | collective-permute-start | bytes 147464 | tf_op jit(solution)/shard_map/ppermute | solution.py:472
  6.7 0.0 collective-permute-start.2
  6.7 0.0 copy-done.1
  6.7 0.0 copy-done
  6.7 2.1 %main_maps.1 = (f32[8,8,128]{2,1,0:T(8,128)S(1)}, f32[8,128]{1,0:T(8,128)S(1)}, f32[5,4,8,128]{3,2,1,0:T(8,128)S(1)}, f32[5,32,8,128]{3,2,1,0:T(8,128)S(1)}, f32...) custom-call(f32[2,5,64,256]{3,2,1,0:T(8,128)S(1)} %get-tuple-element, ...), custom_call_target="tpu_custom_call" | custom-call | flops 2000000 | bytes 4000000 | tf_op jit(solution)/shard_map/main_maps/pallas_call | solution.py:475
  8.8 0.0 collective-permute-done.refs_1_
  8.8 0.5 %collective-permute-done.1.refs_2_ = f32[4,24,128]{2,1,0:T(8,128)S(1)} collective-permute-done((f32[4,24,128]{2,1,0:T(8,128)S(1)}, f32[4,24,128]{2,1,0:T(8,128)S(1)}, u32[]{:S(2)}, u32[]{:S(2)}) %collective-permute-start.1) | collective-permute-done | bytes 49184 | tf_op jit(solution)/shard_map/ppermute | solution.py:472
  9.3 2.4 %collective-permute-done.2.refs_3_ = f32[4,24,128]{2,1,0:T(8,128)S(1)} collective-permute-done((f32[4,24,128]{2,1,0:T(8,128)S(1)}, f32[4,24,128]{2,1,0:T(8,128)S(1)}, u32[]{:S(2)}, u32[]{:S(2)}) %collective-permute-start.2) | collective-permute-done | bytes 49184 | tf_op jit(solution)/shard_map/ppermute | solution.py:472
  11.7 0.1 collective-permute-start.3
  11.8 0.6 %lifts.1.lift_ref = f32[2,5,64,256]{3,2,1,0:T(8,128)S(1)} custom-call(f32[8,128]{1,0:T(8,128)S(1)} %get-tuple-element.32.after_ref.sign_ref.old_sign, f32[5,4,8,128]{3,2,1,0:T(8,128)S(1)} %get-tuple-element.33.ent_ref, f32[5,32,8,128]{3,2,1,0:T(8,128)S(1)} %get-tuple-element.34.c_s, f32[5,64,256]{2,1,0:T(8,128)S(1)} %get-tuple-element.35.scale_ref, ...), custom_call_target="tpu_custom_call" | custom-call | flops 1000000 | bytes 2000000 | tf_op jit(solution)/shard_map/lifts/pallas_call | solution.py:500
  12.4 0.6 %collective-permute-done.3.rest_1_ = f32[8,24,128]{2,1,0:T(8,128)S(1)} collective-permute-done((f32[8,24,128]{2,1,0:T(8,128)S(1)}, f32[8,24,128]{2,1,0:T(8,128)S(1)}, u32[]{:S(2)}, u32[]{:S(2)}) %collective-permute-start.3) | collective-permute-done | bytes 98336 | tf_op jit(solution)/shard_map/ppermute | solution.py:472
  13.1 0.5 %face_maps.1 = (f32[8,8,128]{2,1,0:T(8,128)S(1)}, f32[8,128]{1,0:T(8,128)S(1)}, f32[1,4,8,128]{3,2,1,0:T(8,128)S(1)}, f32[1,32,8,128]{3,2,1,0:T(8,128)S(1)}, f32...) custom-call(f32[2,5,64,256]{3,2,1,0:T(8,128)S(1)} %lifts.1.lift_ref, f32[64,256]{1,0:T(8,128)S(1)} %get-tuple-element.31.in_ref, ...), custom_call_target="tpu_custom_call" | custom-call | tf_op jit(solution)/shard_map/face_maps/pallas_call | solution.py:510
  13.6 3.7 %collective-permute-start.6 = (f32[8,8,128]{2,1,0:T(8,128)S(1)}, f32[8,8,128]{2,1,0:T(8,128)S(1)}, u32[]{:S(2)}, u32[]{:S(2)}) collective-permute-start(f32[8,8,128]{2,1,0:T(8,128)S(1)} %get-tuple-element.51), channel_id=1, source_target_pairs={{0,24},{8,16},{16,8},{24,0},{1,25},{9,17},{17,9},{25,1},{2,26},{10... | collective-permute-start | bytes 98312 | tf_op jit(solution)/shard_map/ppermute | solution.py:523
  17.3 0.0 collective-permute-start.5
  17.3 0.8 %collective-permute-start.4 = (f32[8,8,128]{2,1,0:T(8,128)S(1)}, f32[8,8,128]{2,1,0:T(8,128)S(1)}, u32[]{:S(2)}, u32[]{:S(2)}) collective-permute-start(f32[8,8,128]{2,1,0:T(8,128)S(1)} %get-tuple-element.51), channel_id=1, source_target_pairs={{0,8},{8,0},{16,24},{24,16},{1,9},{9,1},{17,25},{25,17},{2,10},{10... | collective-permute-start | bytes 98312 | tf_op jit(solution)/shard_map/ppermute | solution.py:523
  18.1 0.8 %substitute.1.after_ref.part_ref = f32[2,5,64,256]{3,2,1,0:T(8,128)S(1)} custom-call(f32[64,256]{1,0:T(8,128)S(1)} %get-tuple-element.31.in_ref, f32[2,5,64,256]{3,2,1,0:T(8,128)S(1)} %get-tuple-element.28.adj_ref, f32[8,128]{1,0:T(8,128)S(1)} %get-tuple-element.44.sign_ref, f32[5,4,8,128]{3,2,1,0:T(8,128)S(1)} %get-tuple-element.33.ent_ref, ...), custom_call_target="tpu_custom_call" | custom-call | flops 2000000 | bytes 3000000 | tf_op jit(solution)/shard_map/substitute/pallas_call | solution.py:525
  18.9 1.4 %fluxes.1.flux_ref = f32[2,5,64,256]{3,2,1,0:T(8,128)S(1)} custom-call(f32[2,5,64,256]{3,2,1,0:T(8,128)S(1)} %substitute.1.after_ref.part_ref, f32[64,256]{1,0:T(8,128)S(1)} %get-tuple-element.31.in_ref, f32[2,5,64,256]{3,2,1,0:T(8,128)S(1)} %get-tuple-element.28.adj_ref, f32[5,64,256]{2,1,0:T(8,128)S(1)} %bitcast.18), custom_call_target="tpu_custom_call" | custom-call | flops 1000000 | bytes 2000000 | tf_op jit(solution)/shard_map/fluxes/pallas_call | solution.py:535
  20.3 0.0 collective-permute-done.6.rest_2_
  20.3 1.8 %collective-permute-done.5.rest_1_ = f32[8,8,128]{2,1,0:T(8,128)S(1)} collective-permute-done((f32[8,8,128]{2,1,0:T(8,128)S(1)}, f32[8,8,128]{2,1,0:T(8,128)S(1)}, u32[]{:S(2)}, u32[]{:S(2)}) %collective-permute-start.5) | collective-permute-done | bytes 32800 | tf_op jit(solution)/shard_map/ppermute | solution.py:523
  22.1 0.0 collective-permute-done.4.rest_0_
  22.1 1.9 %finish.1 = (f32[2,5,64,256]{3,2,1,0:T(8,128)}, f32[2,5,64,256]{3,2,1,0:T(8,128)}) custom-call(f32[64,256]{1,0:T(8,128)S(1)} %get-tuple-element.31.in_ref, f32[8,128]{1,0:T(8,128)S(1)} %get-tuple-element.44.sign_ref, f32[2,5,64,256]{3,2,1,0:T(8,128)S(1)} %substitute.1.after_ref.part_ref, f32[2,5,64,256]{3,2,1,0:T(8,128)S(1)} %lifts.1.lift_ref, ...), custom_call_target="tpu_custom_call" | custom-call | tf_op jit(solution)/shard_map/finish/pallas_call | solution.py:544
  (2 shorter events, 0.0 us)
Async XLA Ops:
  0.6 6.1 %copy-start.1 = (f32[64,10,256]{2,0,1:T(8,128)S(1)}, f32[64,10,256]{2,0,1:T(8,128)}, u32[]{:S(2)}) copy-start(f32[64,10,256]{2,0,1:T(8,128)} %param.9) | copy-start | bytes 1966084
  0.6 6.1 %copy-start = (f32[64,5,256]{2,0,1:T(8,128)S(1)}, f32[64,5,256]{2,0,1:T(8,128)}, u32[]{:S(2)}) copy-start(f32[64,5,256]{2,0,1:T(8,128)} %param.10) | copy-start | bytes 983044
  2.2 6.6 %collective-permute-start = (f32[4,24,128]{2,1,0:T(8,128)S(1)}, f32[4,24,128]{2,1,0:T(8,128)S(1)}, u32[]{:S(2)}, u32[]{:S(2)}) collective-permute-start(f32[4,24,128]{2,1,0:T(8,128)S(1)} %get-tuple-element.38), channel_id=1, source_target_pairs={{0,2},{1,3},{2,0},{3,1},{4,6},{5,7},{6,4},{7,5},{8,10},{9,11},{10,... | collective-permute-start | bytes 147464 | tf_op jit(solution)/shard_map/ppermute | solution.py:472
  5.2 4.1 %collective-permute-start.1 = (f32[4,24,128]{2,1,0:T(8,128)S(1)}, f32[4,24,128]{2,1,0:T(8,128)S(1)}, u32[]{:S(2)}, u32[]{:S(2)}) collective-permute-start(f32[4,24,128]{2,1,0:T(8,128)S(1)} %get-tuple-element.39), channel_id=1, source_target_pairs={{0,4},{1,5},{2,6},{3,7},{4,0},{5,1},{6,2},{7,3},{8,12},{9,13},{10,... | collective-permute-start | bytes 147464 | tf_op jit(solution)/shard_map/ppermute | solution.py:472
  6.7 5.0 %collective-permute-start.2 = (f32[4,24,128]{2,1,0:T(8,128)S(1)}, f32[4,24,128]{2,1,0:T(8,128)S(1)}, u32[]{:S(2)}, u32[]{:S(2)}) collective-permute-start(f32[4,24,128]{2,1,0:T(8,128)S(1)} %get-tuple-element.40), channel_id=1, source_target_pairs={{0,6},{1,7},{2,4},{3,5},{4,2},{5,3},{6,0},{7,1},{8,14},{9,15},{10,... | collective-permute-start | bytes 147464 | tf_op jit(solution)/shard_map/ppermute | solution.py:472
  11.7 1.4 %collective-permute-start.3 = (f32[8,24,128]{2,1,0:T(8,128)S(1)}, f32[8,24,128]{2,1,0:T(8,128)S(1)}, u32[]{:S(2)}, u32[]{:S(2)}) collective-permute-start(f32[8,24,128]{2,1,0:T(8,128)S(1)} %get-tuple-element.43), channel_id=1, source_target_pairs={{0,1},{1,0},{2,3},{3,2},{4,5},{5,4},{6,7},{7,6},{8,9},{9,8},{10,11... | collective-permute-start | bytes 294920 | tf_op jit(solution)/shard_map/ppermute | solution.py:472
  13.6 6.7 %collective-permute-start.6 = (f32[8,8,128]{2,1,0:T(8,128)S(1)}, f32[8,8,128]{2,1,0:T(8,128)S(1)}, u32[]{:S(2)}, u32[]{:S(2)}) collective-permute-start(f32[8,8,128]{2,1,0:T(8,128)S(1)} %get-tuple-element.51), channel_id=1, source_target_pairs={{0,24},{8,16},{16,8},{24,0},{1,25},{9,17},{17,9},{25,1},{2,26},{10... | collective-permute-start | bytes 98312 | tf_op jit(solution)/shard_map/ppermute | solution.py:523
  17.3 4.8 %collective-permute-start.5 = (f32[8,8,128]{2,1,0:T(8,128)S(1)}, f32[8,8,128]{2,1,0:T(8,128)S(1)}, u32[]{:S(2)}, u32[]{:S(2)}) collective-permute-start(f32[8,8,128]{2,1,0:T(8,128)S(1)} %get-tuple-element.51), channel_id=1, source_target_pairs={{0,16},{8,24},{16,0},{24,8},{1,17},{9,25},{17,1},{25,9},{2,18},{10... | collective-permute-start | bytes 98312 | tf_op jit(solution)/shard_map/ppermute | solution.py:523
  17.3 4.8 %collective-permute-start.4 = (f32[8,8,128]{2,1,0:T(8,128)S(1)}, f32[8,8,128]{2,1,0:T(8,128)S(1)}, u32[]{:S(2)}, u32[]{:S(2)}) collective-permute-start(f32[8,8,128]{2,1,0:T(8,128)S(1)} %get-tuple-element.51), channel_id=1, source_target_pairs={{0,8},{8,0},{16,24},{24,16},{1,9},{9,1},{17,25},{25,17},{2,10},{10... | collective-permute-start | bytes 98312 | tf_op jit(solution)/shard_map/ppermute | solution.py:523

commit v3 on v2

--- a/solution.py
+++ b/solution.py
@@ -178,22 +178,18 @@
         jnp.where(real, prev(m11, 1, 1.0), prev(m12, 1, 0.0)),
         jnp.where(real, prev(m21, 1, 0.0), prev(m22, 1, 1.0)),
     )
-    return (m11, m12, m21, m22, v1, v2), entry
-
-
-def put_maps(msg_ref, sign_ref, ent_ref, k, slot, state, edges):
+    return (jnp.where(real, m11, m12), jnp.where(real, m21, m22), v1, v2), entry
+
+
+def end_rows(state, edges):
     half = edges.shape[0]
     sign_row = edges[half // 2 : half // 2 + 1]
-    pos, order = orders(sign_row)
-    maps, entry = compose(state, pos, order)
+    maps, entry = compose(state, *orders(sign_row))
     up = sign_row > 0.0
-    for row, value in enumerate(maps):
-        msg_ref[row, k : k + 1, :] = jnp.where(up, value[0:1], value[SEGS - 1 : SEGS])
-    msg_ref[6, k : k + 1, :] = jnp.where(up, edges[0:1], edges[half - 1 : half])
-    msg_ref[7, k : k + 1, :] = jnp.where(up, edges[1:2], edges[half - 2 : half - 1])
-    sign_ref[k : k + 1, :] = sign_row
-    for row, value in enumerate(entry):
-        ent_ref[slot, row] = value
+    rows = [jnp.where(up, value[0:1], value[SEGS - 1 : SEGS]) for value in maps]
+    rows.append(jnp.where(up, edges[0:1], edges[half - 1 : half]))
+    rows.append(jnp.where(up, edges[1:2], edges[half - 2 : half - 1]))
+    return rows, entry, sign_row
 
 
 def main_maps(
@@ -219,7 +215,12 @@
         poses.append(orders(edges[mid : mid + 1])[0])
     states = segment_scan(range(vars_), c_t, b_t, c_s, b_s, poses)
     for k in range(vars_):
-        put_maps(msg_ref, sign_ref, ent_ref, k, k, states[k], all_edges[k])
+        rows, entry, sign_row = end_rows(states[k], all_edges[k])
+        for i, row in enumerate(rows):
+            msg_ref[vars_ * i + k : vars_ * i + k + 1, :] = row
+        for i, value in enumerate(entry):
+            ent_ref[k, i] = value
+        sign_ref[k : k + 1, :] = sign_row
 
 
 def face_maps(
@@ -260,7 +261,17 @@
     state = segment_scan([0], c_t, b_t, c_s, b_s, [orders(edges[mid : mid + 1])[0]])[0]
     msg_ref[...] = old_msg[...]
     sign_ref[...] = old_sign[...]
-    put_maps(msg_ref, sign_ref, ent_ref, vars_, 0, state, edges)
+    rows, entry, sign_row = end_rows(state, edges)
+    for i, value in enumerate(entry):
+        ent_ref[0, i] = value
+    sign_ref[vars_ : vars_ + 1, :] = sign_row
+    width = 2 * lines
+    facing = lax.rem(lax.broadcasted_iota(jnp.int32, (1, width), 1), lines) < FACE_DEV
+    for i in (2, 3):
+        for k in range(vars_):
+            at = slice(vars_ * i + k, vars_ * i + k + 1)
+            moved = pltpu.roll(rows[i], width - FACE_DEV * k, 1) if k else rows[i]
+            msg_ref[at, :] = jnp.where(facing, moved, old_msg[at, :])
 
 
 def unfold(k, t, steps, value, kept, turned, pos):
@@ -349,39 +360,46 @@
             flux_ref[part, k, :, half:] = high * in_ref[:, half:]
 
 
-def finish(count, pairwise, in_ref, sign_ref, part_ref, lift_ref, h_ref, h_f, flux_ref, *rest):
+def finish(count, sources, in_ref, sign_ref, part_ref, lift_ref, h_ref, h_f, flux_ref, *rest):
     got = rest[: count - 1]
     new_hbm, out_hbm, new_ref, out_ref, sems = rest[count - 1 :]
     _, vars_, lines, cells = part_ref.shape
     width = 2 * lines
     place = lax.axis_index("ax")
     odd = lax.rem(place, 2) == 1
-    pos = sign_ref[...] > 0.0
-    zero = jnp.zeros((TABLE, width), F32)
+    pos = sign_ref[:vars_] > 0.0
+    real = lax.broadcasted_iota(jnp.int32, (vars_, width), 1) < lines
+    zero = jnp.zeros((vars_, width), F32)
     z1, z2, g1, g2 = zero, zero, zero, zero
     for i in range(count - 1, 0, -1):
         near = jnp.where(place >= i, 1.0, 0.0)
         far = jnp.where(place + i <= count - 1, 1.0, 0.0)
         has = jnp.where(pos, far, near) > 0.0
 
+        def pick(offset, at):
+            value = got[0][at]
+            for j in range(1, count - 1):
+                here = [p for p in range(count) if p + offset == sources[j][p]]
+                hit = functools.reduce(jnp.logical_or, [place == p for p in here], place < 0)
+                value = jnp.where(hit, got[j][at], value)
+            return value
+
         def field(r):
-            if not pairwise:
-                return jnp.where(pos, got[count - i - 1][r], got[i - 1][r])
-            if i > 1:
-                return got[i - 1][r]
-            one, three = got[0][r], got[2][r]
-            return jnp.where(pos, jnp.where(odd, three, one), jnp.where(odd, one, three))
-
-        m = [field(r) for r in range(8 if i == 1 else 6)]
-        n1 = m[0] * z1 + m[1] * z2 + m[4]
-        n2 = m[2] * z1 + m[3] * z2 + m[5]
-        z1, z2 = jnp.where(has, n1, z1), jnp.where(has, n2, z2)
+            at = slice(vars_ * r, vars_ * (r + 1))
+            return jnp.where(pos, pick(i, at), pick(-i, at))
+
+        n1, n2, b1, b2 = [field(r) for r in range(4)]
+        o1, o2 = pltpu.roll(n1, lines, 1), pltpu.roll(n2, lines, 1)
+        t1 = jnp.where(real, n1, o1) * z1 + jnp.where(real, o1, n1) * z2 + b1
+        t2 = jnp.where(real, n2, o2) * z1 + jnp.where(real, o2, n2) * z2 + b2
+        z1, z2 = jnp.where(has, t1, z1), jnp.where(has, t2, z2)
         if i == 1:
-            g1, g2 = jnp.where(has, m[6], 0.0), jnp.where(has, m[7], 0.0)
+            g1, g2 = jnp.where(has, field(4), 0.0), jnp.where(has, field(5), 0.0)
     r0, r1 = 2.0 * g1 - 0.5 * g2, -0.5 * g1
     down0, down1 = jnp.where(pos, 0.0, r0), jnp.where(pos, 0.0, r1)
     up0, up1 = jnp.where(pos, r0, 0.0), jnp.where(pos, r1, 0.0)
-    table = jnp.concatenate([z1, z2, jnp.zeros((width - 2 * TABLE, width), F32)], axis=0).T
+    fill = jnp.zeros((TABLE - vars_, width), F32)
+    table = jnp.concatenate([z1, fill, z2, fill, jnp.zeros((width - 2 * TABLE, width), F32)], axis=0).T
     half = cells // 2
     sub = lax.broadcasted_iota(jnp.int32, (8, width), 0)
     left = lax.broadcasted_iota(jnp.int32, (lines, half), 1) < half // 2
@@ -396,10 +414,7 @@
             rows = slice(part * lines, (part + 1) * lines)
 
             def entering(r):
-                face, main = TABLE * r + vars_, TABLE * r + k
-                return jnp.concatenate(
-                    [table[at : at + FACE_DEV, face : face + 1],
-                     table[part * lines + FACE_DEV : (part + 1) * lines, main : main + 1]], axis=0)
+                return table[rows, TABLE * r + k : TABLE * r + k + 1]
 
             edge = edges[rows]
             h = jnp.concatenate([h_f[at : at + FACE_DEV], h_ref[part, k, FACE_DEV:]], axis=0)
@@ -439,7 +454,7 @@
     limit = lambda mib: pltpu.CompilerParams(vmem_limit_bytes=mib << 20)
     cost = lambda flops, moved: pl.CostEstimate(
         flops=flops, bytes_accessed=moved, transcendentals=0)
-    table_shape = shape(8, TABLE, width)
+    table_shape = shape(TABLE * pl.cdiv(6 * vars_, TABLE), width)
     sign_shape = shape(TABLE, width)
     order_shape = shape(vars_, steps, SEGS, width)
     field_shape = shape(2, vars_, lines, cells)
@@ -517,11 +532,12 @@
         compiler_params=limit(10),
         name="face_maps",
     )(lift, mask, adj, src, spd, inv, msg, sign, *recv)
-    pairwise = count == 4
-    meet = (lambda i, k: i ^ k) if pairwise else (lambda i, k: (i + k) % count)
-    got = [
-        lax.ppermute(msg, "ax", [(i, meet(i, k)) for i in range(count)]) for k in range(1, count)
-    ]
+    if count == 4:
+        routes = [(1, 0, 3, 2), (3, 2, 0, 1), (2, 3, 1, 0)]
+    else:
+        routes = [[(i + k) % count for i in range(count)] for k in range(1, count)]
+    sources = [[r.index(p) for p in range(count)] for r in routes]
+    got = [lax.ppermute(msg, "ax", list(enumerate(r))) for r in routes]
     part = pl.pallas_call(
         substitute,
         out_shape=field_shape,
@@ -542,7 +558,7 @@
         name="fluxes",
     )(part, mask, adj, spd)
     new, out = pl.pallas_call(
-        functools.partial(finish, count, pairwise),
+        functools.partial(finish, count, sources),
         out_shape=[field_shape] * 2,
         in_specs=[vmem] * (7 + len(got)),
         out_specs=[hbm] * 2,

time: 24.2 us -> 23.1 us (0.955)
  waiting for transfers between devices: 5.35 us -> 4.71 us
  Pallas kernels: 8.87 us -> 8.62 us
    ppermute x3, waiting for transfers between devices: 1.82 us -> 1.19 us  [shards(): got = [lax.ppermute(msg, 'ax', list(enumerate(r))) for r in routes]]
    pallas_call x1, Pallas kernels: 1.93 us -> 1.6 us  [shards(): pl.pallas_call(functools.partial(finish, count, sources), out_shape=[fiel...]
  transfers between devices with their start and end apart: 7 -> 7, of which waited for: 4 -> 5; matrix products, arithmetic and copies ran while one was open for 0% -> 0% of each run, Pallas kernels for 20% -> 21%
where the time goes in v3:
time: 23.1 us; the launch traced here: 22.9 us
  starting transfers between devices  8.84 us (38%)
  Pallas kernels  8.62 us (37%)
  waiting for transfers between devices  4.71 us (20%)
  between operations  0.73 us (3%)
    ppermute x4, starting transfers between devices, shards(): lax.ppermute(x, 'xs', [(i, i ^ m) for i in range(blocks)])  4.62 us
    ppermute x3, starting transfers between devices, shards(): got = [lax.ppermute(msg, 'ax', list(enumerate(r))) for r in routes]  4.22 us
    ppermute x4, waiting for transfers between devices, shards(): lax.ppermute(x, 'xs', [(i, i ^ m) for i in range(blocks)])  3.53 us
    pallas_call x1, Pallas kernels, shards(): pl.pallas_call(main_maps, out_shape=[table_shape, sign_shape, shape(vars_...  2.06 us
    pallas_call x1, Pallas kernels, shards(): pl.pallas_call(functools.partial(finish, count, sources), out_shape=[fiel...  1.6 us
    pallas_call x1, Pallas kernels, shards(): pl.pallas_call(functools.partial(pack_faces, blocks, cap, paired), out_sh...  1.49 us
    pallas_call x1, Pallas kernels, shards(): pl.pallas_call(fluxes, out_shape=field_shape, in_specs=[vmem] * 4, out_sp...  1.37 us
    ppermute x3, waiting for transfers between devices, shards(): got = [lax.ppermute(msg, 'ax', list(enumerate(r))) for r in routes]  1.19 us
  transfers between devices with their start and end apart: 7, of which 5 were waited for; matrix products, arithmetic and copies ran while one was open for 0% of the time, Pallas kernels for 21%

profile of v3, /device:TPU:0, one launch (start us, length us, event | category | flops | bytes accessed | tf_op | source)
XLA Modules:
  0.0 22.9 jit_solution(17199587598248183658)
XLA Ops:
  0.6 0.0 copy-start.1
  0.6 0.0 copy-start
  0.7 1.5 %pack_faces.1 = (f32[2,5,64,256]{3,2,1,0:T(8,128)S(1)}, s32[1,64]{1,0:T(1,128)S(1)}, f32[5,64,256]{2,1,0:T(8,128)S(1)}, f32[16,24,128]{2,1,0:T(8,128)S(1)}) custom-call(s32[16]{0:T(128)} %line_hbm.1, s32[16]{0:T(128)} %owner_hbm.1, f32[2,5,64,256]{3,2,1,0:T(8,128)} %bitcast.21, f32[5,16,256]{2,1,0:T(8,128)} %bitcast.23, s32[1,64]{1,0:T(1,128)} %bitcast.24, ...), custom_call_target="tpu_custom_call" | custom-call | tf_op jit(solution)/shard_map/pack_faces/pallas_call | solution.py:466
  2.2 3.0 %collective-permute-start = (f32[4,24,128]{2,1,0:T(8,128)S(1)}, f32[4,24,128]{2,1,0:T(8,128)S(1)}, u32[]{:S(2)}, u32[]{:S(2)}) collective-permute-start(f32[4,24,128]{2,1,0:T(8,128)S(1)} %get-tuple-element.38), channel_id=1, source_target_pairs={{0,2},{1,3},{2,0},{3,1},{4,6},{5,7},{6,4},{7,5},{8,10},{9,11},{10,... | collective-permute-start | bytes 147464 | tf_op jit(solution)/shard_map/ppermute | solution.py:487
  5.2 1.5 %collective-permute-start.1 = (f32[4,24,128]{2,1,0:T(8,128)S(1)}, f32[4,24,128]{2,1,0:T(8,128)S(1)}, u32[]{:S(2)}, u32[]{:S(2)}) collective-permute-start(f32[4,24,128]{2,1,0:T(8,128)S(1)} %get-tuple-element.39), channel_id=1, source_target_pairs={{0,4},{1,5},{2,6},{3,7},{4,0},{5,1},{6,2},{7,3},{8,12},{9,13},{10,... | collective-permute-start | bytes 147464 | tf_op jit(solution)/shard_map/ppermute | solution.py:487
  6.7 0.0 collective-permute-start.2
  6.7 0.0 copy-done.1
  6.7 0.0 copy-done
  6.7 2.1 %main_maps.1 = (f32[32,128]{1,0:T(8,128)S(1)}, f32[8,128]{1,0:T(8,128)S(1)}, f32[5,4,8,128]{3,2,1,0:T(8,128)S(1)}, f32[5,32,8,128]{3,2,1,0:T(8,128)S(1)}, f32[5,...) custom-call(f32[2,5,64,256]{3,2,1,0:T(8,128)S(1)} %get-tuple-element, ...), custom_call_target="tpu_custom_call" | custom-call | flops 2000000 | bytes 4000000 | tf_op jit(solution)/shard_map/main_maps/pallas_call | solution.py:490
  8.8 0.0 collective-permute-done.refs_1_
  8.8 0.5 %collective-permute-done.1.refs_2_ = f32[4,24,128]{2,1,0:T(8,128)S(1)} collective-permute-done((f32[4,24,128]{2,1,0:T(8,128)S(1)}, f32[4,24,128]{2,1,0:T(8,128)S(1)}, u32[]{:S(2)}, u32[]{:S(2)}) %collective-permute-start.1) | collective-permute-done | bytes 49184 | tf_op jit(solution)/shard_map/ppermute | solution.py:487
  9.3 2.4 %collective-permute-done.2.refs_3_ = f32[4,24,128]{2,1,0:T(8,128)S(1)} collective-permute-done((f32[4,24,128]{2,1,0:T(8,128)S(1)}, f32[4,24,128]{2,1,0:T(8,128)S(1)}, u32[]{:S(2)}, u32[]{:S(2)}) %collective-permute-start.2) | collective-permute-done | bytes 49184 | tf_op jit(solution)/shard_map/ppermute | solution.py:487
  11.7 0.1 collective-permute-start.3
  11.8 0.6 %lifts.1.lift_ref = f32[2,5,64,256]{3,2,1,0:T(8,128)S(1)} custom-call(f32[8,128]{1,0:T(8,128)S(1)} %get-tuple-element.32.after_ref.sign_ref.old_sign, f32[5,4,8,128]{3,2,1,0:T(8,128)S(1)} %get-tuple-element.33.ent_ref, f32[5,32,8,128]{3,2,1,0:T(8,128)S(1)} %get-tuple-element.34.c_s, f32[5,64,256]{2,1,0:T(8,128)S(1)} %get-tuple-element.35.scale_ref, ...), custom_call_target="tpu_custom_call" | custom-call | flops 1000000 | bytes 2000000 | tf_op jit(solution)/shard_map/lifts/pallas_call | solution.py:515
  12.4 0.6 %collective-permute-done.3.rest_1_ = f32[8,24,128]{2,1,0:T(8,128)S(1)} collective-permute-done((f32[8,24,128]{2,1,0:T(8,128)S(1)}, f32[8,24,128]{2,1,0:T(8,128)S(1)}, u32[]{:S(2)}, u32[]{:S(2)}) %collective-permute-start.3) | collective-permute-done | bytes 98336 | tf_op jit(solution)/shard_map/ppermute | solution.py:487
  13.1 0.6 %face_maps.1 = (f32[32,128]{1,0:T(8,128)S(1)}, f32[8,128]{1,0:T(8,128)S(1)}, f32[1,4,8,128]{3,2,1,0:T(8,128)S(1)}, f32[1,32,8,128]{3,2,1,0:T(8,128)S(1)}, f32[1,...) custom-call(f32[2,5,64,256]{3,2,1,0:T(8,128)S(1)} %lifts.1.lift_ref, f32[64,256]{1,0:T(8,128)S(1)} %get-tuple-element.31.in_ref, ...), custom_call_target="tpu_custom_call" | custom-call | tf_op jit(solution)/shard_map/face_maps/pallas_call | solution.py:525
  13.7 2.6 %collective-permute-start.6 = (f32[32,128]{1,0:T(8,128)S(1)}, f32[32,128]{1,0:T(8,128)S(1)}, u32[]{:S(2)}, u32[]{:S(2)}) collective-permute-start(f32[32,128]{1,0:T(8,128)S(1)} %get-tuple-element.51), channel_id=1, source_target_pairs={{0,16},{8,24},{16,8},{24,0},{1,17},{9,25},{17,9},{25,1},{2,18},{10... | collective-permute-start | bytes 49160 | tf_op jit(solution)/shard_map/ppermute | solution.py:540
  16.3 1.2 %collective-permute-start.5 = (f32[32,128]{1,0:T(8,128)S(1)}, f32[32,128]{1,0:T(8,128)S(1)}, u32[]{:S(2)}, u32[]{:S(2)}) collective-permute-start(f32[32,128]{1,0:T(8,128)S(1)} %get-tuple-element.51), channel_id=1, source_target_pairs={{0,24},{8,16},{16,0},{24,8},{1,25},{9,17},{17,1},{25,9},{2,26},{10... | collective-permute-start | bytes 49160 | tf_op jit(solution)/shard_map/ppermute | solution.py:540
  17.6 0.3 %collective-permute-start.4 = (f32[32,128]{1,0:T(8,128)S(1)}, f32[32,128]{1,0:T(8,128)S(1)}, u32[]{:S(2)}, u32[]{:S(2)}) collective-permute-start(f32[32,128]{1,0:T(8,128)S(1)} %get-tuple-element.51), channel_id=1, source_target_pairs={{0,8},{8,0},{16,24},{24,16},{1,9},{9,1},{17,25},{25,17},{2,10},{10... | collective-permute-start | bytes 49160 | tf_op jit(solution)/shard_map/ppermute | solution.py:540
  17.9 0.8 %substitute.1.after_ref.part_ref = f32[2,5,64,256]{3,2,1,0:T(8,128)S(1)} custom-call(f32[64,256]{1,0:T(8,128)S(1)} %get-tuple-element.31.in_ref, f32[2,5,64,256]{3,2,1,0:T(8,128)S(1)} %get-tuple-element.28.adj_ref, f32[8,128]{1,0:T(8,128)S(1)} %get-tuple-element.44.sign_ref, f32[5,4,8,128]{3,2,1,0:T(8,128)S(1)} %get-tuple-element.33.ent_ref, ...), custom_call_target="tpu_custom_call" | custom-call | flops 2000000 | bytes 3000000 | tf_op jit(solution)/shard_map/substitute/pallas_call | solution.py:541
  18.7 1.4 %fluxes.1.flux_ref = f32[2,5,64,256]{3,2,1,0:T(8,128)S(1)} custom-call(f32[2,5,64,256]{3,2,1,0:T(8,128)S(1)} %substitute.1.after_ref.part_ref, f32[64,256]{1,0:T(8,128)S(1)} %get-tuple-element.31.in_ref, f32[2,5,64,256]{3,2,1,0:T(8,128)S(1)} %get-tuple-element.28.adj_ref, f32[5,64,256]{2,1,0:T(8,128)S(1)} %bitcast.18), custom_call_target="tpu_custom_call" | custom-call | flops 1000000 | bytes 2000000 | tf_op jit(solution)/shard_map/fluxes/pallas_call | solution.py:551
  20.1 0.0 collective-permute-done.6.rest_2_
  20.1 0.9 %collective-permute-done.5.rest_1_ = f32[32,128]{1,0:T(8,128)S(1)} collective-permute-done((f32[32,128]{1,0:T(8,128)S(1)}, f32[32,128]{1,0:T(8,128)S(1)}, u32[]{:S(2)}, u32[]{:S(2)}) %collective-permute-start.5) | collective-permute-done | bytes 16416 | tf_op jit(solution)/shard_map/ppermute | solution.py:540
  21.1 0.2 %collective-permute-done.4.rest_0_ = f32[32,128]{1,0:T(8,128)S(1)} collective-permute-done((f32[32,128]{1,0:T(8,128)S(1)}, f32[32,128]{1,0:T(8,128)S(1)}, u32[]{:S(2)}, u32[]{:S(2)}) %collective-permute-start.4) | collective-permute-done | bytes 16416 | tf_op jit(solution)/shard_map/ppermute | solution.py:540
  21.3 1.6 %finish.1 = (f32[2,5,64,256]{3,2,1,0:T(8,128)}, f32[2,5,64,256]{3,2,1,0:T(8,128)}) custom-call(f32[64,256]{1,0:T(8,128)S(1)} %get-tuple-element.31.in_ref, f32[8,128]{1,0:T(8,128)S(1)} %get-tuple-element.44.sign_ref, f32[2,5,64,256]{3,2,1,0:T(8,128)S(1)} %substitute.1.after_ref.part_ref, f32[2,5,64,256]{3,2,1,0:T(8,128)S(1)} %lifts.1.lift_ref, ...), custom_call_target="tpu_custom_call" | custom-call | tf_op jit(solution)/shard_map/finish/pallas_call | solution.py:560
  (2 shorter events, 0.0 us)
Async XLA Ops:
  0.6 6.1 %copy-start.1 = (f32[64,10,256]{2,0,1:T(8,128)S(1)}, f32[64,10,256]{2,0,1:T(8,128)}, u32[]{:S(2)}) copy-start(f32[64,10,256]{2,0,1:T(8,128)} %param.9) | copy-start | bytes 1966084
  0.6 6.1 %copy-start = (f32[64,5,256]{2,0,1:T(8,128)S(1)}, f32[64,5,256]{2,0,1:T(8,128)}, u32[]{:S(2)}) copy-start(f32[64,5,256]{2,0,1:T(8,128)} %param.10) | copy-start | bytes 983044
  2.2 6.6 %collective-permute-start = (f32[4,24,128]{2,1,0:T(8,128)S(1)}, f32[4,24,128]{2,1,0:T(8,128)S(1)}, u32[]{:S(2)}, u32[]{:S(2)}) collective-permute-start(f32[4,24,128]{2,1,0:T(8,128)S(1)} %get-tuple-element.38), channel_id=1, source_target_pairs={{0,2},{1,3},{2,0},{3,1},{4,6},{5,7},{6,4},{7,5},{8,10},{9,11},{10,... | collective-permute-start | bytes 147464 | tf_op jit(solution)/shard_map/ppermute | solution.py:487
  5.2 4.1 %collective-permute-start.1 = (f32[4,24,128]{2,1,0:T(8,128)S(1)}, f32[4,24,128]{2,1,0:T(8,128)S(1)}, u32[]{:S(2)}, u32[]{:S(2)}) collective-permute-start(f32[4,24,128]{2,1,0:T(8,128)S(1)} %get-tuple-element.39), channel_id=1, source_target_pairs={{0,4},{1,5},{2,6},{3,7},{4,0},{5,1},{6,2},{7,3},{8,12},{9,13},{10,... | collective-permute-start | bytes 147464 | tf_op jit(solution)/shard_map/ppermute | solution.py:487
  6.7 5.0 %collective-permute-start.2 = (f32[4,24,128]{2,1,0:T(8,128)S(1)}, f32[4,24,128]{2,1,0:T(8,128)S(1)}, u32[]{:S(2)}, u32[]{:S(2)}) collective-permute-start(f32[4,24,128]{2,1,0:T(8,128)S(1)} %get-tuple-element.40), channel_id=1, source_target_pairs={{0,6},{1,7},{2,4},{3,5},{4,2},{5,3},{6,0},{7,1},{8,14},{9,15},{10,... | collective-permute-start | bytes 147464 | tf_op jit(solution)/shard_map/ppermute | solution.py:487
  11.7 1.4 %collective-permute-start.3 = (f32[8,24,128]{2,1,0:T(8,128)S(1)}, f32[8,24,128]{2,1,0:T(8,128)S(1)}, u32[]{:S(2)}, u32[]{:S(2)}) collective-permute-start(f32[8,24,128]{2,1,0:T(8,128)S(1)} %get-tuple-element.43), channel_id=1, source_target_pairs={{0,1},{1,0},{2,3},{3,2},{4,5},{5,4},{6,7},{7,6},{8,9},{9,8},{10,11... | collective-permute-start | bytes 294920 | tf_op jit(solution)/shard_map/ppermute | solution.py:487
  13.7 6.4 %collective-permute-start.6 = (f32[32,128]{1,0:T(8,128)S(1)}, f32[32,128]{1,0:T(8,128)S(1)}, u32[]{:S(2)}, u32[]{:S(2)}) collective-permute-start(f32[32,128]{1,0:T(8,128)S(1)} %get-tuple-element.51), channel_id=1, source_target_pairs={{0,16},{8,24},{16,8},{24,0},{1,17},{9,25},{17,9},{25,1},{2,18},{10... | collective-permute-start | bytes 49160 | tf_op jit(solution)/shard_map/ppermute | solution.py:540
  16.3 4.7 %collective-permute-start.5 = (f32[32,128]{1,0:T(8,128)S(1)}, f32[32,128]{1,0:T(8,128)S(1)}, u32[]{:S(2)}, u32[]{:S(2)}) collective-permute-start(f32[32,128]{1,0:T(8,128)S(1)} %get-tuple-element.51), channel_id=1, source_target_pairs={{0,24},{8,16},{16,0},{24,8},{1,25},{9,17},{17,1},{25,9},{2,26},{10... | collective-permute-start | bytes 49160 | tf_op jit(solution)/shard_map/ppermute | solution.py:540
  17.6 3.7 %collective-permute-start.4 = (f32[32,128]{1,0:T(8,128)S(1)}, f32[32,128]{1,0:T(8,128)S(1)}, u32[]{:S(2)}, u32[]{:S(2)}) collective-permute-start(f32[32,128]{1,0:T(8,128)S(1)} %get-tuple-element.51), channel_id=1, source_target_pairs={{0,8},{8,0},{16,24},{24,16},{1,9},{9,1},{17,25},{25,17},{2,10},{10... | collective-permute-start | bytes 49160 | tf_op jit(solution)/shard_map/ppermute | solution.py:540

commit v4 on v3

--- a/solution.py
+++ b/solution.py
@@ -486,7 +486,7 @@
     )(packed)
     hop = lambda x, m: lax.ppermute(x, "xs", [(i, i ^ m) for i in range(blocks)])
     if paired:
-        landed = [packed[0]] + [hop(packed[m], 2 * m) for m in range(1, pieces)]
+        landed = [packed[0]] + [hop(packed[m], 2 * m) for m in (1, 3, 2)]
     msg, sign, ent, c_s, b_s, h, scale, mask = pl.pallas_call(
         main_maps,
         out_shape=[table_shape, sign_shape, shape(vars_, 4, SEGS, width), order_shape, order_shape,

time: 23.1 us -> 22.1 us (0.957)
  waiting for transfers between devices: 4.71 us -> 3.79 us
    ppermute x4, waiting for transfers between devices: 3.53 us -> 2.6 us  [shards(): lax.ppermute(x, 'xs', [(i, i ^ m) for i in range(blocks)])]
  transfers between devices with their start and end apart: 7 -> 7, of which waited for: 5 -> 5; matrix products, arithmetic and copies ran while one was open for 0% -> 0% of each run, Pallas kernels for 21% -> 22%
where the time goes in v4:
time: 22.1 us; the launch traced here: 22 us
  starting transfers between devices  8.84 us (40%)
  Pallas kernels  8.62 us (39%)
  waiting for transfers between devices  3.79 us (17%)
  between operations  0.73 us (3%)
    ppermute x4, starting transfers between devices, shards(): lax.ppermute(x, 'xs', [(i, i ^ m) for i in range(blocks)])  4.62 us
    ppermute x3, starting transfers between devices, shards(): got = [lax.ppermute(msg, 'ax', list(enumerate(r))) for r in routes]  4.22 us
    ppermute x4, waiting for transfers between devices, shards(): lax.ppermute(x, 'xs', [(i, i ^ m) for i in range(blocks)])  2.6 us
    pallas_call x1, Pallas kernels, shards(): pl.pallas_call(main_maps, out_shape=[table_shape, sign_shape, shape(vars_...  2.06 us
    pallas_call x1, Pallas kernels, shards(): pl.pallas_call(functools.partial(finish, count, sources), out_shape=[fiel...  1.6 us
    pallas_call x1, Pallas kernels, shards(): pl.pallas_call(functools.partial(pack_faces, blocks, cap, paired), out_sh...  1.49 us
    pallas_call x1, Pallas kernels, shards(): pl.pallas_call(fluxes, out_shape=field_shape, in_specs=[vmem] * 4, out_sp...  1.37 us
    ppermute x3, waiting for transfers between devices, shards(): got = [lax.ppermute(msg, 'ax', list(enumerate(r))) for r in routes]  1.19 us
  transfers between devices with their start and end apart: 7, of which 5 were waited for; matrix products, arithmetic and copies ran while one was open for 0% of the time, Pallas kernels for 22%

profile of v4, /device:TPU:0, one launch (start us, length us, event | category | flops | bytes accessed | tf_op | source)
XLA Modules:
  0.0 22.0 jit_solution(3232205193552835216)
XLA Ops:
  0.6 0.0 copy-start.1
  0.6 0.0 copy-start
  0.7 1.5 %pack_faces.1 = (f32[2,5,64,256]{3,2,1,0:T(8,128)S(1)}, s32[1,64]{1,0:T(1,128)S(1)}, f32[5,64,256]{2,1,0:T(8,128)S(1)}, f32[16,24,128]{2,1,0:T(8,128)S(1)}) custom-call(s32[16]{0:T(128)} %line_hbm.1, s32[16]{0:T(128)} %owner_hbm.1, f32[2,5,64,256]{3,2,1,0:T(8,128)} %bitcast.21, f32[5,16,256]{2,1,0:T(8,128)} %bitcast.23, s32[1,64]{1,0:T(1,128)} %bitcast.24, ...), custom_call_target="tpu_custom_call" | custom-call | tf_op jit(solution)/shard_map/pack_faces/pallas_call | solution.py:466
  2.2 3.0 %collective-permute-start = (f32[4,24,128]{2,1,0:T(8,128)S(1)}, f32[4,24,128]{2,1,0:T(8,128)S(1)}, u32[]{:S(2)}, u32[]{:S(2)}) collective-permute-start(f32[4,24,128]{2,1,0:T(8,128)S(1)} %get-tuple-element.38), channel_id=1, source_target_pairs={{0,2},{1,3},{2,0},{3,1},{4,6},{5,7},{6,4},{7,5},{8,10},{9,11},{10,... | collective-permute-start | bytes 147464 | tf_op jit(solution)/shard_map/ppermute | solution.py:487
  5.2 1.5 %collective-permute-start.1 = (f32[4,24,128]{2,1,0:T(8,128)S(1)}, f32[4,24,128]{2,1,0:T(8,128)S(1)}, u32[]{:S(2)}, u32[]{:S(2)}) collective-permute-start(f32[4,24,128]{2,1,0:T(8,128)S(1)} %get-tuple-element.39), channel_id=1, source_target_pairs={{0,6},{1,7},{2,4},{3,5},{4,2},{5,3},{6,0},{7,1},{8,14},{9,15},{10,... | collective-permute-start | bytes 147464 | tf_op jit(solution)/shard_map/ppermute | solution.py:487
  6.7 0.1 collective-permute-start.2
  6.7 0.0 copy-done.1
  6.7 0.0 copy-done
  6.7 2.1 %main_maps.1 = (f32[32,128]{1,0:T(8,128)S(1)}, f32[8,128]{1,0:T(8,128)S(1)}, f32[5,4,8,128]{3,2,1,0:T(8,128)S(1)}, f32[5,32,8,128]{3,2,1,0:T(8,128)S(1)}, f32[5,...) custom-call(f32[2,5,64,256]{3,2,1,0:T(8,128)S(1)} %get-tuple-element, ...), custom_call_target="tpu_custom_call" | custom-call | flops 2000000 | bytes 4000000 | tf_op jit(solution)/shard_map/main_maps/pallas_call | solution.py:490
  8.8 0.0 collective-permute-done.refs_1_
  8.8 1.4 %collective-permute-done.1.refs_2_ = f32[4,24,128]{2,1,0:T(8,128)S(1)} collective-permute-done((f32[4,24,128]{2,1,0:T(8,128)S(1)}, f32[4,24,128]{2,1,0:T(8,128)S(1)}, u32[]{:S(2)}, u32[]{:S(2)}) %collective-permute-start.1) | collective-permute-done | bytes 49184 | tf_op jit(solution)/shard_map/ppermute | solution.py:487
  10.2 0.6 %collective-permute-done.2.refs_3_ = f32[4,24,128]{2,1,0:T(8,128)S(1)} collective-permute-done((f32[4,24,128]{2,1,0:T(8,128)S(1)}, f32[4,24,128]{2,1,0:T(8,128)S(1)}, u32[]{:S(2)}, u32[]{:S(2)}) %collective-permute-start.2) | collective-permute-done | bytes 49184 | tf_op jit(solution)/shard_map/ppermute | solution.py:487
  10.8 0.1 collective-permute-start.3
  10.9 0.6 %lifts.1.lift_ref = f32[2,5,64,256]{3,2,1,0:T(8,128)S(1)} custom-call(f32[8,128]{1,0:T(8,128)S(1)} %get-tuple-element.32.after_ref.sign_ref.old_sign, f32[5,4,8,128]{3,2,1,0:T(8,128)S(1)} %get-tuple-element.33.ent_ref, f32[5,32,8,128]{3,2,1,0:T(8,128)S(1)} %get-tuple-element.34.c_s, f32[5,64,256]{2,1,0:T(8,128)S(1)} %get-tuple-element.35.scale_ref, ...), custom_call_target="tpu_custom_call" | custom-call | flops 1000000 | bytes 2000000 | tf_op jit(solution)/shard_map/lifts/pallas_call | solution.py:515
  11.5 0.6 %collective-permute-done.3.rest_1_ = f32[8,24,128]{2,1,0:T(8,128)S(1)} collective-permute-done((f32[8,24,128]{2,1,0:T(8,128)S(1)}, f32[8,24,128]{2,1,0:T(8,128)S(1)}, u32[]{:S(2)}, u32[]{:S(2)}) %collective-permute-start.3) | collective-permute-done | bytes 98336 | tf_op jit(solution)/shard_map/ppermute | solution.py:487
  12.1 0.6 %face_maps.1 = (f32[32,128]{1,0:T(8,128)S(1)}, f32[8,128]{1,0:T(8,128)S(1)}, f32[1,4,8,128]{3,2,1,0:T(8,128)S(1)}, f32[1,32,8,128]{3,2,1,0:T(8,128)S(1)}, f32[1,...) custom-call(f32[2,5,64,256]{3,2,1,0:T(8,128)S(1)} %lifts.1.lift_ref, f32[64,256]{1,0:T(8,128)S(1)} %get-tuple-element.31.in_ref, ...), custom_call_target="tpu_custom_call" | custom-call | tf_op jit(solution)/shard_map/face_maps/pallas_call | solution.py:525
  12.8 2.6 %collective-permute-start.6 = (f32[32,128]{1,0:T(8,128)S(1)}, f32[32,128]{1,0:T(8,128)S(1)}, u32[]{:S(2)}, u32[]{:S(2)}) collective-permute-start(f32[32,128]{1,0:T(8,128)S(1)} %get-tuple-element.51), channel_id=1, source_target_pairs={{0,16},{8,24},{16,8},{24,0},{1,17},{9,25},{17,9},{25,1},{2,18},{10... | collective-permute-start | bytes 49160 | tf_op jit(solution)/shard_map/ppermute | solution.py:540
  15.4 1.2 %collective-permute-start.5 = (f32[32,128]{1,0:T(8,128)S(1)}, f32[32,128]{1,0:T(8,128)S(1)}, u32[]{:S(2)}, u32[]{:S(2)}) collective-permute-start(f32[32,128]{1,0:T(8,128)S(1)} %get-tuple-element.51), channel_id=1, source_target_pairs={{0,24},{8,16},{16,0},{24,8},{1,25},{9,17},{17,1},{25,9},{2,26},{10... | collective-permute-start | bytes 49160 | tf_op jit(solution)/shard_map/ppermute | solution.py:540
  16.6 0.3 %collective-permute-start.4 = (f32[32,128]{1,0:T(8,128)S(1)}, f32[32,128]{1,0:T(8,128)S(1)}, u32[]{:S(2)}, u32[]{:S(2)}) collective-permute-start(f32[32,128]{1,0:T(8,128)S(1)} %get-tuple-element.51), channel_id=1, source_target_pairs={{0,8},{8,0},{16,24},{24,16},{1,9},{9,1},{17,25},{25,17},{2,10},{10... | collective-permute-start | bytes 49160 | tf_op jit(solution)/shard_map/ppermute | solution.py:540
  17.0 0.8 %substitute.1.after_ref.part_ref = f32[2,5,64,256]{3,2,1,0:T(8,128)S(1)} custom-call(f32[64,256]{1,0:T(8,128)S(1)} %get-tuple-element.31.in_ref, f32[2,5,64,256]{3,2,1,0:T(8,128)S(1)} %get-tuple-element.28.adj_ref, f32[8,128]{1,0:T(8,128)S(1)} %get-tuple-element.44.sign_ref, f32[5,4,8,128]{3,2,1,0:T(8,128)S(1)} %get-tuple-element.33.ent_ref, ...), custom_call_target="tpu_custom_call" | custom-call | flops 2000000 | bytes 3000000 | tf_op jit(solution)/shard_map/substitute/pallas_call | solution.py:541
  17.8 1.4 %fluxes.1.flux_ref = f32[2,5,64,256]{3,2,1,0:T(8,128)S(1)} custom-call(f32[2,5,64,256]{3,2,1,0:T(8,128)S(1)} %substitute.1.after_ref.part_ref, f32[64,256]{1,0:T(8,128)S(1)} %get-tuple-element.31.in_ref, f32[2,5,64,256]{3,2,1,0:T(8,128)S(1)} %get-tuple-element.28.adj_ref, f32[5,64,256]{2,1,0:T(8,128)S(1)} %bitcast.18), custom_call_target="tpu_custom_call" | custom-call | flops 1000000 | bytes 2000000 | tf_op jit(solution)/shard_map/fluxes/pallas_call | solution.py:551
  19.2 0.0 collective-permute-done.6.rest_2_
  19.2 0.9 %collective-permute-done.5.rest_1_ = f32[32,128]{1,0:T(8,128)S(1)} collective-permute-done((f32[32,128]{1,0:T(8,128)S(1)}, f32[32,128]{1,0:T(8,128)S(1)}, u32[]{:S(2)}, u32[]{:S(2)}) %collective-permute-start.5) | collective-permute-done | bytes 16416 | tf_op jit(solution)/shard_map/ppermute | solution.py:540
  20.1 0.2 %collective-permute-done.4.rest_0_ = f32[32,128]{1,0:T(8,128)S(1)} collective-permute-done((f32[32,128]{1,0:T(8,128)S(1)}, f32[32,128]{1,0:T(8,128)S(1)}, u32[]{:S(2)}, u32[]{:S(2)}) %collective-permute-start.4) | collective-permute-done | bytes 16416 | tf_op jit(solution)/shard_map/ppermute | solution.py:540
  20.4 1.6 %finish.1 = (f32[2,5,64,256]{3,2,1,0:T(8,128)}, f32[2,5,64,256]{3,2,1,0:T(8,128)}) custom-call(f32[64,256]{1,0:T(8,128)S(1)} %get-tuple-element.31.in_ref, f32[8,128]{1,0:T(8,128)S(1)} %get-tuple-element.44.sign_ref, f32[2,5,64,256]{3,2,1,0:T(8,128)S(1)} %substitute.1.after_ref.part_ref, f32[2,5,64,256]{3,2,1,0:T(8,128)S(1)} %lifts.1.lift_ref, ...), custom_call_target="tpu_custom_call" | custom-call | tf_op jit(solution)/shard_map/finish/pallas_call | solution.py:560
  (2 shorter events, 0.0 us)
Async XLA Ops:
  0.6 6.1 %copy-start.1 = (f32[64,10,256]{2,0,1:T(8,128)S(1)}, f32[64,10,256]{2,0,1:T(8,128)}, u32[]{:S(2)}) copy-start(f32[64,10,256]{2,0,1:T(8,128)} %param.9) | copy-start | bytes 1966084
  0.6 6.1 %copy-start = (f32[64,5,256]{2,0,1:T(8,128)S(1)}, f32[64,5,256]{2,0,1:T(8,128)}, u32[]{:S(2)}) copy-start(f32[64,5,256]{2,0,1:T(8,128)} %param.10) | copy-start | bytes 983044
  2.2 6.6 %collective-permute-start = (f32[4,24,128]{2,1,0:T(8,128)S(1)}, f32[4,24,128]{2,1,0:T(8,128)S(1)}, u32[]{:S(2)}, u32[]{:S(2)}) collective-permute-start(f32[4,24,128]{2,1,0:T(8,128)S(1)} %get-tuple-element.38), channel_id=1, source_target_pairs={{0,2},{1,3},{2,0},{3,1},{4,6},{5,7},{6,4},{7,5},{8,10},{9,11},{10,... | collective-permute-start | bytes 147464 | tf_op jit(solution)/shard_map/ppermute | solution.py:487
  5.2 5.0 %collective-permute-start.1 = (f32[4,24,128]{2,1,0:T(8,128)S(1)}, f32[4,24,128]{2,1,0:T(8,128)S(1)}, u32[]{:S(2)}, u32[]{:S(2)}) collective-permute-start(f32[4,24,128]{2,1,0:T(8,128)S(1)} %get-tuple-element.39), channel_id=1, source_target_pairs={{0,6},{1,7},{2,4},{3,5},{4,2},{5,3},{6,0},{7,1},{8,14},{9,15},{10,... | collective-permute-start | bytes 147464 | tf_op jit(solution)/shard_map/ppermute | solution.py:487
  6.7 4.1 %collective-permute-start.2 = (f32[4,24,128]{2,1,0:T(8,128)S(1)}, f32[4,24,128]{2,1,0:T(8,128)S(1)}, u32[]{:S(2)}, u32[]{:S(2)}) collective-permute-start(f32[4,24,128]{2,1,0:T(8,128)S(1)} %get-tuple-element.40), channel_id=1, source_target_pairs={{0,4},{1,5},{2,6},{3,7},{4,0},{5,1},{6,2},{7,3},{8,12},{9,13},{10,... | collective-permute-start | bytes 147464 | tf_op jit(solution)/shard_map/ppermute | solution.py:487
  10.8 1.4 %collective-permute-start.3 = (f32[8,24,128]{2,1,0:T(8,128)S(1)}, f32[8,24,128]{2,1,0:T(8,128)S(1)}, u32[]{:S(2)}, u32[]{:S(2)}) collective-permute-start(f32[8,24,128]{2,1,0:T(8,128)S(1)} %get-tuple-element.43), channel_id=1, source_target_pairs={{0,1},{1,0},{2,3},{3,2},{4,5},{5,4},{6,7},{7,6},{8,9},{9,8},{10,11... | collective-permute-start | bytes 294920 | tf_op jit(solution)/shard_map/ppermute | solution.py:487
  12.8 6.4 %collective-permute-start.6 = (f32[32,128]{1,0:T(8,128)S(1)}, f32[32,128]{1,0:T(8,128)S(1)}, u32[]{:S(2)}, u32[]{:S(2)}) collective-permute-start(f32[32,128]{1,0:T(8,128)S(1)} %get-tuple-element.51), channel_id=1, source_target_pairs={{0,16},{8,24},{16,8},{24,0},{1,17},{9,25},{17,9},{25,1},{2,18},{10... | collective-permute-start | bytes 49160 | tf_op jit(solution)/shard_map/ppermute | solution.py:540
  15.4 4.7 %collective-permute-start.5 = (f32[32,128]{1,0:T(8,128)S(1)}, f32[32,128]{1,0:T(8,128)S(1)}, u32[]{:S(2)}, u32[]{:S(2)}) collective-permute-start(f32[32,128]{1,0:T(8,128)S(1)} %get-tuple-element.51), channel_id=1, source_target_pairs={{0,24},{8,16},{16,0},{24,8},{1,25},{9,17},{17,1},{25,9},{2,26},{10... | collective-permute-start | bytes 49160 | tf_op jit(solution)/shard_map/ppermute | solution.py:540
  16.6 3.7 %collective-permute-start.4 = (f32[32,128]{1,0:T(8,128)S(1)}, f32[32,128]{1,0:T(8,128)S(1)}, u32[]{:S(2)}, u32[]{:S(2)}) collective-permute-start(f32[32,128]{1,0:T(8,128)S(1)} %get-tuple-element.51), channel_id=1, source_target_pairs={{0,8},{8,0},{16,24},{24,16},{1,9},{9,1},{17,25},{25,17},{2,10},{10... | collective-permute-start | bytes 49160 | tf_op jit(solution)/shard_map/ppermute | solution.py:540

commit v5 on v4

--- a/solution.py
+++ b/solution.py
@@ -94,7 +94,7 @@
 
 def coefficients(v, iv, a_re, a_im, inside):
     s = jnp.where(inside, jnp.abs(v), 0.0)
-    rd = 1.0 / (iv + 1.5 * s)
+    rd = 1.0 / jnp.where(inside, iv + 1.5 * s, 1.0)
     c = s * rd
     g_re, g_im = s * a_re, s * a_im
     scale = jnp.where(inside, relaxation * rd, 0.0)

time: 22.1 us -> 22.1 us (level)
  no operation moved by 1% of the time
where the time goes in v5:
time: 22.1 us; the launch traced here: 22 us
  starting transfers between devices  8.84 us (40%)
  Pallas kernels  8.62 us (39%)
  waiting for transfers between devices  3.78 us (17%)
  between operations  0.73 us (3%)
    ppermute x4, starting transfers between devices, shards(): lax.ppermute(x, 'xs', [(i, i ^ m) for i in range(blocks)])  4.62 us
    ppermute x3, starting transfers between devices, shards(): got = [lax.ppermute(msg, 'ax', list(enumerate(r))) for r in routes]  4.22 us
    ppermute x4, waiting for transfers between devices, shards(): lax.ppermute(x, 'xs', [(i, i ^ m) for i in range(blocks)])  2.59 us
    pallas_call x1, Pallas kernels, shards(): pl.pallas_call(main_maps, out_shape=[table_shape, sign_shape, shape(vars_...  2.06 us
    pallas_call x1, Pallas kernels, shards(): pl.pallas_call(functools.partial(finish, count, sources), out_shape=[fiel...  1.6 us
    pallas_call x1, Pallas kernels, shards(): pl.pallas_call(functools.partial(pack_faces, blocks, cap, paired), out_sh...  1.49 us
    pallas_call x1, Pallas kernels, shards(): pl.pallas_call(fluxes, out_shape=field_shape, in_specs=[vmem] * 4, out_sp...  1.37 us
    ppermute x3, waiting for transfers between devices, shards(): got = [lax.ppermute(msg, 'ax', list(enumerate(r))) for r in routes]  1.19 us
  transfers between devices with their start and end apart: 7, of which 5 were waited for; matrix products, arithmetic and copies ran while one was open for 0% of the time, Pallas kernels for 22%

profile of v5, /device:TPU:0, one launch (start us, length us, event | category | flops | bytes accessed | tf_op | source)
XLA Modules:
  0.0 22.0 jit_solution(10364918114172363468)
XLA Ops:
  0.6 0.0 copy-start.1
  0.6 0.0 copy-start
  0.7 1.5 %pack_faces.1 = (f32[2,5,64,256]{3,2,1,0:T(8,128)S(1)}, s32[1,64]{1,0:T(1,128)S(1)}, f32[5,64,256]{2,1,0:T(8,128)S(1)}, f32[16,24,128]{2,1,0:T(8,128)S(1)}) custom-call(s32[16]{0:T(128)} %line_hbm.1, s32[16]{0:T(128)} %owner_hbm.1, f32[2,5,64,256]{3,2,1,0:T(8,128)} %bitcast.21, f32[5,16,256]{2,1,0:T(8,128)} %bitcast.23, s32[1,64]{1,0:T(1,128)} %bitcast.24, ...), custom_call_target="tpu_custom_call" | custom-call | tf_op jit(solution)/shard_map/pack_faces/pallas_call | solution.py:466
  2.2 3.0 %collective-permute-start = (f32[4,24,128]{2,1,0:T(8,128)S(1)}, f32[4,24,128]{2,1,0:T(8,128)S(1)}, u32[]{:S(2)}, u32[]{:S(2)}) collective-permute-start(f32[4,24,128]{2,1,0:T(8,128)S(1)} %get-tuple-element.38), channel_id=1, source_target_pairs={{0,2},{1,3},{2,0},{3,1},{4,6},{5,7},{6,4},{7,5},{8,10},{9,11},{10,... | collective-permute-start | bytes 147464 | tf_op jit(solution)/shard_map/ppermute | solution.py:487
  5.2 1.5 %collective-permute-start.1 = (f32[4,24,128]{2,1,0:T(8,128)S(1)}, f32[4,24,128]{2,1,0:T(8,128)S(1)}, u32[]{:S(2)}, u32[]{:S(2)}) collective-permute-start(f32[4,24,128]{2,1,0:T(8,128)S(1)} %get-tuple-element.39), channel_id=1, source_target_pairs={{0,6},{1,7},{2,4},{3,5},{4,2},{5,3},{6,0},{7,1},{8,14},{9,15},{10,... | collective-permute-start | bytes 147464 | tf_op jit(solution)/shard_map/ppermute | solution.py:487
  6.7 0.1 collective-permute-start.2
  6.7 0.0 copy-done.1
  6.7 0.0 copy-done
  6.7 2.1 %main_maps.1 = (f32[32,128]{1,0:T(8,128)S(1)}, f32[8,128]{1,0:T(8,128)S(1)}, f32[5,4,8,128]{3,2,1,0:T(8,128)S(1)}, f32[5,32,8,128]{3,2,1,0:T(8,128)S(1)}, f32[5,...) custom-call(f32[2,5,64,256]{3,2,1,0:T(8,128)S(1)} %get-tuple-element, ...), custom_call_target="tpu_custom_call" | custom-call | flops 2000000 | bytes 4000000 | tf_op jit(solution)/shard_map/main_maps/pallas_call | solution.py:490
  8.8 0.0 collective-permute-done.refs_1_
  8.8 1.4 %collective-permute-done.1.refs_2_ = f32[4,24,128]{2,1,0:T(8,128)S(1)} collective-permute-done((f32[4,24,128]{2,1,0:T(8,128)S(1)}, f32[4,24,128]{2,1,0:T(8,128)S(1)}, u32[]{:S(2)}, u32[]{:S(2)}) %collective-permute-start.1) | collective-permute-done | bytes 49184 | tf_op jit(solution)/shard_map/ppermute | solution.py:487
  10.2 0.6 %collective-permute-done.2.refs_3_ = f32[4,24,128]{2,1,0:T(8,128)S(1)} collective-permute-done((f32[4,24,128]{2,1,0:T(8,128)S(1)}, f32[4,24,128]{2,1,0:T(8,128)S(1)}, u32[]{:S(2)}, u32[]{:S(2)}) %collective-permute-start.2) | collective-permute-done | bytes 49184 | tf_op jit(solution)/shard_map/ppermute | solution.py:487
  10.8 0.1 collective-permute-start.3
  10.9 0.6 %lifts.1.lift_ref = f32[2,5,64,256]{3,2,1,0:T(8,128)S(1)} custom-call(f32[8,128]{1,0:T(8,128)S(1)} %get-tuple-element.32.after_ref.sign_ref.old_sign, f32[5,4,8,128]{3,2,1,0:T(8,128)S(1)} %get-tuple-element.33.ent_ref, f32[5,32,8,128]{3,2,1,0:T(8,128)S(1)} %get-tuple-element.34.c_s, f32[5,64,256]{2,1,0:T(8,128)S(1)} %get-tuple-element.35.scale_ref, ...), custom_call_target="tpu_custom_call" | custom-call | flops 1000000 | bytes 2000000 | tf_op jit(solution)/shard_map/lifts/pallas_call | solution.py:515
  11.5 0.6 %collective-permute-done.3.rest_1_ = f32[8,24,128]{2,1,0:T(8,128)S(1)} collective-permute-done((f32[8,24,128]{2,1,0:T(8,128)S(1)}, f32[8,24,128]{2,1,0:T(8,128)S(1)}, u32[]{:S(2)}, u32[]{:S(2)}) %collective-permute-start.3) | collective-permute-done | bytes 98336 | tf_op jit(solution)/shard_map/ppermute | solution.py:487
  12.1 0.6 %face_maps.1 = (f32[32,128]{1,0:T(8,128)S(1)}, f32[8,128]{1,0:T(8,128)S(1)}, f32[1,4,8,128]{3,2,1,0:T(8,128)S(1)}, f32[1,32,8,128]{3,2,1,0:T(8,128)S(1)}, f32[1,...) custom-call(f32[2,5,64,256]{3,2,1,0:T(8,128)S(1)} %lifts.1.lift_ref, f32[64,256]{1,0:T(8,128)S(1)} %get-tuple-element.31.in_ref, ...), custom_call_target="tpu_custom_call" | custom-call | tf_op jit(solution)/shard_map/face_maps/pallas_call | solution.py:525
  12.8 2.6 %collective-permute-start.6 = (f32[32,128]{1,0:T(8,128)S(1)}, f32[32,128]{1,0:T(8,128)S(1)}, u32[]{:S(2)}, u32[]{:S(2)}) collective-permute-start(f32[32,128]{1,0:T(8,128)S(1)} %get-tuple-element.51), channel_id=1, source_target_pairs={{0,16},{8,24},{16,8},{24,0},{1,17},{9,25},{17,9},{25,1},{2,18},{10... | collective-permute-start | bytes 49160 | tf_op jit(solution)/shard_map/ppermute | solution.py:540
  15.4 1.2 %collective-permute-start.5 = (f32[32,128]{1,0:T(8,128)S(1)}, f32[32,128]{1,0:T(8,128)S(1)}, u32[]{:S(2)}, u32[]{:S(2)}) collective-permute-start(f32[32,128]{1,0:T(8,128)S(1)} %get-tuple-element.51), channel_id=1, source_target_pairs={{0,24},{8,16},{16,0},{24,8},{1,25},{9,17},{17,1},{25,9},{2,26},{10... | collective-permute-start | bytes 49160 | tf_op jit(solution)/shard_map/ppermute | solution.py:540
  16.6 0.3 %collective-permute-start.4 = (f32[32,128]{1,0:T(8,128)S(1)}, f32[32,128]{1,0:T(8,128)S(1)}, u32[]{:S(2)}, u32[]{:S(2)}) collective-permute-start(f32[32,128]{1,0:T(8,128)S(1)} %get-tuple-element.51), channel_id=1, source_target_pairs={{0,8},{8,0},{16,24},{24,16},{1,9},{9,1},{17,25},{25,17},{2,10},{10... | collective-permute-start | bytes 49160 | tf_op jit(solution)/shard_map/ppermute | solution.py:540
  17.0 0.8 %substitute.1.after_ref.part_ref = f32[2,5,64,256]{3,2,1,0:T(8,128)S(1)} custom-call(f32[64,256]{1,0:T(8,128)S(1)} %get-tuple-element.31.in_ref, f32[2,5,64,256]{3,2,1,0:T(8,128)S(1)} %get-tuple-element.28.adj_ref, f32[8,128]{1,0:T(8,128)S(1)} %get-tuple-element.44.sign_ref, f32[5,4,8,128]{3,2,1,0:T(8,128)S(1)} %get-tuple-element.33.ent_ref, ...), custom_call_target="tpu_custom_call" | custom-call | flops 2000000 | bytes 3000000 | tf_op jit(solution)/shard_map/substitute/pallas_call | solution.py:541
  17.8 1.4 %fluxes.1.flux_ref = f32[2,5,64,256]{3,2,1,0:T(8,128)S(1)} custom-call(f32[2,5,64,256]{3,2,1,0:T(8,128)S(1)} %substitute.1.after_ref.part_ref, f32[64,256]{1,0:T(8,128)S(1)} %get-tuple-element.31.in_ref, f32[2,5,64,256]{3,2,1,0:T(8,128)S(1)} %get-tuple-element.28.adj_ref, f32[5,64,256]{2,1,0:T(8,128)S(1)} %bitcast.18), custom_call_target="tpu_custom_call" | custom-call | flops 1000000 | bytes 2000000 | tf_op jit(solution)/shard_map/fluxes/pallas_call | solution.py:551
  19.2 0.0 collective-permute-done.6.rest_2_
  19.2 0.9 %collective-permute-done.5.rest_1_ = f32[32,128]{1,0:T(8,128)S(1)} collective-permute-done((f32[32,128]{1,0:T(8,128)S(1)}, f32[32,128]{1,0:T(8,128)S(1)}, u32[]{:S(2)}, u32[]{:S(2)}) %collective-permute-start.5) | collective-permute-done | bytes 16416 | tf_op jit(solution)/shard_map/ppermute | solution.py:540
  20.1 0.2 %collective-permute-done.4.rest_0_ = f32[32,128]{1,0:T(8,128)S(1)} collective-permute-done((f32[32,128]{1,0:T(8,128)S(1)}, f32[32,128]{1,0:T(8,128)S(1)}, u32[]{:S(2)}, u32[]{:S(2)}) %collective-permute-start.4) | collective-permute-done | bytes 16416 | tf_op jit(solution)/shard_map/ppermute | solution.py:540
  20.4 1.6 %finish.1 = (f32[2,5,64,256]{3,2,1,0:T(8,128)}, f32[2,5,64,256]{3,2,1,0:T(8,128)}) custom-call(f32[64,256]{1,0:T(8,128)S(1)} %get-tuple-element.31.in_ref, f32[8,128]{1,0:T(8,128)S(1)} %get-tuple-element.44.sign_ref, f32[2,5,64,256]{3,2,1,0:T(8,128)S(1)} %substitute.1.after_ref.part_ref, f32[2,5,64,256]{3,2,1,0:T(8,128)S(1)} %lifts.1.lift_ref, ...), custom_call_target="tpu_custom_call" | custom-call | tf_op jit(solution)/shard_map/finish/pallas_call | solution.py:560
  (2 shorter events, 0.0 us)
Async XLA Ops:
  0.6 6.1 %copy-start.1 = (f32[64,10,256]{2,0,1:T(8,128)S(1)}, f32[64,10,256]{2,0,1:T(8,128)}, u32[]{:S(2)}) copy-start(f32[64,10,256]{2,0,1:T(8,128)} %param.9) | copy-start | bytes 1966084
  0.6 6.1 %copy-start = (f32[64,5,256]{2,0,1:T(8,128)S(1)}, f32[64,5,256]{2,0,1:T(8,128)}, u32[]{:S(2)}) copy-start(f32[64,5,256]{2,0,1:T(8,128)} %param.10) | copy-start | bytes 983044
  2.2 6.6 %collective-permute-start = (f32[4,24,128]{2,1,0:T(8,128)S(1)}, f32[4,24,128]{2,1,0:T(8,128)S(1)}, u32[]{:S(2)}, u32[]{:S(2)}) collective-permute-start(f32[4,24,128]{2,1,0:T(8,128)S(1)} %get-tuple-element.38), channel_id=1, source_target_pairs={{0,2},{1,3},{2,0},{3,1},{4,6},{5,7},{6,4},{7,5},{8,10},{9,11},{10,... | collective-permute-start | bytes 147464 | tf_op jit(solution)/shard_map/ppermute | solution.py:487
  5.2 5.0 %collective-permute-start.1 = (f32[4,24,128]{2,1,0:T(8,128)S(1)}, f32[4,24,128]{2,1,0:T(8,128)S(1)}, u32[]{:S(2)}, u32[]{:S(2)}) collective-permute-start(f32[4,24,128]{2,1,0:T(8,128)S(1)} %get-tuple-element.39), channel_id=1, source_target_pairs={{0,6},{1,7},{2,4},{3,5},{4,2},{5,3},{6,0},{7,1},{8,14},{9,15},{10,... | collective-permute-start | bytes 147464 | tf_op jit(solution)/shard_map/ppermute | solution.py:487
  6.7 4.1 %collective-permute-start.2 = (f32[4,24,128]{2,1,0:T(8,128)S(1)}, f32[4,24,128]{2,1,0:T(8,128)S(1)}, u32[]{:S(2)}, u32[]{:S(2)}) collective-permute-start(f32[4,24,128]{2,1,0:T(8,128)S(1)} %get-tuple-element.40), channel_id=1, source_target_pairs={{0,4},{1,5},{2,6},{3,7},{4,0},{5,1},{6,2},{7,3},{8,12},{9,13},{10,... | collective-permute-start | bytes 147464 | tf_op jit(solution)/shard_map/ppermute | solution.py:487
  10.8 1.4 %collective-permute-start.3 = (f32[8,24,128]{2,1,0:T(8,128)S(1)}, f32[8,24,128]{2,1,0:T(8,128)S(1)}, u32[]{:S(2)}, u32[]{:S(2)}) collective-permute-start(f32[8,24,128]{2,1,0:T(8,128)S(1)} %get-tuple-element.43), channel_id=1, source_target_pairs={{0,1},{1,0},{2,3},{3,2},{4,5},{5,4},{6,7},{7,6},{8,9},{9,8},{10,11... | collective-permute-start | bytes 294920 | tf_op jit(solution)/shard_map/ppermute | solution.py:487
  12.8 6.4 %collective-permute-start.6 = (f32[32,128]{1,0:T(8,128)S(1)}, f32[32,128]{1,0:T(8,128)S(1)}, u32[]{:S(2)}, u32[]{:S(2)}) collective-permute-start(f32[32,128]{1,0:T(8,128)S(1)} %get-tuple-element.51), channel_id=1, source_target_pairs={{0,16},{8,24},{16,8},{24,0},{1,17},{9,25},{17,9},{25,1},{2,18},{10... | collective-permute-start | bytes 49160 | tf_op jit(solution)/shard_map/ppermute | solution.py:540
  15.4 4.7 %collective-permute-start.5 = (f32[32,128]{1,0:T(8,128)S(1)}, f32[32,128]{1,0:T(8,128)S(1)}, u32[]{:S(2)}, u32[]{:S(2)}) collective-permute-start(f32[32,128]{1,0:T(8,128)S(1)} %get-tuple-element.51), channel_id=1, source_target_pairs={{0,24},{8,16},{16,0},{24,8},{1,25},{9,17},{17,1},{25,9},{2,26},{10... | collective-permute-start | bytes 49160 | tf_op jit(solution)/shard_map/ppermute | solution.py:540
  16.6 3.7 %collective-permute-start.4 = (f32[32,128]{1,0:T(8,128)S(1)}, f32[32,128]{1,0:T(8,128)S(1)}, u32[]{:S(2)}, u32[]{:S(2)}) collective-permute-start(f32[32,128]{1,0:T(8,128)S(1)} %get-tuple-element.51), channel_id=1, source_target_pairs={{0,8},{8,0},{16,24},{24,16},{1,9},{9,1},{17,25},{25,17},{2,10},{10... | collective-permute-start | bytes 49160 | tf_op jit(solution)/shard_map/ppermute | solution.py:540

commit v6 on v5

--- a/solution.py
+++ b/solution.py
@@ -224,7 +224,7 @@
 
 
 def face_maps(
-    counts, lift_ref, in_ref, adj_ref, src_ref, speed_ref, inv_ref, old_msg, old_sign, *rest
+    counts, after_ref, in_ref, adj_ref, src_ref, speed_ref, inv_ref, old_msg, old_sign, *rest
 ):
     recv = rest[: len(counts)]
     msg_ref, sign_ref, ent_ref, c_s, b_s, h_ref, c_t, b_t = rest[len(counts) :]
@@ -334,11 +334,12 @@
             part_ref[part, k] = jnp.where(inside, adj_ref[part, k], 0.0) + (h + us) * scale
 
 
-def fluxes(after_ref, in_ref, adj_ref, speed_ref, flux_ref):
+def fluxes(begin, after_ref, in_ref, adj_ref, speed_ref, flux_ref):
     vars_, lines, cells = speed_ref.shape
     half = cells // 2
     lane = lax.broadcasted_iota(jnp.int32, (lines, half), 1)
-    for k in range(vars_):
+    for i in range(flux_ref.shape[1]):
+        k = begin + i
         v = speed_ref[k]
         s = jnp.abs(v) * in_ref[...]
         up = v[:, :half] > 0.0
@@ -356,11 +357,11 @@
             low, high = g[:, :half], g[:, half:]
             near = shifted(low, high)
             low, high = shifted(2.0 * low - 0.5 * near[0], 2.0 * high - 0.5 * near[1])
-            flux_ref[part, k, :, :half] = low * in_ref[:, :half]
-            flux_ref[part, k, :, half:] = high * in_ref[:, half:]
-
-
-def finish(count, sources, in_ref, sign_ref, part_ref, lift_ref, h_ref, h_f, flux_ref, *rest):
+            flux_ref[part, i, :, :half] = low * in_ref[:, :half]
+            flux_ref[part, i, :, half:] = high * in_ref[:, half:]
+
+
+def finish(count, sources, in_ref, sign_ref, part_ref, lift_ref, h_ref, h_f, early_ref, late_ref, *rest):
     got = rest[: count - 1]
     new_hbm, out_hbm, new_ref, out_ref, sems = rest[count - 1 :]
     _, vars_, lines, cells = part_ref.shape
@@ -418,7 +419,8 @@
 
             edge = edges[rows]
             h = jnp.concatenate([h_f[at : at + FACE_DEV], h_ref[part, k, FACE_DEV:]], axis=0)
-            h = h + flux_ref[part, k]
+            split = early_ref.shape[1]
+            h = h + (early_ref[part, k] if k < split else late_ref[part, k - split])
             out_ref[part, k, :, :half] = h[:, :half] + jnp.where(left, edge, 0.0) * in_ref[:, :half]
             out_ref[part, k, :, half:] = h[:, half:] + jnp.where(left, 0.0, edge) * in_ref[:, half:]
             new_ref[part, k] = part_ref[part, k] + (
@@ -522,6 +524,17 @@
         cost_estimate=cost(10**6, 2 * 10**6),
         name="lifts",
     )(sign, ent, c_s, scale, after)
+    flux = lambda begin, number, when: pl.pallas_call(
+        functools.partial(fluxes, begin),
+        out_shape=shape(2, number, lines, cells),
+        in_specs=[vmem] * 4,
+        out_specs=vmem,
+        compiler_params=limit(6),
+        cost_estimate=cost(10**6, 2 * 10**6),
+        name="fluxes",
+    )(when, mask, adj, spd)
+    early_vars = vars_ * 2 // 5
+    early = flux(0, early_vars, lift)
     msg, sign, ent_f, c_f, b_f, h_f = pl.pallas_call(
         functools.partial(face_maps, counts),
         out_shape=[table_shape, sign_shape, shape(1, 4, SEGS, width), face_order, face_order,
@@ -531,7 +544,7 @@
         scratch_shapes=[scratch(1, cells, width)] * 2,
         compiler_params=limit(10),
         name="face_maps",
-    )(lift, mask, adj, src, spd, inv, msg, sign, *recv)
+    )(early, mask, adj, src, spd, inv, msg, sign, *recv)
     if count == 4:
         routes = [(1, 0, 3, 2), (3, 2, 0, 1), (2, 3, 1, 0)]
     else:
@@ -548,24 +561,16 @@
         cost_estimate=cost(2 * 10**6, 3 * 10**6),
         name="substitute",
     )(mask, adj, sign, ent, c_s, b_s, h, scale, ent_f, c_f, b_f, h_f)
-    flux = pl.pallas_call(
-        fluxes,
-        out_shape=field_shape,
-        in_specs=[vmem] * 4,
-        out_specs=vmem,
-        compiler_params=limit(6),
-        cost_estimate=cost(10**6, 2 * 10**6),
-        name="fluxes",
-    )(part, mask, adj, spd)
+    late = flux(early_vars, vars_ - early_vars, part)
     new, out = pl.pallas_call(
         functools.partial(finish, count, sources),
         out_shape=[field_shape] * 2,
-        in_specs=[vmem] * (7 + len(got)),
+        in_specs=[vmem] * (8 + len(got)),
         out_specs=[hbm] * 2,
         scratch_shapes=[scratch(2, vars_, lines, cells)] * 2 + [dma(4 * vars_)],
         compiler_params=limit(10),
         name="finish",
-    )(mask, sign, part, lift, h, h_f, flux, *got)
+    )(mask, sign, part, lift, h, h_f, early, late, *got)
     back = lambda x: jnp.transpose(x.reshape(rows, lines, cells), (1, 0, 2))
     return (back(new), back(out))
 

time: 22.1 us -> 22.1 us (level)
    ppermute x4, waiting for transfers between devices: 2.59 us -> 2 us  [shards(): lax.ppermute(x, 'xs', [(i, i ^ m) for i in range(blocks)])]
    ppermute x3, waiting for transfers between devices: 1.19 us -> 1.71 us  [shards(): got = [lax.ppermute(msg, 'ax', list(enumerate(r))) for r in routes]]
    pallas_call x1 -> x2, Pallas kernels: 1.37 us -> 1.43 us  [shards(): pl.pallas_call(functools.partial(fluxes, begin), out_shape=shape(2, numbe...]
  transfers between devices with their start and end apart: 7 -> 7, of which waited for: 5 -> 4; matrix products, arithmetic and copies ran while one was open for 0% -> 0% of each run, Pallas kernels for 22% -> 23%
where the time goes in v6:
time: 22.1 us; the launch traced here: 22 us
  starting transfers between devices  8.84 us (40%)
  Pallas kernels  8.68 us (39%)
  waiting for transfers between devices  3.71 us (17%)
  between operations  0.74 us (3%)
    ppermute x4, starting transfers between devices, shards(): lax.ppermute(x, 'xs', [(i, i ^ m) for i in range(blocks)])  4.62 us
    ppermute x3, starting transfers between devices, shards(): got = [lax.ppermute(msg, 'ax', list(enumerate(r))) for r in routes]  4.22 us
    pallas_call x1, Pallas kernels, shards(): pl.pallas_call(main_maps, out_shape=[table_shape, sign_shape, shape(vars_...  2.06 us
    ppermute x4, waiting for transfers between devices, shards(): lax.ppermute(x, 'xs', [(i, i ^ m) for i in range(blocks)])  2 us
    ppermute x3, waiting for transfers between devices, shards(): got = [lax.ppermute(msg, 'ax', list(enumerate(r))) for r in routes]  1.71 us
    pallas_call x1, Pallas kernels, shards(): pl.pallas_call(functools.partial(finish, count, sources), out_shape=[fiel...  1.6 us
    pallas_call x1, Pallas kernels, shards(): pl.pallas_call(functools.partial(pack_faces, blocks, cap, paired), out_sh...  1.49 us
    pallas_call x2, Pallas kernels, shards(): pl.pallas_call(functools.partial(fluxes, begin), out_shape=shape(2, numbe...  1.43 us
  transfers between devices with their start and end apart: 7, of which 4 were waited for; matrix products, arithmetic and copies ran while one was open for 0% of the time, Pallas kernels for 23%

profile of v6, /device:TPU:0, one launch (start us, length us, event | category | flops | bytes accessed | tf_op | source)
XLA Modules:
  0.0 22.0 jit_solution(13235708411552705891)
XLA Ops:
  0.6 0.0 copy-start.1
  0.6 0.0 copy-start
  0.7 1.5 %pack_faces.1 = (f32[2,5,64,256]{3,2,1,0:T(8,128)S(1)}, s32[1,64]{1,0:T(1,128)S(1)}, f32[5,64,256]{2,1,0:T(8,128)S(1)}, f32[16,24,128]{2,1,0:T(8,128)S(1)}) custom-call(s32[16]{0:T(128)} %line_hbm.1, s32[16]{0:T(128)} %owner_hbm.1, f32[2,5,64,256]{3,2,1,0:T(8,128)} %bitcast.22, f32[5,16,256]{2,1,0:T(8,128)} %bitcast.24, s32[1,64]{1,0:T(1,128)} %bitcast.25, ...), custom_call_target="tpu_custom_call" | custom-call | tf_op jit(solution)/shard_map/pack_faces/pallas_call | solution.py:468
  2.2 3.0 %collective-permute-start = (f32[4,24,128]{2,1,0:T(8,128)S(1)}, f32[4,24,128]{2,1,0:T(8,128)S(1)}, u32[]{:S(2)}, u32[]{:S(2)}) collective-permute-start(f32[4,24,128]{2,1,0:T(8,128)S(1)} %get-tuple-element.38), channel_id=1, source_target_pairs={{0,2},{1,3},{2,0},{3,1},{4,6},{5,7},{6,4},{7,5},{8,10},{9,11},{10,... | collective-permute-start | bytes 147464 | tf_op jit(solution)/shard_map/ppermute | solution.py:489
  5.2 1.5 %collective-permute-start.1 = (f32[4,24,128]{2,1,0:T(8,128)S(1)}, f32[4,24,128]{2,1,0:T(8,128)S(1)}, u32[]{:S(2)}, u32[]{:S(2)}) collective-permute-start(f32[4,24,128]{2,1,0:T(8,128)S(1)} %get-tuple-element.39), channel_id=1, source_target_pairs={{0,6},{1,7},{2,4},{3,5},{4,2},{5,3},{6,0},{7,1},{8,14},{9,15},{10,... | collective-permute-start | bytes 147464 | tf_op jit(solution)/shard_map/ppermute | solution.py:489
  6.7 0.1 collective-permute-start.2
  6.7 0.0 copy-done.1
  6.7 0.0 copy-done
  6.7 2.1 %main_maps.1 = (f32[32,128]{1,0:T(8,128)S(1)}, f32[8,128]{1,0:T(8,128)S(1)}, f32[5,4,8,128]{3,2,1,0:T(8,128)S(1)}, f32[5,32,8,128]{3,2,1,0:T(8,128)S(1)}, f32[5,...) custom-call(f32[2,5,64,256]{3,2,1,0:T(8,128)S(1)} %get-tuple-element, ...), custom_call_target="tpu_custom_call" | custom-call | flops 2000000 | bytes 4000000 | tf_op jit(solution)/shard_map/main_maps/pallas_call | solution.py:492
  8.8 0.0 collective-permute-done.refs_1_
  8.8 1.4 %collective-permute-done.1.refs_2_ = f32[4,24,128]{2,1,0:T(8,128)S(1)} collective-permute-done((f32[4,24,128]{2,1,0:T(8,128)S(1)}, f32[4,24,128]{2,1,0:T(8,128)S(1)}, u32[]{:S(2)}, u32[]{:S(2)}) %collective-permute-start.1) | collective-permute-done | bytes 49184 | tf_op jit(solution)/shard_map/ppermute | solution.py:489
  10.2 0.6 %collective-permute-done.2.refs_3_ = f32[4,24,128]{2,1,0:T(8,128)S(1)} collective-permute-done((f32[4,24,128]{2,1,0:T(8,128)S(1)}, f32[4,24,128]{2,1,0:T(8,128)S(1)}, u32[]{:S(2)}, u32[]{:S(2)}) %collective-permute-start.2) | collective-permute-done | bytes 49184 | tf_op jit(solution)/shard_map/ppermute | solution.py:489
  10.8 0.1 collective-permute-start.3
  10.9 0.6 %lifts.1.after_ref.lift_ref = f32[2,5,64,256]{3,2,1,0:T(8,128)S(1)} custom-call(f32[8,128]{1,0:T(8,128)S(1)} %get-tuple-element.32.after_ref.sign_ref.old_sign, f32[5,4,8,128]{3,2,1,0:T(8,128)S(1)} %get-tuple-element.33.ent_ref, f32[5,32,8,128]{3,2,1,0:T(8,128)S(1)} %get-tuple-element.34.c_s, f32[5,64,256]{2,1,0:T(8,128)S(1)} %get-tuple-element.35.scale_ref, ...), custom_call_target="tpu_custom_call" | custom-call | flops 1000000 | bytes 2000000 | tf_op jit(solution)/shard_map/lifts/pallas_call | solution.py:517
  11.5 0.6 %fluxes.2.after_ref.early_ref = f32[2,2,64,256]{3,2,1,0:T(8,128)S(1)} custom-call(f32[2,5,64,256]{3,2,1,0:T(8,128)S(1)} %lifts.1.after_ref.lift_ref, f32[64,256]{1,0:T(8,128)S(1)} %get-tuple-element.31.in_ref, f32[2,5,64,256]{3,2,1,0:T(8,128)S(1)} %get-tuple-element.28.adj_ref, f32[5,64,256]{2,1,0:T(8,128)S(1)} %bitcast.17), custom_call_target="tpu_custom_call" | custom-call | flops 1000000 | bytes 2000000 | tf_op jit(solution)/shard_map/fluxes/pallas_call | solution.py:527
  12.1 0.0 collective-permute-done.3.rest_1_
  12.1 0.6 %face_maps.1 = (f32[32,128]{1,0:T(8,128)S(1)}, f32[8,128]{1,0:T(8,128)S(1)}, f32[1,4,8,128]{3,2,1,0:T(8,128)S(1)}, f32[1,32,8,128]{3,2,1,0:T(8,128)S(1)}, f32[1,...) custom-call(f32[2,2,64,256]{3,2,1,0:T(8,128)S(1)} %fluxes.2.after_ref.early_ref, f32[64,256]{1,0:T(8,128)S(1)} %get-tuple-element.31.in_ref, ...), custom_call_target="tpu_custom_call" | custom-call | tf_op jit(solution)/shard_map/face_maps/pallas_call | solution.py:538
  12.8 2.6 %collective-permute-start.6 = (f32[32,128]{1,0:T(8,128)S(1)}, f32[32,128]{1,0:T(8,128)S(1)}, u32[]{:S(2)}, u32[]{:S(2)}) collective-permute-start(f32[32,128]{1,0:T(8,128)S(1)} %get-tuple-element.51), channel_id=1, source_target_pairs={{0,16},{8,24},{16,8},{24,0},{1,17},{9,25},{17,9},{25,1},{2,18},{10... | collective-permute-start | bytes 49160 | tf_op jit(solution)/shard_map/ppermute | solution.py:553
  15.4 1.2 %collective-permute-start.5 = (f32[32,128]{1,0:T(8,128)S(1)}, f32[32,128]{1,0:T(8,128)S(1)}, u32[]{:S(2)}, u32[]{:S(2)}) collective-permute-start(f32[32,128]{1,0:T(8,128)S(1)} %get-tuple-element.51), channel_id=1, source_target_pairs={{0,24},{8,16},{16,0},{24,8},{1,25},{9,17},{17,1},{25,9},{2,26},{10... | collective-permute-start | bytes 49160 | tf_op jit(solution)/shard_map/ppermute | solution.py:553
  16.6 0.3 %collective-permute-start.4 = (f32[32,128]{1,0:T(8,128)S(1)}, f32[32,128]{1,0:T(8,128)S(1)}, u32[]{:S(2)}, u32[]{:S(2)}) collective-permute-start(f32[32,128]{1,0:T(8,128)S(1)} %get-tuple-element.51), channel_id=1, source_target_pairs={{0,8},{8,0},{16,24},{24,16},{1,9},{9,1},{17,25},{25,17},{2,10},{10... | collective-permute-start | bytes 49160 | tf_op jit(solution)/shard_map/ppermute | solution.py:553
  17.0 0.8 %substitute.1.after_ref.part_ref = f32[2,5,64,256]{3,2,1,0:T(8,128)S(1)} custom-call(f32[64,256]{1,0:T(8,128)S(1)} %get-tuple-element.31.in_ref, f32[2,5,64,256]{3,2,1,0:T(8,128)S(1)} %get-tuple-element.28.adj_ref, f32[8,128]{1,0:T(8,128)S(1)} %get-tuple-element.44.sign_ref, f32[5,4,8,128]{3,2,1,0:T(8,128)S(1)} %get-tuple-element.33.ent_ref, ...), custom_call_target="tpu_custom_call" | custom-call | flops 2000000 | bytes 3000000 | tf_op jit(solution)/shard_map/substitute/pallas_call | solution.py:554
  17.8 0.8 %fluxes.3.late_ref = f32[2,3,64,256]{3,2,1,0:T(8,128)S(1)} custom-call(f32[2,5,64,256]{3,2,1,0:T(8,128)S(1)} %substitute.1.after_ref.part_ref, f32[64,256]{1,0:T(8,128)S(1)} %get-tuple-element.31.in_ref, f32[2,5,64,256]{3,2,1,0:T(8,128)S(1)} %get-tuple-element.28.adj_ref, f32[5,64,256]{2,1,0:T(8,128)S(1)} %bitcast.19), custom_call_target="tpu_custom_call" | custom-call | flops 1000000 | bytes 2000000 | tf_op jit(solution)/shard_map/fluxes/pallas_call | solution.py:527
  18.7 0.0 collective-permute-done.6.rest_2_
  18.7 1.4 %collective-permute-done.5.rest_1_ = f32[32,128]{1,0:T(8,128)S(1)} collective-permute-done((f32[32,128]{1,0:T(8,128)S(1)}, f32[32,128]{1,0:T(8,128)S(1)}, u32[]{:S(2)}, u32[]{:S(2)}) %collective-permute-start.5) | collective-permute-done | bytes 16416 | tf_op jit(solution)/shard_map/ppermute | solution.py:553
  20.0 0.3 %collective-permute-done.4.rest_0_ = f32[32,128]{1,0:T(8,128)S(1)} collective-permute-done((f32[32,128]{1,0:T(8,128)S(1)}, f32[32,128]{1,0:T(8,128)S(1)}, u32[]{:S(2)}, u32[]{:S(2)}) %collective-permute-start.4) | collective-permute-done | bytes 16416 | tf_op jit(solution)/shard_map/ppermute | solution.py:553
  20.4 1.6 %finish.1 = (f32[2,5,64,256]{3,2,1,0:T(8,128)}, f32[2,5,64,256]{3,2,1,0:T(8,128)}) custom-call(f32[64,256]{1,0:T(8,128)S(1)} %get-tuple-element.31.in_ref, f32[8,128]{1,0:T(8,128)S(1)} %get-tuple-element.44.sign_ref, f32[2,5,64,256]{3,2,1,0:T(8,128)S(1)} %substitute.1.after_ref.part_ref, f32[2,5,64,256]{3,2,1,0:T(8,128)S(1)} %lifts.1.after_ref.lift_ref, ...), custom_call_target="tpu_custom_call" | custom-call | tf_op jit(solution)/shard_map/finish/pallas_call | solution.py:565
  (2 shorter events, 0.0 us)
Async XLA Ops:
  0.6 6.1 %copy-start.1 = (f32[64,10,256]{2,0,1:T(8,128)S(1)}, f32[64,10,256]{2,0,1:T(8,128)}, u32[]{:S(2)}) copy-start(f32[64,10,256]{2,0,1:T(8,128)} %param.9) | copy-start | bytes 1966084
  0.6 6.1 %copy-start = (f32[64,5,256]{2,0,1:T(8,128)S(1)}, f32[64,5,256]{2,0,1:T(8,128)}, u32[]{:S(2)}) copy-start(f32[64,5,256]{2,0,1:T(8,128)} %param.10) | copy-start | bytes 983044
  2.2 6.6 %collective-permute-start = (f32[4,24,128]{2,1,0:T(8,128)S(1)}, f32[4,24,128]{2,1,0:T(8,128)S(1)}, u32[]{:S(2)}, u32[]{:S(2)}) collective-permute-start(f32[4,24,128]{2,1,0:T(8,128)S(1)} %get-tuple-element.38), channel_id=1, source_target_pairs={{0,2},{1,3},{2,0},{3,1},{4,6},{5,7},{6,4},{7,5},{8,10},{9,11},{10,... | collective-permute-start | bytes 147464 | tf_op jit(solution)/shard_map/ppermute | solution.py:489
  5.2 5.0 %collective-permute-start.1 = (f32[4,24,128]{2,1,0:T(8,128)S(1)}, f32[4,24,128]{2,1,0:T(8,128)S(1)}, u32[]{:S(2)}, u32[]{:S(2)}) collective-permute-start(f32[4,24,128]{2,1,0:T(8,128)S(1)} %get-tuple-element.39), channel_id=1, source_target_pairs={{0,6},{1,7},{2,4},{3,5},{4,2},{5,3},{6,0},{7,1},{8,14},{9,15},{10,... | collective-permute-start | bytes 147464 | tf_op jit(solution)/shard_map/ppermute | solution.py:489
  6.7 4.1 %collective-permute-start.2 = (f32[4,24,128]{2,1,0:T(8,128)S(1)}, f32[4,24,128]{2,1,0:T(8,128)S(1)}, u32[]{:S(2)}, u32[]{:S(2)}) collective-permute-start(f32[4,24,128]{2,1,0:T(8,128)S(1)} %get-tuple-element.40), channel_id=1, source_target_pairs={{0,4},{1,5},{2,6},{3,7},{4,0},{5,1},{6,2},{7,3},{8,12},{9,13},{10,... | collective-permute-start | bytes 147464 | tf_op jit(solution)/shard_map/ppermute | solution.py:489
  10.8 1.4 %collective-permute-start.3 = (f32[8,24,128]{2,1,0:T(8,128)S(1)}, f32[8,24,128]{2,1,0:T(8,128)S(1)}, u32[]{:S(2)}, u32[]{:S(2)}) collective-permute-start(f32[8,24,128]{2,1,0:T(8,128)S(1)} %get-tuple-element.43), channel_id=1, source_target_pairs={{0,1},{1,0},{2,3},{3,2},{4,5},{5,4},{6,7},{7,6},{8,9},{9,8},{10,11... | collective-permute-start | bytes 294920 | tf_op jit(solution)/shard_map/ppermute | solution.py:489
  12.8 5.9 %collective-permute-start.6 = (f32[32,128]{1,0:T(8,128)S(1)}, f32[32,128]{1,0:T(8,128)S(1)}, u32[]{:S(2)}, u32[]{:S(2)}) collective-permute-start(f32[32,128]{1,0:T(8,128)S(1)} %get-tuple-element.51), channel_id=1, source_target_pairs={{0,16},{8,24},{16,8},{24,0},{1,17},{9,25},{17,9},{25,1},{2,18},{10... | collective-permute-start | bytes 49160 | tf_op jit(solution)/shard_map/ppermute | solution.py:553
  15.4 4.6 %collective-permute-start.5 = (f32[32,128]{1,0:T(8,128)S(1)}, f32[32,128]{1,0:T(8,128)S(1)}, u32[]{:S(2)}, u32[]{:S(2)}) collective-permute-start(f32[32,128]{1,0:T(8,128)S(1)} %get-tuple-element.51), channel_id=1, source_target_pairs={{0,24},{8,16},{16,0},{24,8},{1,25},{9,17},{17,1},{25,9},{2,26},{10... | collective-permute-start | bytes 49160 | tf_op jit(solution)/shard_map/ppermute | solution.py:553
  16.6 3.7 %collective-permute-start.4 = (f32[32,128]{1,0:T(8,128)S(1)}, f32[32,128]{1,0:T(8,128)S(1)}, u32[]{:S(2)}, u32[]{:S(2)}) collective-permute-start(f32[32,128]{1,0:T(8,128)S(1)} %get-tuple-element.51), channel_id=1, source_target_pairs={{0,8},{8,0},{16,24},{24,16},{1,9},{9,1},{17,25},{25,17},{2,10},{10... | collective-permute-start | bytes 49160 | tf_op jit(solution)/shard_map/ppermute | solution.py:553
